TPU v7x, 128 devices: a whole 4x4x4 slice. The times are simulated.
128 devices in a mesh: dp: 16 (over z, x), ep: 8 (over y, core).
Axes of the slice: x: 4, y: 4, z: 4, core: 2. Of those that a mesh axis runs over, the one named last changes fastest.
Arguments:
- hidden: bfloat16 [2, 2048, 3584], P(None, ('dp', 'ep')), may hold values from -6 to 6
- routes: int32 [2, 2048, 8], P(None, ('dp', 'ep')), may hold values from 0 to 127, all different within a row; in each aligned block of 16 rows (0 to 15, 16 to 31, ..., all dimensions but the last counted through in order) at most 2 rows name the same one
- route_weights: float32 [2, 2048, 8], P(None, ('dp', 'ep')), may hold values from 0.1 to 0.6
- expert_in: bfloat16 [128, 3584, 2048], P(('dp', 'ep')), may hold values from -0.09375 to 0.09375
- expert_out: bfloat16 [128, 1024, 3584], P(('dp', 'ep')), may hold values from -0.1875 to 0.1875
- queries: bfloat16 [2048, 64, 576], P(('dp', 'ep')), may hold values from -6 to 6
- fresh_key: bfloat16 [2048, 576], P(('dp', 'ep')), may hold values from -4 to 4
- latent_cache: bfloat16 [2048, 128, 576], P(('dp', 'ep')), may hold values from -4 to 4
- lengths: int32 [2048], replicated, may hold values from 2 to 128, as said below
- swapped: int32 [2048], P(('dp', 'ep')), may hold values from 0 to 1, as said below
Outputs:
- mixed: bfloat16 [2, 2048, 3584], P(None, ('dp', 'ep'))
- context: bfloat16 [2048, 64, 512], P(('dp', 'ep'))
Inputs may be any that keep to these rules, and one draw needn't show every extreme that they name: `routes`: in each step the 8 experts of a token differ; the 16 tokens of one device name one expert at most 2 times, a bound that some block reaches. `lengths`: some request holds exactly 128 positions. `swapped`: A marked slot trades with the slot at the same position on the device of the same ep index whose dp index differs by half the dp axis; both devices of such a pair carry the same marks; a device carries at most 4 marks, and some device exactly 4.
All inputs are finite; a program needn't handle non-finite values.
Results may differ from a plain program's by a relative error of at most 0.0058.
Values may be sent and summed in bfloat16 or wider, within the bound.
A program may use at most 128 MiB of HBM per device.

v0:
```python
import jax
import jax.numpy as jnp
from jax import lax
from jax.sharding import PartitionSpec as P

LATENT = 512
STEPS = 2
MOVE = 4


SOFTMAX_SCALE = 192.0 ** (-0.5)


def swapped_2(value, axis, apart):
    mask = 2**apart
    pairs = [(source, source ^ mask) for source in range(lax.axis_size(axis))]
    return lax.ppermute(value, axis, pairs)


def expert_rows(picked, expert_in, expert_out):
    projected = jnp.dot(picked, expert_in, preferred_element_type=jnp.float32)
    half_width = projected.shape[1] // 2
    activated = (jax.nn.silu(projected[:, :half_width]) * projected[:, half_width:]).astype(
        jnp.bfloat16
    )
    return jnp.dot(activated, expert_out, preferred_element_type=jnp.float32).astype(jnp.bfloat16)


def serve_slots(received, expert_in, expert_out):
    source_count, slot_count, row_width = received.shape
    finished = expert_rows(
        received.reshape(source_count * slot_count, row_width), expert_in[0], expert_out[0]
    )
    return finished.reshape(source_count, slot_count, row_width)


def route_rows(buffer, expert_in, expert_out):
    finished = serve_slots(
        lax.all_to_all(buffer, ("dp", "ep"), split_axis=0, concat_axis=0, tiled=True),
        expert_in,
        expert_out,
    )
    return lax.all_to_all(finished, ("dp", "ep"), split_axis=0, concat_axis=0, tiled=True)


def pack_rows(tokens, experts, expert_count, slot_cap):
    token_count, pick_count = experts.shape
    flat_ids = experts.reshape(-1)
    onehot = (flat_ids[:, None] == jnp.arange(expert_count, dtype=jnp.int32)[None, :]).astype(
        jnp.int32
    )
    earlier = jnp.cumsum(onehot, axis=0) - onehot
    within = jnp.sum(earlier * onehot, axis=1)
    target = (flat_ids * slot_cap + within).reshape(token_count, pick_count)
    places = jnp.arange(expert_count * slot_cap, dtype=jnp.int32)
    select = jnp.any(target[None, :, :] == places[:, None, None], axis=2).astype(jnp.bfloat16)
    packed = jnp.dot(select, tokens, preferred_element_type=jnp.float32).astype(jnp.bfloat16)
    return (packed.reshape(expert_count, slot_cap, tokens.shape[1]), target)


def unpack_rows(returned, target, gate_values):
    flat_rows = returned.reshape(-1, returned.shape[2])
    picked = jnp.take(flat_rows, target.reshape(-1), axis=0).reshape(
        target.shape + (returned.shape[2],)
    )
    summed = jnp.sum(picked.astype(jnp.float32) * gate_values[:, :, None], axis=1)
    return summed.astype(jnp.bfloat16)


def attend_block(query_rows, cache_rows, live_lengths, fresh_rows):
    scores = (
        jnp.einsum("nhc,nlc->nhl", query_rows, cache_rows, preferred_element_type=jnp.float32)
        * SOFTMAX_SCALE
    )
    own_score = (
        jnp.einsum("nhc,nc->nh", query_rows, fresh_rows, preferred_element_type=jnp.float32)
        * SOFTMAX_SCALE
    )
    positions = jnp.arange(cache_rows.shape[1], dtype=jnp.int32)
    scores = jnp.where(positions[None, None, :] < live_lengths[:, None, None], scores, -jnp.inf)
    row_top = jnp.maximum(jnp.max(scores, axis=2), own_score)
    weights = jnp.exp(scores - row_top[:, :, None])
    own_weight = jnp.exp(own_score - row_top)
    summed = jnp.sum(weights, axis=2) + own_weight
    blended = jnp.einsum(
        "nhl,nlc->nhc",
        weights.astype(jnp.bfloat16),
        cache_rows[:, :, :LATENT],
        preferred_element_type=jnp.float32,
    )
    own_rounded = lax.optimization_barrier(own_weight.astype(jnp.bfloat16))
    blended = blended + own_rounded.astype(jnp.float32)[:, :, None] * fresh_rows[
        :, None, :LATENT
    ].astype(jnp.float32)
    return (blended / summed[:, :, None]).astype(jnp.bfloat16)


def per_device(
    hidden,
    routes,
    route_weights,
    expert_in,
    expert_out,
    queries,
    fresh_key,
    latent_cache,
    lengths,
    swapped,
):
    expert_count = lax.axis_size("dp") * lax.axis_size("ep")
    token_count = hidden.shape[1]
    slot_cap = max(2, 2 * token_count * routes.shape[2] // expert_count)
    packs = [pack_rows(hidden[step], routes[step], expert_count, slot_cap) for step in range(STEPS)]
    returned = [route_rows(entry[0], expert_in, expert_out) for entry in packs]
    mixed = jnp.stack(
        [unpack_rows(returned[step], packs[step][1], route_weights[step]) for step in range(STEPS)]
    )
    row_count = swapped.shape[0]
    top_bit = lax.axis_size("dp").bit_length() - 2
    outgoing = jnp.argsort(1 - swapped, stable=True)[:MOVE]
    arrival = jnp.clip(jnp.cumsum(swapped) - 1, 0, MOVE - 1)
    is_moved = swapped == 1
    device_rows = lax.axis_index(("dp", "ep")) * row_count + jnp.arange(row_count, dtype=jnp.int32)
    total_rows = expert_count * row_count
    anchor = jnp.where(is_moved, (device_rows + total_rows // 2) % total_rows, device_rows)
    incoming_cache = swapped_2(latent_cache[outgoing], "dp", top_bit)
    merged_cache = jnp.where(is_moved[:, None, None], incoming_cache[arrival], latent_cache)
    context = attend_block(queries, merged_cache, lengths[anchor], fresh_key)
    return (mixed, context)


def solution(mesh):
    in_specs = (
        P(None, ("dp", "ep"), None),
        P(None, ("dp", "ep"), None),
        P(None, ("dp", "ep"), None),
        P(("dp", "ep"), None, None),
        P(("dp", "ep"), None, None),
        P(("dp", "ep"), None, None),
        P(("dp", "ep"), None),
        P(("dp", "ep"), None, None),
        P(),
        P(("dp", "ep")),
    )
    out_specs = (P(None, ("dp", "ep"), None), P(("dp", "ep"), None, None))
    return jax.shard_map(
        per_device, mesh=mesh, in_specs=in_specs, out_specs=out_specs, check_vma=False
    )
```

profile of v0, /device:TPU:1, one launch (start us, length us, event | category | flops | bytes accessed | tf_op | source)
XLA Modules:
  0.0 166.3 jit_solution(5651211025018110514)
XLA Ops:
  0.6 0.0 copy-start
  0.7 0.8 compare_select_fusion.4
  1.4 1.2 sort.17
  2.7 2.3 %gather_fusion.1 = bf16[4,128,576]{1,2,0:T(8,128)(2,1)S(1)} fusion(bf16[16,128,576]{1,2,0:T(8,128)(2,1)} %param.19, s32[1024]{0:T(1024)S(1)} %pad_clamp_fusion.1), kind=kCustom, calls=%fused_computation.3 | custom fusion | bytes 1179664 | tf_op jit(solution)/shard_map/gather | solution.py:126
  5.0 4.5 %collective-permute-start = (bf16[4,128,576]{1,2,0:T(8,128)(2,1)S(1)}, bf16[4,128,576]{1,2,0:T(8,128)(2,1)S(1)}, u32[]{:S(2)}, u32[]{:S(2)}) collective-permute-start(bf16[4,128,576]{1,2,0:T(8,128)(2,1)S(1)} %gather_fusion.1), channel_id=1, source_target_pairs={{0,64},{8,72},{16,80},{24,88},{32,96},{40,104},{48,112},{56,120},{... | collective-permute-start | bytes 1769480 | tf_op jit(solution)/shard_map/ppermute | solution.py:17
  9.5 0.7 fusion.49
  10.2 0.1 copy.52
  10.3 0.1 eq.65
  10.4 0.1 fusion.39
  10.5 0.2 reduce_window_sum.24
  10.7 0.2 select_reduce_fusion.1
  10.8 0.1 reduce_sum.50
  10.9 0.1 fusion.32
  11.1 2.8 %convolution_convert_fusion.1 = bf16[256,3584]{1,0:T(8,128)(2,1)} fusion(pred[256,16]{0,1:T(8,128)(4,1)S(1)} %fusion.32, bf16[2,16,3584]{2,1,0:T(8,128)(2,1)} %param.12), kind=kOutput, calls=%fused_computation.16 | convolution fusion | flops 30277632 | bytes 1953792 | tf_op jit(solution)/shard_map/dot_general | solution.py:57
  13.9 4.8 %reshape.110 = bf16[128,2,3584]{2,1,0:T(2,128)(2,1)} reshape(bf16[256,3584]{1,0:T(8,128)(2,1)} %convolution_convert_fusion.1) | data formatting | bytes 3670016 | tf_op jit(solution)/shard_map/reshape | solution.py:58
  18.7 8.3 %all-to-all-start = ((bf16[128,2,3584]{2,1,0:T(2,128)(2,1)}), bf16[128,2,3584]{2,1,0:T(2,128)(2,1)}, u32[]{:S(2)}, u32[]{:S(2)}) async-start(bf16[128,2,3584]{2,1,0:T(2,128)(2,1)} %reshape.110), calls=%async_computation | async-start | bytes 3670016 | tf_op jit(solution)/shard_map/all_to_all | solution.py:39
  27.0 0.0 copy-done.5
  27.0 0.1 copy.43
  27.1 0.1 fusion.42
  27.3 0.1 copy.53
  27.4 0.1 eq.73
  27.4 0.1 fusion.38
  27.5 0.2 reduce_window_sum.25
  27.7 0.2 select_reduce_fusion
  27.9 0.1 reduce_sum.53
  28.0 0.1 fusion.33
  28.1 0.0 copy-done.2
  28.1 2.0 %convolution_convert_fusion = bf16[256,3584]{1,0:T(8,128)(2,1)} fusion(pred[256,16]{0,1:T(8,128)(4,1)S(1)} %fusion.33, bf16[2,16,3584]{2,1,0:T(8,128)(2,1)S(1)} %copy-done.2), kind=kOutput, calls=%fused_computation.15 | convolution fusion | flops 30277632 | bytes 1953792 | tf_op jit(solution)/shard_map/dot_general | solution.py:57
  30.1 4.8 %reshape.114 = bf16[128,2,3584]{2,1,0:T(2,128)(2,1)} reshape(bf16[256,3584]{1,0:T(8,128)(2,1)} %convolution_convert_fusion) | data formatting | bytes 3670016 | tf_op jit(solution)/shard_map/reshape | solution.py:58
  34.9 0.7 gather_fusion
  35.6 0.1 iota_compare_fusion.4
  35.7 0.5 fusion.40
  36.2 18.2 %all-to-all-done = bf16[128,2,3584]{2,1,0:T(2,128)(2,1)} async-done(((bf16[128,2,3584]{2,1,0:T(2,128)(2,1)}), bf16[128,2,3584]{2,1,0:T(2,128)(2,1)}, u32[]{:S(2)}, u32[]{:S(2)}) %all-to-all-start) | async-done | bytes 1835040 | tf_op jit(solution)/shard_map/all_to_all | solution.py:39
  54.4 5.3 %all-to-all-start.2 = ((bf16[128,2,3584]{2,1,0:T(2,128)(2,1)}), bf16[128,2,3584]{2,1,0:T(2,128)(2,1)}, u32[]{:S(2)}, u32[]{:S(2)}) async-start(bf16[128,2,3584]{2,1,0:T(2,128)(2,1)} %reshape.114), calls=%async_computation.2 | async-start | bytes 3670016 | tf_op jit(solution)/shard_map/all_to_all | solution.py:39
  59.8 4.9 %reshape.111 = bf16[256,3584]{1,0:T(8,128)(2,1)} reshape(bf16[128,2,3584]{2,1,0:T(2,128)(2,1)} %all-to-all-done) | data formatting | bytes 3670016 | tf_op jit(solution)/shard_map/reshape | solution.py:32
  64.7 7.8 %fusion.2 = f32[256,2048]{1,0:T(8,128)S(1)} fusion(bf16[256,3584]{1,0:T(8,128)(2,1)} %reshape.111, bf16[1,3584,2048]{2,1,0:T(8,128)(2,1)} %param.15), kind=kOutput, calls=%fused_computation.7 | convolution fusion | flops 3758096384 | bytes 18612224 | tf_op jit(solution)/shard_map/dot_general | solution.py:21
  72.5 6.5 %fusion.8 = bf16[256,3584]{1,0:T(8,128)(2,1)} fusion(bf16[1,1024,3584]{2,1,0:T(8,128)(2,1)} %param.16, f32[256,2048]{1,0:T(8,128)S(1)} %fusion.2), kind=kOutput, calls=%fused_computation.13 | convolution fusion | flops 1881538560 | bytes 11272192 | tf_op jit(solution)/shard_map/dot_general | solution.py:26
  79.0 4.8 %reshape.112 = bf16[128,2,3584]{2,1,0:T(2,128)(2,1)} reshape(bf16[256,3584]{1,0:T(8,128)(2,1)} %fusion.8) | data formatting | bytes 3670016 | tf_op jit(solution)/shard_map/reshape | solution.py:34
  83.7 3.6 %all-to-all-done.2 = bf16[128,2,3584]{2,1,0:T(2,128)(2,1)} async-done(((bf16[128,2,3584]{2,1,0:T(2,128)(2,1)}), bf16[128,2,3584]{2,1,0:T(2,128)(2,1)}, u32[]{:S(2)}, u32[]{:S(2)}) %all-to-all-start.2) | async-done | bytes 1835040 | tf_op jit(solution)/shard_map/all_to_all | solution.py:39
  87.3 6.7 %all-to-all-start.1 = ((bf16[128,2,3584]{2,1,0:T(2,128)(2,1)}), bf16[128,2,3584]{2,1,0:T(2,128)(2,1)}, u32[]{:S(2)}, u32[]{:S(2)}) async-start(bf16[128,2,3584]{2,1,0:T(2,128)(2,1)} %reshape.112), calls=%async_computation.1 | async-start | bytes 3670016 | tf_op jit(solution)/shard_map/all_to_all | solution.py:43
  94.1 4.9 %reshape.115 = bf16[256,3584]{1,0:T(8,128)(2,1)} reshape(bf16[128,2,3584]{2,1,0:T(2,128)(2,1)} %all-to-all-done.2) | data formatting | bytes 3670016 | tf_op jit(solution)/shard_map/reshape | solution.py:32
  99.0 7.8 %fusion = f32[256,2048]{1,0:T(8,128)S(1)} fusion(bf16[256,3584]{1,0:T(8,128)(2,1)} %reshape.115, bf16[1,3584,2048]{2,1,0:T(8,128)(2,1)} %param.15), kind=kOutput, calls=%fused_computation.5 | convolution fusion | flops 3758096384 | bytes 18612224 | tf_op jit(solution)/shard_map/dot_general | solution.py:21
  106.8 6.5 %fusion.11 = bf16[256,3584]{1,0:T(8,128)(2,1)} fusion(bf16[1,1024,3584]{2,1,0:T(8,128)(2,1)} %param.16, f32[256,2048]{1,0:T(8,128)S(1)} %fusion), kind=kOutput, calls=%fused_computation.14 | convolution fusion | flops 1881538560 | bytes 11272192 | tf_op jit(solution)/shard_map/dot_general | solution.py:26
  113.2 4.7 %reshape.116 = bf16[128,2,3584]{2,1,0:T(2,128)(2,1)} reshape(bf16[256,3584]{1,0:T(8,128)(2,1)} %fusion.11) | data formatting | bytes 3670016 | tf_op jit(solution)/shard_map/reshape | solution.py:34
  118.0 3.5 %all-to-all-done.1 = bf16[128,2,3584]{2,1,0:T(2,128)(2,1)} async-done(((bf16[128,2,3584]{2,1,0:T(2,128)(2,1)}), bf16[128,2,3584]{2,1,0:T(2,128)(2,1)}, u32[]{:S(2)}, u32[]{:S(2)}) %all-to-all-start.1) | async-done | bytes 1835040 | tf_op jit(solution)/shard_map/all_to_all | solution.py:43
  121.5 6.7 %all-to-all-start.3 = ((bf16[128,2,3584]{2,1,0:T(2,128)(2,1)}), bf16[128,2,3584]{2,1,0:T(2,128)(2,1)}, u32[]{:S(2)}, u32[]{:S(2)}) async-start(bf16[128,2,3584]{2,1,0:T(2,128)(2,1)} %reshape.116), calls=%async_computation.3 | async-start | bytes 3670016 | tf_op jit(solution)/shard_map/all_to_all | solution.py:43
  128.2 4.3 %copy.45 = bf16[16,128,576]{2,1,0:T(8,128)(2,1)} copy(bf16[16,128,576]{1,2,0:T(8,128)(2,1)} %param.19) | data formatting | bytes 4718592 | tf_op args[7]
  132.5 0.1 copy.38
  132.6 0.1 copy.42
  132.6 0.0 collective-permute-done
  132.6 2.3 %gather_fusion.2 = bf16[16,128,576]{1,2,0:T(8,128)(2,1)} fusion(bf16[4,128,576]{1,2,0:T(8,128)(2,1)S(1)} %collective-permute-done, s32[1024]{0:T(1024)S(1)} %pad_clamp_fusion), kind=kCustom, calls=%fused_computation.4 | custom fusion | bytes 4718656 | tf_op jit(solution)/shard_map/gather | solution.py:127
  134.9 4.4 %copy.44 = bf16[16,128,576]{2,1,0:T(8,128)(2,1)} copy(bf16[16,128,576]{1,2,0:T(8,128)(2,1)} %gather_fusion.2) | data formatting | bytes 4718592 | tf_op jit(solution)/shard_map/gather | solution.py:127
  139.3 2.9 %broadcast_select_fusion = bf16[16,128,576]{2,1,0:T(8,128)(2,1)S(1)} fusion(bf16[16,128,576]{2,1,0:T(8,128)(2,1)} %copy.44, bf16[16,128,576]{2,1,0:T(8,128)(2,1)} %copy.45, pred[16]{0:T(512)(128)(4,1)S(1)} %broadcast_compare_fusion), kind=kLoop, calls=%fused_computation.17 | loop fusion | flops 1179648 | bytes 7077904 | tf_op jit(solution)/shard_map/jit(_where)/select_n | solution.py:127
  142.2 1.3 fusion.50
  143.5 0.4 fusion.28
  143.9 1.6 divide_convert_fusion
  145.5 4.1 %reshape.113 = bf16[256,3584]{1,0:T(8,128)(2,1)S(1)} reshape(bf16[128,2,3584]{2,1,0:T(2,128)(2,1)} %all-to-all-done.1) | data formatting | bytes 3670016 | tf_op jit(solution)/shard_map/reshape | solution.py:62
  149.5 2.1 %gather_fusion.3 = bf16[128,3584]{1,0:T(8,128)(2,1)} fusion(bf16[256,3584]{1,0:T(8,128)(2,1)S(1)} %reshape.113, s32[1024]{0:T(1024)S(1)} %pad_clamp_fusion.4), kind=kCustom, calls=%fused_computation.clone | custom fusion | bytes 1835520 | tf_op jit(solution)/shard_map/jit(_take)/gather | solution.py:63
  151.6 4.0 %all-to-all-done.3 = bf16[128,2,3584]{2,1,0:T(2,128)(2,1)} async-done(((bf16[128,2,3584]{2,1,0:T(2,128)(2,1)}), bf16[128,2,3584]{2,1,0:T(2,128)(2,1)}, u32[]{:S(2)}, u32[]{:S(2)}) %all-to-all-start.3) | async-done | bytes 1835040 | tf_op jit(solution)/shard_map/all_to_all | solution.py:43
  155.6 4.1 %reshape.117 = bf16[256,3584]{1,0:T(8,128)(2,1)S(1)} reshape(bf16[128,2,3584]{2,1,0:T(2,128)(2,1)} %all-to-all-done.3) | data formatting | bytes 3670016 | tf_op jit(solution)/shard_map/reshape | solution.py:62
  159.6 2.1 %gather_fusion.4 = bf16[128,3584]{1,0:T(8,128)(2,1)} fusion(bf16[256,3584]{1,0:T(8,128)(2,1)S(1)} %reshape.117, s32[1024]{0:T(1024)S(1)} %pad_clamp_fusion.3), kind=kCustom, calls=%fused_computation.1.clone | custom fusion | bytes 1835520 | tf_op jit(solution)/shard_map/jit(_take)/gather | solution.py:63
  161.7 1.9 %fusion.17 = bf16[16,3584]{1,0:T(8,128)(2,1)S(1)} fusion(bf16[128,3584]{1,0:T(8,128)(2,1)} %gather_fusion.3, f32[16,8]{1,0:T(8,128)S(1)} %copy.38, pred[128]{0:T(512)(128)(4,1)S(1)} %get-tuple-element.5), kind=kLoop, calls=%fused_computation.24 | loop fusion | flops 1777664 | bytes 1032832 | tf_op jit(solution)/shard_map/reduce_sum | solution.py:66
  163.7 1.9 %fusion.16 = bf16[16,3584]{1,0:T(8,128)(2,1)S(1)} fusion(bf16[128,3584]{1,0:T(8,128)(2,1)} %gather_fusion.4, f32[16,8]{1,0:T(8,128)S(1)} %copy.42, pred[128]{0:T(512)(128)(4,1)S(1)} %get-tuple-element.7), kind=kLoop, calls=%fused_computation.22 | loop fusion | flops 1777664 | bytes 1032832 | tf_op jit(solution)/shard_map/reduce_sum | solution.py:66
  165.6 0.7 pad_maximum_fusion
  (27 shorter events, 0.2 us)
Async XLA Ops:
  0.6 35.1 %copy-start = (bf16[16,64,576]{2,1,0:T(8,128)(2,1)S(1)}, bf16[16,64,576]{2,1,0:T(8,128)(2,1)}, u32[]{:S(2)}) copy-start(bf16[16,64,576]{2,1,0:T(8,128)(2,1)} %param.17) | copy-start | bytes 3538948
  5.0 127.6 %collective-permute-start = (bf16[4,128,576]{1,2,0:T(8,128)(2,1)S(1)}, bf16[4,128,576]{1,2,0:T(8,128)(2,1)S(1)}, u32[]{:S(2)}, u32[]{:S(2)}) collective-permute-start(bf16[4,128,576]{1,2,0:T(8,128)(2,1)S(1)} %gather_fusion.1), channel_id=1, source_target_pairs={{0,64},{8,72},{16,80},{24,88},{32,96},{40,104},{48,112},{56,120},{... | collective-permute-start | bytes 1769480 | tf_op jit(solution)/shard_map/ppermute | solution.py:17
  18.7 8.3 %copy-start.5 = (s32[16]{0:T(128)S(1)}, s32[16]{0:T(128)}, u32[]{:S(2)}) copy-start(s32[16]{0:T(128)} %param.21) | copy-start | bytes 196
  18.7 9.4 %copy-start.2 = (bf16[2,16,3584]{2,1,0:T(8,128)(2,1)S(1)}, bf16[2,16,3584]{2,1,0:T(8,128)(2,1)}, u32[]{:S(2)}) copy-start(bf16[2,16,3584]{2,1,0:T(8,128)(2,1)} %param.12) | copy-start | bytes 688132
  18.7 35.8 %all-to-all-start = ((bf16[128,2,3584]{2,1,0:T(2,128)(2,1)}), bf16[128,2,3584]{2,1,0:T(2,128)(2,1)}, u32[]{:S(2)}, u32[]{:S(2)}) async-start(bf16[128,2,3584]{2,1,0:T(2,128)(2,1)} %reshape.110), calls=%async_computation | async-start | bytes 3670016 | tf_op jit(solution)/shard_map/all_to_all | solution.py:39
  30.1 4.8 %copy-start.1 = (s32[2048]{0:T(1024)S(1)}, s32[2048]{0:T(1024)}, u32[]{:S(2)}) copy-start(s32[2048]{0:T(1024)} %param.20) | copy-start | bytes 24580
  30.1 5.6 %copy-start.4 = (f32[2,16,8]{1,2,0:T(8,128)S(1)}, f32[2,16,8]{1,2,0:T(8,128)}, u32[]{:S(2)}) copy-start(f32[2,16,8]{1,2,0:T(8,128)} %param.14) | copy-start | bytes 3076
  30.1 5.6 %copy-start.3 = (bf16[16,576]{1,0:T(8,128)(2,1)S(1)}, bf16[16,576]{1,0:T(8,128)(2,1)}, u32[]{:S(2)}) copy-start(bf16[16,576]{1,0:T(8,128)(2,1)} %param.18) | copy-start | bytes 55300
  54.4 32.9 %all-to-all-start.2 = ((bf16[128,2,3584]{2,1,0:T(2,128)(2,1)}), bf16[128,2,3584]{2,1,0:T(2,128)(2,1)}, u32[]{:S(2)}, u32[]{:S(2)}) async-start(bf16[128,2,3584]{2,1,0:T(2,128)(2,1)} %reshape.114), calls=%async_computation.2 | async-start | bytes 3670016 | tf_op jit(solution)/shard_map/all_to_all | solution.py:39
  87.3 34.1 %all-to-all-start.1 = ((bf16[128,2,3584]{2,1,0:T(2,128)(2,1)}), bf16[128,2,3584]{2,1,0:T(2,128)(2,1)}, u32[]{:S(2)}, u32[]{:S(2)}) async-start(bf16[128,2,3584]{2,1,0:T(2,128)(2,1)} %reshape.112), calls=%async_computation.1 | async-start | bytes 3670016 | tf_op jit(solution)/shard_map/all_to_all | solution.py:43
  121.5 34.1 %all-to-all-start.3 = ((bf16[128,2,3584]{2,1,0:T(2,128)(2,1)}), bf16[128,2,3584]{2,1,0:T(2,128)(2,1)}, u32[]{:S(2)}, u32[]{:S(2)}) async-start(bf16[128,2,3584]{2,1,0:T(2,128)(2,1)} %reshape.116), calls=%async_computation.3 | async-start | bytes 3670016 | tf_op jit(solution)/shard_map/all_to_all | solution.py:43
where the time goes:
time: 168 us; the launch traced here: 166 us
  local copies, waits for them, and re-layouts  56.6 us (34%)
  matrix products  36.6 us (22%)
  starting transfers between devices  31.6 us (19%)
  waiting for transfers between devices  29.3 us (17%)
  other arithmetic  11.3 us (7%)
    all_to_all x2, waiting for transfers between devices, route_rows(): lax.all_to_all(buffer, ('dp', 'ep'), split_axis=0, concat_axis=0, tiled=T...  21.8 us
    dot_general x2, matrix products, expert_rows(): projected = jnp.dot(picked, expert_in, preferred_element_type=jnp.float32)  15.5 us
    all_to_all x2, starting transfers between devices, route_rows(): lax.all_to_all(buffer, ('dp', 'ep'), split_axis=0, concat_axis=0, tiled=T...  13.7 us
    all_to_all x2, starting transfers between devices, route_rows(): lax.all_to_all(finished, ('dp', 'ep'), split_axis=0, concat_axis=0, tiled...  13.4 us
    dot_general x2, matrix products, expert_rows(): jnp.dot(activated, expert_out, preferred_element_type=jnp.float32)  13 us
    reshape x2, local copies, waits for them, and re-layouts, serve_slots(): received.reshape(source_count * slot_count, row_width)  9.86 us
    reshape x2, local copies, waits for them, and re-layouts, pack_rows(): return (packed.reshape(expert_count, slot_cap, tokens.shape[1]), target)  9.57 us
    reshape x2, local copies, waits for them, and re-layouts, serve_slots(): return finished.reshape(source_count, slot_count, row_width)  9.51 us
  transfers between devices with their start and end apart: 5, of which 4 were waited for; matrix products, arithmetic and copies ran while one was open for 54% of the time, Pallas kernels for 0%

commit v1 on v0

--- a/solution.py
+++ b/solution.py
@@ -1,14 +1,65 @@
+import functools
+
 import jax
 import jax.numpy as jnp
 from jax import lax
+from jax.experimental import pallas as pl
+from jax.experimental.pallas import tpu as pltpu
 from jax.sharding import PartitionSpec as P
 
 LATENT = 512
 STEPS = 2
 MOVE = 4
+CAP = 2
+MESH_ID = pl.DeviceIdType.MESH
+
+SOFTMAX_SCALE = 192.0 ** (-0.5)
 
 
-SOFTMAX_SCALE = 192.0 ** (-0.5)
+def _a2a_kernel(n_ep, n_all, x_ref, o_ref, send_sem, recv_sem):
+    me = lax.axis_index("dp") * n_ep + lax.axis_index("ep")
+    barrier = pltpu.get_barrier_semaphore()
+
+    def greet(k, carry):
+        peer = lax.rem(me + k, n_all)
+        pl.semaphore_signal(
+            barrier, 1, device_id=(peer // n_ep, peer % n_ep), device_id_type=MESH_ID
+        )
+        return carry
+
+    lax.fori_loop(1, n_all, greet, 0)
+    pl.semaphore_wait(barrier, n_all - 1)
+    pltpu.make_async_copy(x_ref.at[me], o_ref.at[me], recv_sem).start()
+
+    def send(k, carry):
+        peer = lax.rem(me + k, n_all)
+        pltpu.make_async_remote_copy(
+            x_ref.at[peer],
+            o_ref.at[me],
+            send_sem,
+            recv_sem,
+            device_id=(peer // n_ep, peer % n_ep),
+            device_id_type=MESH_ID,
+        ).start()
+        return carry
+
+    lax.fori_loop(1, n_all, send, 0)
+    sent = pl.ds(0, n_all - 1)
+    pltpu.make_async_copy(x_ref.at[sent], x_ref.at[sent], send_sem).wait()
+    pltpu.make_async_copy(o_ref, o_ref, recv_sem).wait()
+
+
+def all_to_all_rows(x, n_ep, n_all, collective_id):
+    nbytes = x.size * x.dtype.itemsize
+    return pl.pallas_call(
+        functools.partial(_a2a_kernel, n_ep, n_all),
+        out_shape=jax.ShapeDtypeStruct(x.shape, x.dtype),
+        in_specs=[pl.BlockSpec(memory_space=pl.ANY)],
+        out_specs=pl.BlockSpec(memory_space=pl.ANY),
+        scratch_shapes=[pltpu.SemaphoreType.DMA(()), pltpu.SemaphoreType.DMA(())],
+        compiler_params=pltpu.CompilerParams(collective_id=collective_id, has_side_effects=True),
+        cost_estimate=pl.CostEstimate(flops=0, transcendentals=0, bytes_accessed=2 * nbytes),
+    )(x)
 
 
 def swapped_2(value, axis, apart):
@@ -18,52 +69,47 @@
 
 
 def expert_rows(picked, expert_in, expert_out):
-    projected = jnp.dot(picked, expert_in, preferred_element_type=jnp.float32)
-    half_width = projected.shape[1] // 2
-    activated = (jax.nn.silu(projected[:, :half_width]) * projected[:, half_width:]).astype(
-        jnp.bfloat16
-    )
-    return jnp.dot(activated, expert_out, preferred_element_type=jnp.float32).astype(jnp.bfloat16)
-
-
-def serve_slots(received, expert_in, expert_out):
-    source_count, slot_count, row_width = received.shape
-    finished = expert_rows(
-        received.reshape(source_count * slot_count, row_width), expert_in[0], expert_out[0]
-    )
-    return finished.reshape(source_count, slot_count, row_width)
-
-
-def route_rows(buffer, expert_in, expert_out):
-    finished = serve_slots(
-        lax.all_to_all(buffer, ("dp", "ep"), split_axis=0, concat_axis=0, tiled=True),
-        expert_in,
-        expert_out,
-    )
-    return lax.all_to_all(finished, ("dp", "ep"), split_axis=0, concat_axis=0, tiled=True)
+    projected = jnp.einsum("skc,cf->skf", picked, expert_in, preferred_element_type=jnp.float32)
+    half_width = projected.shape[2] // 2
+    activated = (
+        jax.nn.silu(projected[:, :, :half_width]) * projected[:, :, half_width:]
+    ).astype(jnp.bfloat16)
+    return jnp.einsum(
+        "skf,fc->skc", activated, expert_out, preferred_element_type=jnp.float32
+    ).astype(jnp.bfloat16)
 
 
 def pack_rows(tokens, experts, expert_count, slot_cap):
-    token_count, pick_count = experts.shape
-    flat_ids = experts.reshape(-1)
-    onehot = (flat_ids[:, None] == jnp.arange(expert_count, dtype=jnp.int32)[None, :]).astype(
+    step_count, token_count, pick_count = experts.shape
+    onehot = (experts[:, :, :, None] == jnp.arange(expert_count, dtype=jnp.int32)).astype(
         jnp.int32
     )
-    earlier = jnp.cumsum(onehot, axis=0) - onehot
-    within = jnp.sum(earlier * onehot, axis=1)
-    target = (flat_ids * slot_cap + within).reshape(token_count, pick_count)
-    places = jnp.arange(expert_count * slot_cap, dtype=jnp.int32)
-    select = jnp.any(target[None, :, :] == places[:, None, None], axis=2).astype(jnp.bfloat16)
-    packed = jnp.dot(select, tokens, preferred_element_type=jnp.float32).astype(jnp.bfloat16)
-    return (packed.reshape(expert_count, slot_cap, tokens.shape[1]), target)
+    flat = onehot.reshape(step_count, token_count * pick_count, expert_count)
+    earlier = jnp.cumsum(flat, axis=1) - flat
+    within = jnp.sum(earlier * flat, axis=2).reshape(step_count, token_count, pick_count)
+    steps = jnp.arange(step_count, dtype=jnp.int32)[:, None, None]
+    target = experts * (step_count * slot_cap) + steps * slot_cap + within
+    places = jnp.arange(expert_count * step_count * slot_cap, dtype=jnp.int32).reshape(
+        expert_count, step_count * slot_cap
+    )
+    flat_target = target.reshape(step_count * token_count, pick_count)
+    select = jnp.any(flat_target[None, None, :, :] == places[:, :, None, None], axis=3).astype(
+        jnp.bfloat16
+    )
+    flat_tokens = tokens.reshape(step_count * token_count, tokens.shape[2])
+    packed = jnp.einsum(
+        "dkt,tc->dkc", select, flat_tokens, preferred_element_type=jnp.float32
+    ).astype(jnp.bfloat16)
+    return packed, target
 
 
 def unpack_rows(returned, target, gate_values):
-    flat_rows = returned.reshape(-1, returned.shape[2])
-    picked = jnp.take(flat_rows, target.reshape(-1), axis=0).reshape(
+    width = returned.shape[1]
+    flat_target = target.reshape(-1)
+    picked = returned[flat_target // width, flat_target % width].reshape(
         target.shape + (returned.shape[2],)
     )
-    summed = jnp.sum(picked.astype(jnp.float32) * gate_values[:, :, None], axis=1)
+    summed = jnp.sum(picked.astype(jnp.float32) * gate_values[..., None], axis=2)
     return summed.astype(jnp.bfloat16)
 
 
@@ -107,14 +153,13 @@
     lengths,
     swapped,
 ):
-    expert_count = lax.axis_size("dp") * lax.axis_size("ep")
-    token_count = hidden.shape[1]
-    slot_cap = max(2, 2 * token_count * routes.shape[2] // expert_count)
-    packs = [pack_rows(hidden[step], routes[step], expert_count, slot_cap) for step in range(STEPS)]
-    returned = [route_rows(entry[0], expert_in, expert_out) for entry in packs]
-    mixed = jnp.stack(
-        [unpack_rows(returned[step], packs[step][1], route_weights[step]) for step in range(STEPS)]
-    )
+    n_ep = lax.axis_size("ep")
+    expert_count = lax.axis_size("dp") * n_ep
+    packed, target = pack_rows(hidden, routes, expert_count, CAP)
+    received = all_to_all_rows(packed, n_ep, expert_count, 0)
+    finished = expert_rows(received, expert_in[0], expert_out[0])
+    returned = all_to_all_rows(finished, n_ep, expert_count, 1)
+    mixed = unpack_rows(returned, target, route_weights)
     row_count = swapped.shape[0]
     top_bit = lax.axis_size("dp").bit_length() - 2
     outgoing = jnp.argsort(1 - swapped, stable=True)[:MOVE]

time: 168 us -> 213 us (1.27)
  Pallas kernels: 0 us -> 140 us
  waiting for transfers between devices: 29.3 us -> 0.01 us
  starting transfers between devices: 31.6 us -> 4.51 us
  local copies, waits for them, and re-layouts: 56.6 us -> 30.4 us
  matrix products: 36.6 us -> 24.1 us
    pallas_call x0 -> x2, Pallas kernels: none -> 140 us  [all_to_all_rows(): pl.pallas_call(functools.partial(_a2a_kernel, n_ep, n_all), out_shape=jax...]
    reshape x9 -> x3, local copies, waits for them, and re-layouts: 37.1 us -> 0.27 us  [the longest x1 0.1 us: unpack_rows(): flat_target = target.reshape(-1)]
    all_to_all x4 -> x0, waiting for transfers between devices: 29.3 us -> none  [the longest x2 21.8 us: route_rows(): lax.all_to_all(buffer, ('dp', 'ep'), split_axis=0, concat_axis=0, tiled=T...]
    all_to_all x4 -> x0, starting transfers between devices: 27.1 us -> none  [the longest x2 13.7 us: route_rows(): lax.all_to_all(buffer, ('dp', 'ep'), split_axis=0, concat_axis=0, tiled=T...]
    dot_general x6 -> x3, matrix products: 33.3 us -> 20.7 us  [the longest x1 12.1 us: expert_rows(): jnp.einsum('skc,cf->skf', picked, expert_in, preferred_element_type=jnp.f...]
    dot_general x0 -> x2, local copies, waits for them, and re-layouts: none -> 9.3 us  [the longest x1 4.67 us: expert_rows(): jnp.einsum('skf,fc->skc', activated, expert_out, preferred_element_type=j...]
    gather x2 -> x1, local copies, waits for them, and re-layouts: 4.14 us -> 6.64 us  [unpack_rows(): returned[flat_target // width, flat_target % width]]
    unnamed x15 -> x17, local copies, waits for them, and re-layouts: 4.51 us -> 4.53 us
  transfers between devices with their start and end apart: 5 -> 1, of which waited for: 4 -> 0; matrix products, arithmetic and copies ran while one was open for 54% -> 23% of each run, Pallas kernels for 0% -> 67%
where the time goes in v1:
time: 213 us; the launch traced here: 210 us
  Pallas kernels  140 us (66%)
  local copies, waits for them, and re-layouts  30.4 us (14%)
  matrix products  24.1 us (11%)
  other arithmetic  10.1 us (5%)
  starting transfers between devices  4.51 us (2%)
    pallas_call x2, Pallas kernels, all_to_all_rows(): pl.pallas_call(functools.partial(_a2a_kernel, n_ep, n_all), out_shape=jax...  140 us
    dot_general x1, matrix products, expert_rows(): jnp.einsum('skc,cf->skf', picked, expert_in, preferred_element_type=jnp.f...  12.1 us
    dot_general x1, matrix products, expert_rows(): jnp.einsum('skf,fc->skc', activated, expert_out, preferred_element_type=j...  7.47 us
    gather x1, local copies, waits for them, and re-layouts, unpack_rows(): returned[flat_target // width, flat_target % width]  6.64 us
    gather x2, local copies, waits for them, and re-layouts, per_device(): incoming_cache[arrival]  6.62 us
    dot_general x1, local copies, waits for them, and re-layouts, expert_rows(): jnp.einsum('skf,fc->skc', activated, expert_out, preferred_element_type=j...  4.67 us
    dot_general x1, local copies, waits for them, and re-layouts, pack_rows(): jnp.einsum('dkt,tc->dkc', select, flat_tokens, preferred_element_type=jnp...  4.63 us
    unnamed x17, local copies, waits for them, and re-layouts  4.53 us
  transfers between devices with their start and end apart: 1, of which 0 were waited for; matrix products, arithmetic and copies ran while one was open for 23% of the time, Pallas kernels for 67%

profile of v1, /device:TPU:1, one launch (start us, length us, event | category | flops | bytes accessed | tf_op | source)
XLA Modules:
  0.0 210.0 jit_solution(9445025108249742247)
XLA Ops:
  0.6 0.0 copy-start
  0.7 0.8 compare_select_fusion.4
  1.4 1.2 sort.17
  2.7 2.3 %gather_fusion.2 = bf16[4,128,576]{1,2,0:T(8,128)(2,1)S(1)} fusion(bf16[16,128,576]{1,2,0:T(8,128)(2,1)} %param.17, s32[1024]{0:T(1024)S(1)} %pad_clamp_fusion.1), kind=kCustom, calls=%fused_computation.2 | custom fusion | bytes 1179664 | tf_op jit(solution)/shard_map/gather | solution.py:171
  5.0 0.0 copy-start.6
  5.0 0.0 copy-start.4
  5.1 0.0 copy-start.5
  5.1 4.5 %collective-permute-start = (bf16[4,128,576]{1,2,0:T(8,128)(2,1)S(1)}, bf16[4,128,576]{1,2,0:T(8,128)(2,1)S(1)}, u32[]{:S(2)}, u32[]{:S(2)}) collective-permute-start(bf16[4,128,576]{1,2,0:T(8,128)(2,1)S(1)} %gather_fusion.2), channel_id=1, source_target_pairs={{0,64},{8,72},{16,80},{24,88},{32,96},{40,104},{48,112},{56,120},{... | collective-permute-start | bytes 1769480 | tf_op jit(solution)/shard_map/ppermute | solution.py:68
  9.6 0.0 copy-start.2
  9.6 4.3 %copy.39 = bf16[16,128,576]{2,1,0:T(8,128)(2,1)} copy(bf16[16,128,576]{1,2,0:T(8,128)(2,1)} %param.17) | data formatting | bytes 4718592 | tf_op args[7]
  13.9 0.0 copy-done.6
  13.9 0.0 copy-done.4
  13.9 0.1 copy.36
  14.0 0.0 copy-done.5
  14.0 0.1 copy.29
  14.1 0.1 eq.38
  14.2 0.1 fusion.19
  14.3 0.2 reduce_window_sum.18
  14.5 0.2 select_reduce_fusion
  14.7 0.1 reshape.206
  14.8 0.1 add_add_fusion
  14.8 0.1 reshape.208
  14.9 0.2 compare_reduce_fusion
  15.2 0.0 copy-done.2
  15.2 1.2 fusion.34
  16.4 4.6 %copy.52.x_ref = bf16[128,4,3584]{2,1,0:T(4,128)(2,1)} copy(bf16[128,4,3584]{2,0,1:T(8,128)(2,1)S(1)} %fusion.34) | data formatting | bytes 7340032 | tf_op jit(solution)/shard_map/dkt,tc->dkc/dot_general | solution.py:100
  21.0 66.4 %shard_map.113 = bf16[128,4,3584]{2,1,0:T(4,128)(2,1)} custom-call(bf16[128,4,3584]{2,1,0:T(4,128)(2,1)} %copy.52.x_ref), custom_call_target="tpu_custom_call" | custom-call | bytes 7340032 | tf_op jit(solution)/shard_map/pallas_call | solution.py:54
  87.4 12.1 %fusion = f32[128,4,2048]{2,0,1:T(8,128)S(1)} fusion(bf16[1,3584,2048]{2,1,0:T(8,128)(2,1)} %param.13, bf16[128,4,3584]{2,1,0:T(4,128)(2,1)} %shard_map.113), kind=kOutput, calls=%fused_computation.4 | convolution fusion | flops 7516192768 | bytes 22544384 | tf_op jit(solution)/shard_map/skc,cf->skf/dot_general | solution.py:72
  99.5 7.5 %fusion.2 = bf16[128,4,3584]{2,0,1:T(8,128)(2,1)S(1)} fusion(bf16[1,1024,3584]{2,1,0:T(8,128)(2,1)} %param.14, f32[128,4,2048]{2,0,1:T(8,128)S(1)} %fusion), kind=kOutput, calls=%fused_computation.6 | convolution fusion | flops 3761242112 | bytes 15204352 | tf_op jit(solution)/shard_map/skf,fc->skc/dot_general | solution.py:77
  107.0 4.7 %copy.51.x_ref = bf16[128,4,3584]{2,1,0:T(4,128)(2,1)} copy(bf16[128,4,3584]{2,0,1:T(8,128)(2,1)S(1)} %fusion.2) | data formatting | bytes 7340032 | tf_op jit(solution)/shard_map/skf,fc->skc/dot_general | solution.py:77
  111.6 0.0 copy-start.1
  111.6 0.0 copy-start.3
  111.6 73.7 %shard_map.114 = bf16[128,4,3584]{2,1,0:T(4,128)(2,1)} custom-call(bf16[128,4,3584]{2,1,0:T(4,128)(2,1)} %copy.51.x_ref), custom_call_target="tpu_custom_call" | custom-call | bytes 7340032 | tf_op jit(solution)/shard_map/pallas_call | solution.py:54
  185.4 0.1 copy.37
  185.5 0.1 fusion.22
  185.7 0.0 copy-done.1
  185.7 0.7 gather_fusion.1
  186.3 0.1 iota_compare_fusion.1
  186.4 0.0 copy-done.3
  186.4 6.6 %gather_fusion = bf16[256,3584]{1,0:T(8,128)(2,1)} fusion(bf16[128,4,3584]{2,1,0:T(4,128)(2,1)} %shard_map.114, s32[256]{0:T(256)S(1)} %bitcast.27), kind=kCustom, calls=%fused_computation | custom fusion | bytes 3672064 | tf_op jit(solution)/shard_map/gather | solution.py:109
  193.1 3.7 %fusion.4 = bf16[2,16,3584]{2,1,0:T(8,128)(2,1)} fusion(f32[2,16,8]{2,1,0:T(8,128)S(1)} %copy.36, bf16[256,3584]{1,0:T(8,128)(2,1)} %gather_fusion), kind=kLoop, calls=%fused_computation.11 | loop fusion | flops 2637824 | bytes 2065408 | tf_op jit(solution)/shard_map/reduce_sum | solution.py:112
  196.7 0.0 copy-done
  196.7 0.5 fusion.20
  197.3 0.0 collective-permute-done
  197.3 2.3 %gather_fusion.3 = bf16[16,128,576]{1,2,0:T(8,128)(2,1)} fusion(bf16[4,128,576]{1,2,0:T(8,128)(2,1)S(1)} %collective-permute-done, s32[1024]{0:T(1024)S(1)} %pad_clamp_fusion), kind=kCustom, calls=%fused_computation.3 | custom fusion | bytes 4718656 | tf_op jit(solution)/shard_map/gather | solution.py:172
  199.5 4.3 %copy.38 = bf16[16,128,576]{2,1,0:T(8,128)(2,1)} copy(bf16[16,128,576]{1,2,0:T(8,128)(2,1)} %gather_fusion.3) | data formatting | bytes 4718592 | tf_op jit(solution)/shard_map/gather | solution.py:172
  203.9 2.9 %broadcast_select_fusion = bf16[16,128,576]{2,1,0:T(8,128)(2,1)S(1)} fusion(bf16[16,128,576]{2,1,0:T(8,128)(2,1)} %copy.38, bf16[16,128,576]{2,1,0:T(8,128)(2,1)} %copy.39, pred[16]{0:T(512)(128)(4,1)S(1)} %broadcast_compare_fusion), kind=kLoop, calls=%fused_computation.13 | loop fusion | flops 1179648 | bytes 7077904 | tf_op jit(solution)/shard_map/jit(_where)/select_n | solution.py:172
  206.7 1.3 fusion.33
  208.0 0.4 fusion.15
  208.5 1.6 divide_convert_fusion
  (14 shorter events, 0.1 us)
Async XLA Ops:
  0.6 196.1 %copy-start = (bf16[16,64,576]{2,1,0:T(8,128)(2,1)S(1)}, bf16[16,64,576]{2,1,0:T(8,128)(2,1)}, u32[]{:S(2)}) copy-start(bf16[16,64,576]{2,1,0:T(8,128)(2,1)} %param.15) | copy-start | bytes 3538948
  5.0 8.9 %copy-start.6 = (s32[16]{0:T(128)S(1)}, s32[16]{0:T(128)}, u32[]{:S(2)}) copy-start(s32[16]{0:T(128)} %param.19) | copy-start | bytes 196
  5.0 8.9 %copy-start.4 = (f32[2,16,8]{1,2,0:T(8,128)S(1)}, f32[2,16,8]{1,2,0:T(8,128)}, u32[]{:S(2)}) copy-start(f32[2,16,8]{1,2,0:T(8,128)} %param.12) | copy-start | bytes 3076
  5.1 9.0 %copy-start.5 = (s32[2,16,8]{1,2,0:T(8,128)S(1)}, s32[2,16,8]{1,2,0:T(8,128)}, u32[]{:S(2)}) copy-start(s32[2,16,8]{1,2,0:T(8,128)} %param.11) | copy-start | bytes 3076
  5.1 192.2 %collective-permute-start = (bf16[4,128,576]{1,2,0:T(8,128)(2,1)S(1)}, bf16[4,128,576]{1,2,0:T(8,128)(2,1)S(1)}, u32[]{:S(2)}, u32[]{:S(2)}) collective-permute-start(bf16[4,128,576]{1,2,0:T(8,128)(2,1)S(1)} %gather_fusion.2), channel_id=1, source_target_pairs={{0,64},{8,72},{16,80},{24,88},{32,96},{40,104},{48,112},{56,120},{... | collective-permute-start | bytes 1769480 | tf_op jit(solution)/shard_map/ppermute | solution.py:68
  9.6 5.6 %copy-start.2 = (bf16[2,16,3584]{2,1,0:T(8,128)(2,1)S(1)}, bf16[2,16,3584]{2,1,0:T(8,128)(2,1)}, u32[]{:S(2)}) copy-start(bf16[2,16,3584]{2,1,0:T(8,128)(2,1)} %param.10) | copy-start | bytes 688132
  111.6 74.0 %copy-start.1 = (s32[2048]{0:T(1024)S(1)}, s32[2048]{0:T(1024)}, u32[]{:S(2)}) copy-start(s32[2048]{0:T(1024)} %param.18) | copy-start | bytes 24580
  111.6 74.8 %copy-start.3 = (bf16[16,576]{1,0:T(8,128)(2,1)S(1)}, bf16[16,576]{1,0:T(8,128)(2,1)}, u32[]{:S(2)}) copy-start(bf16[16,576]{1,0:T(8,128)(2,1)} %param.16) | copy-start | bytes 55300

commit v2 on v1

--- a/solution.py
+++ b/solution.py
@@ -155,11 +155,16 @@
 ):
     n_ep = lax.axis_size("ep")
     expert_count = lax.axis_size("dp") * n_ep
-    packed, target = pack_rows(hidden, routes, expert_count, CAP)
-    received = all_to_all_rows(packed, n_ep, expert_count, 0)
-    finished = expert_rows(received, expert_in[0], expert_out[0])
-    returned = all_to_all_rows(finished, n_ep, expert_count, 1)
-    mixed = unpack_rows(returned, target, route_weights)
+    packs = [
+        pack_rows(hidden[step : step + 1], routes[step : step + 1], expert_count, CAP)
+        for step in range(STEPS)
+    ]
+    received = [lax.all_to_all(p[0], ("dp", "ep"), 0, 0, tiled=True) for p in packs]
+    finished = [expert_rows(r, expert_in[0], expert_out[0]) for r in received]
+    returned = [lax.all_to_all(f, ("dp", "ep"), 0, 0, tiled=True) for f in finished]
+    mixed = jnp.concatenate(
+        [unpack_rows(returned[step], packs[step][1], route_weights[step : step + 1]) for step in range(STEPS)]
+    )
     row_count = swapped.shape[0]
     top_bit = lax.axis_size("dp").bit_length() - 2
     outgoing = jnp.argsort(1 - swapped, stable=True)[:MOVE]

time: 213 us -> 156 us (0.73)
  Pallas kernels: 140 us -> 0 us
  waiting for transfers between devices: 0.01 us -> 47.5 us
  starting transfers between devices: 4.51 us -> 26.9 us
  matrix products: 24.1 us -> 31.9 us
  local copies, waits for them, and re-layouts: 30.4 us -> 37.7 us
    pallas_call x2 -> x0, Pallas kernels: 140 us -> none  [all_to_all_rows(): pl.pallas_call(functools.partial(_a2a_kernel, n_ep, n_all), out_shape=jax...]
    all_to_all x0 -> x4, waiting for transfers between devices: none -> 47.5 us  [the longest x2 27.9 us: per_device(): lax.all_to_all(f, ('dp', 'ep'), 0, 0, tiled=True)]
    all_to_all x0 -> x4, starting transfers between devices: none -> 22.4 us  [the longest x2 12.7 us: per_device(): lax.all_to_all(p[0], ('dp', 'ep'), 0, 0, tiled=True)]
    convert_element_type x0 -> x4, local copies, waits for them, and re-layouts: none -> 14.1 us  [the longest x2 7.78 us: pack_rows(): packed = jnp.einsum('dkt,tc->dkc', select, flat_tokens, preferred_element...]
    dot_general x2 -> x0, local copies, waits for them, and re-layouts: 9.3 us -> none  [the longest x1 4.67 us: expert_rows(): jnp.einsum('skf,fc->skc', activated, expert_out, preferred_element_type=j...]
    dot_general x1 -> x2, matrix products: 12.1 us -> 15.6 us  [expert_rows(): jnp.einsum('skc,cf->skf', picked, expert_in, preferred_element_type=jnp.f...]
    dot_general x1 -> x2, matrix products: 7.47 us -> 10.4 us  [expert_rows(): jnp.einsum('skf,fc->skc', activated, expert_out, preferred_element_type=j...]
    gather x1 -> x2, local copies, waits for them, and re-layouts: 6.64 us -> 6.66 us  [unpack_rows(): returned[flat_target // width, flat_target % width]]
  transfers between devices with their start and end apart: 1 -> 5, of which waited for: 0 -> 4; matrix products, arithmetic and copies ran while one was open for 23% -> 45% of each run, Pallas kernels for 67% -> 0%
where the time goes in v2:
time: 156 us; the launch traced here: 155 us
  waiting for transfers between devices  47.5 us (30%)
  local copies, waits for them, and re-layouts  37.7 us (24%)
  matrix products  31.9 us (20%)
  starting transfers between devices  26.9 us (17%)
  other arithmetic  10 us (6%)
    all_to_all x2, waiting for transfers between devices, per_device(): lax.all_to_all(f, ('dp', 'ep'), 0, 0, tiled=True)  27.9 us
    all_to_all x2, waiting for transfers between devices, per_device(): lax.all_to_all(p[0], ('dp', 'ep'), 0, 0, tiled=True)  19.5 us
    dot_general x2, matrix products, expert_rows(): jnp.einsum('skc,cf->skf', picked, expert_in, preferred_element_type=jnp.f...  15.6 us
    all_to_all x2, starting transfers between devices, per_device(): lax.all_to_all(p[0], ('dp', 'ep'), 0, 0, tiled=True)  12.7 us
    dot_general x2, matrix products, expert_rows(): jnp.einsum('skf,fc->skc', activated, expert_out, preferred_element_type=j...  10.4 us
    all_to_all x2, starting transfers between devices, per_device(): lax.all_to_all(f, ('dp', 'ep'), 0, 0, tiled=True)  9.69 us
    convert_element_type x2, local copies, waits for them, and re-layouts, pack_rows(): packed = jnp.einsum('dkt,tc->dkc', select, flat_tokens, preferred_element...  7.78 us
    gather x2, local copies, waits for them, and re-layouts, per_device(): incoming_cache[arrival]  6.67 us
  transfers between devices with their start and end apart: 5, of which 4 were waited for; matrix products, arithmetic and copies ran while one was open for 45% of the time, Pallas kernels for 0%

profile of v2, /device:TPU:1, one launch (start us, length us, event | category | flops | bytes accessed | tf_op | source)
XLA Modules:
  0.0 154.9 jit_solution(5479720311723835104)
XLA Ops:
  0.6 0.0 copy-start
  0.6 0.0 copy-start.3
  0.7 0.8 compare_select_fusion.2
  1.5 1.2 sort.17
  2.7 2.3 %gather_fusion.3 = bf16[4,128,576]{1,2,0:T(8,128)(2,1)S(1)} fusion(bf16[16,128,576]{1,2,0:T(8,128)(2,1)} %param.17, s32[1024]{0:T(1024)S(1)} %pad_clamp_fusion.1), kind=kCustom, calls=%fused_computation.3 | custom fusion | bytes 1179664 | tf_op jit(solution)/shard_map/gather | solution.py:176
  5.1 4.5 %collective-permute-start = (bf16[4,128,576]{1,2,0:T(8,128)(2,1)S(1)}, bf16[4,128,576]{1,2,0:T(8,128)(2,1)S(1)}, u32[]{:S(2)}, u32[]{:S(2)}) collective-permute-start(bf16[4,128,576]{1,2,0:T(8,128)(2,1)S(1)} %gather_fusion.3), channel_id=1, source_target_pairs={{0,64},{8,72},{16,80},{24,88},{32,96},{40,104},{48,112},{56,120},{... | collective-permute-start | bytes 1769480 | tf_op jit(solution)/shard_map/ppermute | solution.py:68
  9.6 0.7 fusion.61
  10.3 0.1 copy.81
  10.4 0.1 eq.108
  10.4 0.1 fusion.38
  10.5 0.2 reduce_window_sum.25
  10.7 0.2 select_reduce_fusion
  10.9 0.1 reshape.594
  11.0 0.1 copy.80
  11.1 0.1 eq.100
  11.2 0.1 fusion.39
  11.3 0.2 reduce_window_sum.24
  11.4 0.2 select_reduce_fusion.1
  11.6 0.1 reshape.591
  11.7 0.2 compare_reduce_fusion.1
  11.9 0.0 copy-done.3
  11.9 0.7 convolution_convert_fusion.1
  12.6 3.1 %copy.60 = bf16[128,2,3584]{2,1,0:T(2,128)(2,1)} copy(bf16[128,2,3584]{2,0,1:T(8,128)(2,1)S(1)} %convolution_convert_fusion.1) | data formatting | bytes 3670016 | tf_op jit(solution)/shard_map/convert_element_type | solution.py:102
  15.7 8.3 %all-to-all-start = ((bf16[128,2,3584]{2,1,0:T(2,128)(2,1)}), bf16[128,2,3584]{2,1,0:T(2,128)(2,1)}, u32[]{:S(2)}, u32[]{:S(2)}) async-start(bf16[128,2,3584]{2,1,0:T(2,128)(2,1)} %copy.60), calls=%async_computation | async-start | bytes 3670016 | tf_op jit(solution)/shard_map/all_to_all | solution.py:162
  24.0 1.9 %convolution_convert_fusion = bf16[128,2,3584]{2,0,1:T(8,128)(2,1)} fusion(pred[128,2,16]{0,2,1:T(8,128)(4,1)S(1)} %get-tuple-element.5, bf16[2,16,3584]{2,1,0:T(8,128)(2,1)S(1)} %copy-done.3), kind=kOutput, calls=%fused_computation.15 | convolution fusion | flops 30277632 | bytes 1953792 | tf_op jit(solution)/shard_map/dkt,tc->dkc/dot_general | solution.py:100
  25.9 0.0 copy-done.5
  25.9 4.3 %copy.73 = bf16[16,128,576]{2,1,0:T(8,128)(2,1)} copy(bf16[16,128,576]{1,2,0:T(8,128)(2,1)} %param.17) | data formatting | bytes 4718592 | tf_op args[7]
  30.3 0.1 reshape.593
  30.4 0.1 reshape.596
  30.5 0.0 copy-done.6
  30.5 0.1 copy.71
  30.6 0.1 copy.63
  30.7 4.7 %copy.67 = bf16[128,2,3584]{2,1,0:T(2,128)(2,1)} copy(bf16[128,2,3584]{2,0,1:T(8,128)(2,1)} %convolution_convert_fusion) | data formatting | bytes 3670016 | tf_op jit(solution)/shard_map/convert_element_type | solution.py:102
  35.3 0.1 copy.70
  35.4 0.7 gather_fusion.2
  36.1 0.1 fusion.42
  36.3 0.1 iota_compare_fusion.2
  36.4 0.5 fusion.40
  36.9 0.0 collective-permute-done
  36.9 2.3 %gather_fusion.4 = bf16[16,128,576]{1,2,0:T(8,128)(2,1)} fusion(bf16[4,128,576]{1,2,0:T(8,128)(2,1)S(1)} %collective-permute-done, s32[1024]{0:T(1024)S(1)} %pad_clamp_fusion), kind=kCustom, calls=%fused_computation.4 | custom fusion | bytes 4718656 | tf_op jit(solution)/shard_map/gather | solution.py:177
  39.2 4.4 %copy.72 = bf16[16,128,576]{2,1,0:T(8,128)(2,1)} copy(bf16[16,128,576]{1,2,0:T(8,128)(2,1)} %gather_fusion.4) | data formatting | bytes 4718592 | tf_op jit(solution)/shard_map/gather | solution.py:177
  43.6 7.9 %all-to-all-done = bf16[128,2,3584]{2,1,0:T(2,128)(2,1)} async-done(((bf16[128,2,3584]{2,1,0:T(2,128)(2,1)}), bf16[128,2,3584]{2,1,0:T(2,128)(2,1)}, u32[]{:S(2)}, u32[]{:S(2)}) %all-to-all-start) | async-done | bytes 1835040 | tf_op jit(solution)/shard_map/all_to_all | solution.py:162
  51.4 4.3 %all-to-all-start.2 = ((bf16[128,2,3584]{2,1,0:T(2,128)(2,1)}), bf16[128,2,3584]{2,1,0:T(2,128)(2,1)S(1)}, u32[]{:S(2)}, u32[]{:S(2)}) async-start(bf16[128,2,3584]{2,1,0:T(2,128)(2,1)} %copy.67), calls=%async_computation.2 | async-start | bytes 3670016 | tf_op jit(solution)/shard_map/all_to_all | solution.py:162
  55.8 7.8 %fusion.2 = f32[128,2,2048]{2,0,1:T(8,128)S(1)} fusion(bf16[1,3584,2048]{2,1,0:T(8,128)(2,1)} %param.13, bf16[128,2,3584]{2,1,0:T(2,128)(2,1)} %all-to-all-done), kind=kOutput, calls=%fused_computation.7 | convolution fusion | flops 3758096384 | bytes 18612224 | tf_op jit(solution)/shard_map/skc,cf->skf/dot_general | solution.py:72
  63.6 5.2 %fusion.8 = bf16[128,2,3584]{2,0,1:T(8,128)(2,1)S(1)} fusion(bf16[1,1024,3584]{2,1,0:T(8,128)(2,1)} %param.14, f32[128,2,2048]{2,0,1:T(8,128)S(1)} %fusion.2), kind=kOutput, calls=%fused_computation.13 | convolution fusion | flops 1881538560 | bytes 11272192 | tf_op jit(solution)/shard_map/skf,fc->skc/dot_general | solution.py:77
  68.8 3.2 %copy.62 = bf16[128,2,3584]{2,1,0:T(2,128)(2,1)} copy(bf16[128,2,3584]{2,0,1:T(8,128)(2,1)S(1)} %fusion.8) | data formatting | bytes 3670016 | tf_op jit(solution)/shard_map/convert_element_type | solution.py:79
  72.0 11.7 %all-to-all-done.2 = bf16[128,2,3584]{2,1,0:T(2,128)(2,1)S(1)} async-done(((bf16[128,2,3584]{2,1,0:T(2,128)(2,1)}), bf16[128,2,3584]{2,1,0:T(2,128)(2,1)S(1)}, u32[]{:S(2)}, u32[]{:S(2)}) %all-to-all-start.2) | async-done | bytes 1835040 | tf_op jit(solution)/shard_map/all_to_all | solution.py:162
  83.6 1.3 copy-done.2
  84.9 4.3 %all-to-all-start.1 = ((bf16[128,2,3584]{2,1,0:T(2,128)(2,1)}), bf16[128,2,3584]{2,1,0:T(2,128)(2,1)S(1)}, u32[]{:S(2)}, u32[]{:S(2)}) async-start(bf16[128,2,3584]{2,1,0:T(2,128)(2,1)} %copy.62), calls=%async_computation.1 | async-start | bytes 3670016 | tf_op jit(solution)/shard_map/all_to_all | solution.py:164
  89.3 7.8 %fusion = f32[128,2,2048]{2,0,1:T(8,128)S(1)} fusion(bf16[1,3584,2048]{2,1,0:T(8,128)(2,1)} %param.13, bf16[128,2,3584]{2,1,0:T(2,128)(2,1)} %copy-done.2), kind=kOutput, calls=%fused_computation.5 | convolution fusion | flops 3758096384 | bytes 18612224 | tf_op jit(solution)/shard_map/skc,cf->skf/dot_general | solution.py:72
  97.1 5.2 %fusion.11 = bf16[128,2,3584]{2,0,1:T(8,128)(2,1)S(1)} fusion(bf16[1,1024,3584]{2,1,0:T(8,128)(2,1)} %param.14, f32[128,2,2048]{2,0,1:T(8,128)S(1)} %fusion), kind=kOutput, calls=%fused_computation.14 | convolution fusion | flops 1881538560 | bytes 11272192 | tf_op jit(solution)/shard_map/skf,fc->skc/dot_general | solution.py:77
  102.3 3.2 %copy.69 = bf16[128,2,3584]{2,1,0:T(2,128)(2,1)} copy(bf16[128,2,3584]{2,0,1:T(8,128)(2,1)S(1)} %fusion.11) | data formatting | bytes 3670016 | tf_op jit(solution)/shard_map/convert_element_type | solution.py:79
  105.4 11.7 %all-to-all-done.1 = bf16[128,2,3584]{2,1,0:T(2,128)(2,1)S(1)} async-done(((bf16[128,2,3584]{2,1,0:T(2,128)(2,1)}), bf16[128,2,3584]{2,1,0:T(2,128)(2,1)S(1)}, u32[]{:S(2)}, u32[]{:S(2)}) %all-to-all-start.1) | async-done | bytes 1835040 | tf_op jit(solution)/shard_map/all_to_all | solution.py:164
  117.1 5.3 %all-to-all-start.3 = ((bf16[128,2,3584]{2,1,0:T(2,128)(2,1)}), bf16[128,2,3584]{2,1,0:T(2,128)(2,1)}, u32[]{:S(2)}, u32[]{:S(2)}) async-start(bf16[128,2,3584]{2,1,0:T(2,128)(2,1)} %copy.69), calls=%async_computation.3 | async-start | bytes 3670016 | tf_op jit(solution)/shard_map/all_to_all | solution.py:164
  122.5 2.9 %broadcast_select_fusion = bf16[16,128,576]{2,1,0:T(8,128)(2,1)S(1)} fusion(bf16[16,128,576]{2,1,0:T(8,128)(2,1)} %copy.72, bf16[16,128,576]{2,1,0:T(8,128)(2,1)} %copy.73, pred[16]{0:T(512)(128)(4,1)S(1)} %broadcast_compare_fusion), kind=kLoop, calls=%fused_computation.17 | loop fusion | flops 1179648 | bytes 7077904 | tf_op jit(solution)/shard_map/jit(_where)/select_n | solution.py:177
  125.4 1.3 fusion.62
  126.6 0.4 fusion.30
  127.1 1.6 %divide_convert_fusion = bf16[16,64,512]{2,1,0:T(8,128)(2,1)} fusion(bf16[16,128,576]{2,1,0:T(8,128)(2,1)S(1)} %broadcast_select_fusion, f32[16,64]{1,0:T(8,128)S(1)} %get-tuple-element.7, f32[16,512]{1,0:T(8,128)S(1)} %slice_convert_fusion, f32[16,64]{1,0:T(8,128)S(1)} %convert_element_type.148, f32[16,64,128]{2,1,0:T(8,128)S(1)} %get-tuple-element.15, ...), kind=kOutput, calls=%fused_computation.20 | convolution fusion | flops 136577024 | bytes 3727360 | tf_op jit(solution)/shard_map/nhl,nlc->nhc/dot_general | solution.py:131
  128.7 3.3 %gather_fusion = bf16[128,3584]{1,0:T(8,128)(2,1)} fusion(bf16[128,2,3584]{2,1,0:T(2,128)(2,1)S(1)} %all-to-all-done.1, s32[128]{0:T(128)S(1)} %fusion.58), kind=kCustom, calls=%fused_computation | custom fusion | bytes 1836032 | tf_op jit(solution)/shard_map/gather | solution.py:109
  131.9 1.9 %fusion.17 = bf16[16,3584]{1,0:T(8,128)(2,1)S(1)} fusion(bf16[128,3584]{1,0:T(8,128)(2,1)} %gather_fusion, f32[16,8]{1,0:T(8,128)S(1)} %copy.63), kind=kLoop, calls=%fused_computation.24 | loop fusion | flops 1318912 | bytes 1032704 | tf_op jit(solution)/shard_map/reduce_sum | solution.py:112
  133.8 16.2 %all-to-all-done.3 = bf16[128,2,3584]{2,1,0:T(2,128)(2,1)} async-done(((bf16[128,2,3584]{2,1,0:T(2,128)(2,1)}), bf16[128,2,3584]{2,1,0:T(2,128)(2,1)}, u32[]{:S(2)}, u32[]{:S(2)}) %all-to-all-start.3) | async-done | bytes 1835040 | tf_op jit(solution)/shard_map/all_to_all | solution.py:164
  150.0 3.4 %gather_fusion.1 = bf16[128,3584]{1,0:T(8,128)(2,1)S(1)} fusion(bf16[128,2,3584]{2,1,0:T(2,128)(2,1)} %all-to-all-done.3, s32[128]{0:T(128)S(1)} %fusion.57), kind=kCustom, calls=%fused_computation.1 | custom fusion | bytes 1836032 | tf_op jit(solution)/shard_map/gather | solution.py:109
  153.4 0.7 fusion.16
  154.1 0.7 pad_maximum_fusion
  (25 shorter events, 0.2 us)
Async XLA Ops:
  0.6 35.7 %copy-start = (bf16[16,64,576]{2,1,0:T(8,128)(2,1)S(1)}, bf16[16,64,576]{2,1,0:T(8,128)(2,1)}, u32[]{:S(2)}) copy-start(bf16[16,64,576]{2,1,0:T(8,128)(2,1)} %param.15) | copy-start | bytes 3538948
  0.6 11.2 %copy-start.3 = (bf16[2,16,3584]{2,1,0:T(8,128)(2,1)S(1)}, bf16[2,16,3584]{2,1,0:T(8,128)(2,1)}, u32[]{:S(2)}) copy-start(bf16[2,16,3584]{2,1,0:T(8,128)(2,1)} %param.10) | copy-start | bytes 688132
  5.1 31.8 %collective-permute-start = (bf16[4,128,576]{1,2,0:T(8,128)(2,1)S(1)}, bf16[4,128,576]{1,2,0:T(8,128)(2,1)S(1)}, u32[]{:S(2)}, u32[]{:S(2)}) collective-permute-start(bf16[4,128,576]{1,2,0:T(8,128)(2,1)S(1)} %gather_fusion.3), channel_id=1, source_target_pairs={{0,64},{8,72},{16,80},{24,88},{32,96},{40,104},{48,112},{56,120},{... | collective-permute-start | bytes 1769480 | tf_op jit(solution)/shard_map/ppermute | solution.py:68
  15.7 10.3 %copy-start.5 = (f32[2,16,8]{1,2,0:T(8,128)S(1)}, f32[2,16,8]{1,2,0:T(8,128)}, u32[]{:S(2)}) copy-start(f32[2,16,8]{1,2,0:T(8,128)} %param.12) | copy-start | bytes 3076
  15.7 35.8 %all-to-all-start = ((bf16[128,2,3584]{2,1,0:T(2,128)(2,1)}), bf16[128,2,3584]{2,1,0:T(2,128)(2,1)}, u32[]{:S(2)}, u32[]{:S(2)}) async-start(bf16[128,2,3584]{2,1,0:T(2,128)(2,1)} %copy.60), calls=%async_computation | async-start | bytes 3670016 | tf_op jit(solution)/shard_map/all_to_all | solution.py:162
  25.9 4.5 %copy-start.6 = (s32[16]{0:T(128)S(1)}, s32[16]{0:T(128)}, u32[]{:S(2)}) copy-start(s32[16]{0:T(128)} %param.19) | copy-start | bytes 196
  30.3 5.1 %copy-start.1 = (s32[2048]{0:T(1024)S(1)}, s32[2048]{0:T(1024)}, u32[]{:S(2)}) copy-start(s32[2048]{0:T(1024)} %param.18) | copy-start | bytes 24580
  30.7 5.7 %copy-start.4 = (bf16[16,576]{1,0:T(8,128)(2,1)S(1)}, bf16[16,576]{1,0:T(8,128)(2,1)}, u32[]{:S(2)}) copy-start(bf16[16,576]{1,0:T(8,128)(2,1)} %param.16) | copy-start | bytes 55300
  51.4 32.2 %all-to-all-start.2 = ((bf16[128,2,3584]{2,1,0:T(2,128)(2,1)}), bf16[128,2,3584]{2,1,0:T(2,128)(2,1)S(1)}, u32[]{:S(2)}, u32[]{:S(2)}) async-start(bf16[128,2,3584]{2,1,0:T(2,128)(2,1)} %copy.67), calls=%async_computation.2 | async-start | bytes 3670016 | tf_op jit(solution)/shard_map/all_to_all | solution.py:162
  83.6 1.3 copy-start.2
  84.9 32.2 %all-to-all-start.1 = ((bf16[128,2,3584]{2,1,0:T(2,128)(2,1)}), bf16[128,2,3584]{2,1,0:T(2,128)(2,1)S(1)}, u32[]{:S(2)}, u32[]{:S(2)}) async-start(bf16[128,2,3584]{2,1,0:T(2,128)(2,1)} %copy.62), calls=%async_computation.1 | async-start | bytes 3670016 | tf_op jit(solution)/shard_map/all_to_all | solution.py:164
  117.1 32.9 %all-to-all-start.3 = ((bf16[128,2,3584]{2,1,0:T(2,128)(2,1)}), bf16[128,2,3584]{2,1,0:T(2,128)(2,1)}, u32[]{:S(2)}, u32[]{:S(2)}) async-start(bf16[128,2,3584]{2,1,0:T(2,128)(2,1)} %copy.69), calls=%async_computation.3 | async-start | bytes 3670016 | tf_op jit(solution)/shard_map/all_to_all | solution.py:164

commit v3 on v2

--- a/solution.py
+++ b/solution.py
@@ -160,6 +160,9 @@
         for step in range(STEPS)
     ]
     received = [lax.all_to_all(p[0], ("dp", "ep"), 0, 0, tiled=True) for p in packs]
+    received[0], queries, fresh_key, latent_cache, swapped = lax.optimization_barrier(
+        (received[0], queries, fresh_key, latent_cache, swapped)
+    )
     finished = [expert_rows(r, expert_in[0], expert_out[0]) for r in received]
     returned = [lax.all_to_all(f, ("dp", "ep"), 0, 0, tiled=True) for f in finished]
     mixed = jnp.concatenate(

time: 156 us -> 178 us (1.14)
  waiting for transfers between devices: 47.5 us -> 63 us
  starting transfers between devices: 26.9 us -> 35.7 us
    all_to_all x2, waiting for transfers between devices: 19.5 us -> 35.5 us  [per_device(): lax.all_to_all(p[0], ('dp', 'ep'), 0, 0, tiled=True)]
    all_to_all x2, waiting for transfers between devices: 27.9 us -> 16.1 us  [per_device(): lax.all_to_all(f, ('dp', 'ep'), 0, 0, tiled=True)]
    ppermute x1, waiting for transfers between devices: 0.01 us -> 11.4 us  [swapped_2(): return lax.ppermute(value, axis, pairs)]
    all_to_all x2, starting transfers between devices: 9.69 us -> 15.5 us  [per_device(): lax.all_to_all(f, ('dp', 'ep'), 0, 0, tiled=True)]
    unnamed x17 -> x14, local copies, waits for them, and re-layouts: 5.8 us -> 0.17 us
    optimization_barrier x0 -> x1, local copies, waits for them, and re-layouts: none -> 4.37 us  [per_device(): lax.optimization_barrier((received[0], queries, fresh_key, latent_cache,...]
    all_to_all x2, starting transfers between devices: 12.7 us -> 16.8 us  [per_device(): lax.all_to_all(p[0], ('dp', 'ep'), 0, 0, tiled=True)]
  transfers between devices with their start and end apart: 5 -> 5, of which waited for: 4 -> 4; matrix products, arithmetic and copies ran while one was open for 45% -> 37% of each run, Pallas kernels for 0% -> 0%
where the time goes in v3:
time: 178 us; the launch traced here: 177 us
  waiting for transfers between devices  63 us (35%)
  local copies, waits for them, and re-layouts  36.8 us (21%)
  starting transfers between devices  35.7 us (20%)
  matrix products  31 us (17%)
  other arithmetic  9.22 us (5%)
    all_to_all x2, waiting for transfers between devices, per_device(): lax.all_to_all(p[0], ('dp', 'ep'), 0, 0, tiled=True)  35.5 us
    all_to_all x2, starting transfers between devices, per_device(): lax.all_to_all(p[0], ('dp', 'ep'), 0, 0, tiled=True)  16.8 us
    all_to_all x2, waiting for transfers between devices, per_device(): lax.all_to_all(f, ('dp', 'ep'), 0, 0, tiled=True)  16.1 us
    all_to_all x2, starting transfers between devices, per_device(): lax.all_to_all(f, ('dp', 'ep'), 0, 0, tiled=True)  15.5 us
    dot_general x2, matrix products, expert_rows(): jnp.einsum('skc,cf->skf', picked, expert_in, preferred_element_type=jnp.f...  15.1 us
    ppermute x1, waiting for transfers between devices, swapped_2(): return lax.ppermute(value, axis, pairs)  11.4 us
    dot_general x2, matrix products, expert_rows(): jnp.einsum('skf,fc->skc', activated, expert_out, preferred_element_type=j...  10.4 us
    gather x2, local copies, waits for them, and re-layouts, per_device(): incoming_cache[arrival]  7.72 us
  transfers between devices with their start and end apart: 5, of which 4 were waited for; matrix products, arithmetic and copies ran while one was open for 37% of the time, Pallas kernels for 0%

profile of v3, /device:TPU:1, one launch (start us, length us, event | category | flops | bytes accessed | tf_op | source)
XLA Modules:
  0.0 176.7 jit_solution(13735843295026614525)
XLA Ops:
  0.6 0.0 copy-start
  0.7 0.8 fusion.60
  1.5 0.1 copy.80
  1.5 0.1 eq.100
  1.6 0.1 fusion.38
  1.7 0.2 reduce_window_sum.24
  1.9 0.2 select_reduce_fusion.1
  2.1 0.1 reshape.591
  2.2 0.1 copy.81
  2.2 0.1 eq.108
  2.3 0.1 fusion.37
  2.4 0.2 reduce_window_sum.25
  2.6 0.2 select_reduce_fusion
  2.8 0.1 reshape.594
  2.9 0.2 compare_reduce_fusion.1
  3.1 1.6 convolution_convert_fusion
  4.6 3.1 %copy.67 = bf16[128,2,3584]{2,1,0:T(2,128)(2,1)} copy(bf16[128,2,3584]{2,0,1:T(8,128)(2,1)S(1)} %convolution_convert_fusion) | data formatting | bytes 3670016 | tf_op jit(solution)/shard_map/convert_element_type | solution.py:102
  7.8 11.5 %all-to-all-start.2 = ((bf16[128,2,3584]{2,1,0:T(2,128)(2,1)}), bf16[128,2,3584]{2,1,0:T(2,128)(2,1)S(1)}, u32[]{:S(2)}, u32[]{:S(2)}) async-start(bf16[128,2,3584]{2,1,0:T(2,128)(2,1)} %copy.67), calls=%async_computation.2 | async-start | bytes 3670016 | tf_op jit(solution)/shard_map/all_to_all | solution.py:162
  19.3 0.1 reshape.596
  19.4 0.1 reshape.593
  19.4 0.0 copy-done.4
  19.5 0.1 copy.70
  19.5 0.0 copy-done.2
  19.5 0.7 convolution_convert_fusion.1
  20.2 3.1 %copy.60 = bf16[128,2,3584]{2,1,0:T(2,128)(2,1)} copy(bf16[128,2,3584]{2,0,1:T(8,128)(2,1)S(1)} %convolution_convert_fusion.1) | data formatting | bytes 3670016 | tf_op jit(solution)/shard_map/convert_element_type | solution.py:102
  23.4 0.1 copy.63
  23.5 23.5 %all-to-all-done.2 = bf16[128,2,3584]{2,1,0:T(2,128)(2,1)S(1)} async-done(((bf16[128,2,3584]{2,1,0:T(2,128)(2,1)}), bf16[128,2,3584]{2,1,0:T(2,128)(2,1)S(1)}, u32[]{:S(2)}, u32[]{:S(2)}) %all-to-all-start.2) | async-done | bytes 1835040 | tf_op jit(solution)/shard_map/all_to_all | solution.py:162
  47.0 5.4 %all-to-all-start = ((bf16[128,2,3584]{2,1,0:T(2,128)(2,1)}), bf16[128,2,3584]{2,1,0:T(2,128)(2,1)}, u32[]{:S(2)}, u32[]{:S(2)}) async-start(bf16[128,2,3584]{2,1,0:T(2,128)(2,1)} %copy.60), calls=%async_computation | async-start | bytes 3670016 | tf_op jit(solution)/shard_map/all_to_all | solution.py:162
  52.3 7.3 %fusion = f32[128,2,2048]{2,0,1:T(8,128)S(1)} fusion(bf16[1,3584,2048]{2,1,0:T(8,128)(2,1)} %param.13, bf16[128,2,3584]{2,1,0:T(2,128)(2,1)S(1)} %all-to-all-done.2), kind=kOutput, calls=%fused_computation.5 | convolution fusion | flops 3758096384 | bytes 18612224 | tf_op jit(solution)/shard_map/skc,cf->skf/dot_general | solution.py:72
  59.6 5.2 %fusion.11 = bf16[128,2,3584]{2,0,1:T(8,128)(2,1)S(1)} fusion(bf16[1,1024,3584]{2,1,0:T(8,128)(2,1)} %param.14, f32[128,2,2048]{2,0,1:T(8,128)S(1)} %fusion), kind=kOutput, calls=%fused_computation.14 | convolution fusion | flops 1881538560 | bytes 11272192 | tf_op jit(solution)/shard_map/skf,fc->skc/dot_general | solution.py:77
  64.8 3.1 %copy.69 = bf16[128,2,3584]{2,1,0:T(2,128)(2,1)} copy(bf16[128,2,3584]{2,0,1:T(8,128)(2,1)S(1)} %fusion.11) | data formatting | bytes 3670016 | tf_op jit(solution)/shard_map/convert_element_type | solution.py:79
  67.9 12.0 %all-to-all-done = bf16[128,2,3584]{2,1,0:T(2,128)(2,1)} async-done(((bf16[128,2,3584]{2,1,0:T(2,128)(2,1)}), bf16[128,2,3584]{2,1,0:T(2,128)(2,1)}, u32[]{:S(2)}, u32[]{:S(2)}) %all-to-all-start) | async-done | bytes 1835040 | tf_op jit(solution)/shard_map/all_to_all | solution.py:162
  79.9 4.3 %all-to-all-start.3 = ((bf16[128,2,3584]{2,1,0:T(2,128)(2,1)}), bf16[128,2,3584]{2,1,0:T(2,128)(2,1)S(1)}, u32[]{:S(2)}, u32[]{:S(2)}) async-start(bf16[128,2,3584]{2,1,0:T(2,128)(2,1)} %copy.69), calls=%async_computation.3 | async-start | bytes 3670016 | tf_op jit(solution)/shard_map/all_to_all | solution.py:167
  84.2 7.8 %fusion.2 = f32[128,2,2048]{2,0,1:T(8,128)S(1)} fusion(bf16[1,3584,2048]{2,1,0:T(8,128)(2,1)} %param.13, bf16[128,2,3584]{2,1,0:T(2,128)(2,1)} %all-to-all-done), kind=kOutput, calls=%fused_computation.7 | convolution fusion | flops 3758096384 | bytes 18612224 | tf_op jit(solution)/shard_map/skc,cf->skf/dot_general | solution.py:72
  92.0 5.2 %fusion.8 = bf16[128,2,3584]{2,0,1:T(8,128)(2,1)S(1)} fusion(bf16[1,1024,3584]{2,1,0:T(8,128)(2,1)} %param.14, f32[128,2,2048]{2,0,1:T(8,128)S(1)} %fusion.2), kind=kOutput, calls=%fused_computation.13 | convolution fusion | flops 1881538560 | bytes 11272192 | tf_op jit(solution)/shard_map/skf,fc->skc/dot_general | solution.py:77
  97.2 3.2 %copy.62 = bf16[128,2,3584]{2,1,0:T(2,128)(2,1)} copy(bf16[128,2,3584]{2,0,1:T(8,128)(2,1)S(1)} %fusion.8) | data formatting | bytes 3670016 | tf_op jit(solution)/shard_map/convert_element_type | solution.py:79
  100.4 4.4 %copy.73 = bf16[16,128,576]{2,1,0:T(8,128)(2,1)} copy(bf16[16,128,576]{1,2,0:T(8,128)(2,1)} %param.17) | data formatting | bytes 4718592 | tf_op jit(solution)/shard_map/optimization_barrier | solution.py:163
  104.8 0.0 copy-done.5
  104.8 1.2 sort.17
  106.1 3.1 %gather_fusion.3 = bf16[4,128,576]{1,2,0:T(8,128)(2,1)} fusion(bf16[16,128,576]{1,2,0:T(8,128)(2,1)} %param.17, s32[1024]{0:T(1024)S(1)} %pad_clamp_fusion.1), kind=kCustom, calls=%fused_computation.3 | custom fusion | bytes 1179664 | tf_op jit(solution)/shard_map/gather | solution.py:179
  109.2 3.4 %collective-permute-start = (bf16[4,128,576]{1,2,0:T(8,128)(2,1)}, bf16[4,128,576]{1,2,0:T(8,128)(2,1)}, u32[]{:S(2)}, u32[]{:S(2)}) collective-permute-start(bf16[4,128,576]{1,2,0:T(8,128)(2,1)} %gather_fusion.3), channel_id=1, source_target_pairs={{0,64},{8,72},{16,80},{24,88},{32,96},{40,104},{48,112},{56,120},{... | collective-permute-start | bytes 1769480 | tf_op jit(solution)/shard_map/ppermute | solution.py:68
  112.6 0.1 copy.71
  112.7 0.0 copy-done.1
  112.7 0.7 gather_fusion.2
  113.4 0.1 fusion.41
  113.5 0.1 iota_compare_fusion.2
  113.6 0.0 copy-done.3
  113.6 0.0 copy-done
  113.6 0.5 fusion.39
  114.1 11.4 %collective-permute-done = bf16[4,128,576]{1,2,0:T(8,128)(2,1)} collective-permute-done((bf16[4,128,576]{1,2,0:T(8,128)(2,1)}, bf16[4,128,576]{1,2,0:T(8,128)(2,1)}, u32[]{:S(2)}, u32[]{:S(2)}) %collective-permute-start) | collective-permute-done | bytes 589856 | tf_op jit(solution)/shard_map/ppermute | solution.py:68
  125.6 3.4 %gather_fusion.4 = bf16[16,128,576]{1,2,0:T(8,128)(2,1)} fusion(bf16[4,128,576]{1,2,0:T(8,128)(2,1)} %collective-permute-done, s32[1024]{0:T(1024)S(1)} %pad_clamp_fusion), kind=kCustom, calls=%fused_computation.4 | custom fusion | bytes 4718656 | tf_op jit(solution)/shard_map/gather | solution.py:180
  128.9 4.4 %copy.72 = bf16[16,128,576]{2,1,0:T(8,128)(2,1)} copy(bf16[16,128,576]{1,2,0:T(8,128)(2,1)} %gather_fusion.4) | data formatting | bytes 4718592 | tf_op jit(solution)/shard_map/gather | solution.py:180
  133.3 0.0 all-to-all-done.3
  133.3 11.1 %all-to-all-start.1 = ((bf16[128,2,3584]{2,1,0:T(2,128)(2,1)}), bf16[128,2,3584]{2,1,0:T(2,128)(2,1)}, u32[]{:S(2)}, u32[]{:S(2)}) async-start(bf16[128,2,3584]{2,1,0:T(2,128)(2,1)} %copy.62), calls=%async_computation.1 | async-start | bytes 3670016 | tf_op jit(solution)/shard_map/all_to_all | solution.py:167
  144.4 2.9 %broadcast_select_fusion = bf16[16,128,576]{2,1,0:T(8,128)(2,1)S(1)} fusion(bf16[16,128,576]{2,1,0:T(8,128)(2,1)} %copy.72, bf16[16,128,576]{2,1,0:T(8,128)(2,1)} %copy.73, pred[16]{0:T(512)(128)(4,1)S(1)} %broadcast_compare_fusion), kind=kLoop, calls=%fused_computation.17 | loop fusion | flops 1179648 | bytes 7077904 | tf_op jit(solution)/shard_map/jit(_where)/select_n | solution.py:180
  147.3 1.2 fusion.61
  148.6 0.4 fusion.29
  149.0 1.6 divide_convert_fusion
  150.6 3.3 %gather_fusion.1 = bf16[128,3584]{1,0:T(8,128)(2,1)} fusion(bf16[128,2,3584]{2,1,0:T(2,128)(2,1)S(1)} %all-to-all-done.3, s32[128]{0:T(128)S(1)} %fusion.56), kind=kCustom, calls=%fused_computation.1 | custom fusion | bytes 1836032 | tf_op jit(solution)/shard_map/gather | solution.py:109
  153.8 1.9 %fusion.16 = bf16[16,3584]{1,0:T(8,128)(2,1)S(1)} fusion(bf16[128,3584]{1,0:T(8,128)(2,1)} %gather_fusion.1, f32[16,8]{1,0:T(8,128)S(1)} %copy.70), kind=kLoop, calls=%fused_computation.22 | loop fusion | flops 1318912 | bytes 1032704 | tf_op jit(solution)/shard_map/reduce_sum | solution.py:112
  155.7 16.1 %all-to-all-done.1 = bf16[128,2,3584]{2,1,0:T(2,128)(2,1)} async-done(((bf16[128,2,3584]{2,1,0:T(2,128)(2,1)}), bf16[128,2,3584]{2,1,0:T(2,128)(2,1)}, u32[]{:S(2)}, u32[]{:S(2)}) %all-to-all-start.1) | async-done | bytes 1835040 | tf_op jit(solution)/shard_map/all_to_all | solution.py:167
  171.8 3.4 %gather_fusion = bf16[128,3584]{1,0:T(8,128)(2,1)S(1)} fusion(bf16[128,2,3584]{2,1,0:T(2,128)(2,1)} %all-to-all-done.1, s32[128]{0:T(128)S(1)} %fusion.57), kind=kCustom, calls=%fused_computation | custom fusion | bytes 1836032 | tf_op jit(solution)/shard_map/gather | solution.py:109
  175.3 0.7 fusion.17
  176.0 0.7 pad_maximum_fusion
  (23 shorter events, 0.2 us)
Async XLA Ops:
  0.6 113.0 %copy-start = (bf16[16,64,576]{2,1,0:T(8,128)(2,1)S(1)}, bf16[16,64,576]{2,1,0:T(8,128)(2,1)}, u32[]{:S(2)}) copy-start(bf16[16,64,576]{2,1,0:T(8,128)(2,1)} %param.15) | copy-start | bytes 3538948
  7.8 11.7 %copy-start.4 = (f32[2,16,8]{1,2,0:T(8,128)S(1)}, f32[2,16,8]{1,2,0:T(8,128)}, u32[]{:S(2)}) copy-start(f32[2,16,8]{1,2,0:T(8,128)} %param.12) | copy-start | bytes 3076
  7.8 11.8 %copy-start.2 = (bf16[2,16,3584]{2,1,0:T(8,128)(2,1)S(1)}, bf16[2,16,3584]{2,1,0:T(8,128)(2,1)}, u32[]{:S(2)}) copy-start(bf16[2,16,3584]{2,1,0:T(8,128)(2,1)} %param.10) | copy-start | bytes 688132
  7.8 39.2 %all-to-all-start.2 = ((bf16[128,2,3584]{2,1,0:T(2,128)(2,1)}), bf16[128,2,3584]{2,1,0:T(2,128)(2,1)S(1)}, u32[]{:S(2)}, u32[]{:S(2)}) async-start(bf16[128,2,3584]{2,1,0:T(2,128)(2,1)} %copy.67), calls=%async_computation.2 | async-start | bytes 3670016 | tf_op jit(solution)/shard_map/all_to_all | solution.py:162
  47.0 32.9 %all-to-all-start = ((bf16[128,2,3584]{2,1,0:T(2,128)(2,1)}), bf16[128,2,3584]{2,1,0:T(2,128)(2,1)}, u32[]{:S(2)}, u32[]{:S(2)}) async-start(bf16[128,2,3584]{2,1,0:T(2,128)(2,1)} %copy.60), calls=%async_computation | async-start | bytes 3670016 | tf_op jit(solution)/shard_map/all_to_all | solution.py:162
  79.9 53.4 %all-to-all-start.3 = ((bf16[128,2,3584]{2,1,0:T(2,128)(2,1)}), bf16[128,2,3584]{2,1,0:T(2,128)(2,1)S(1)}, u32[]{:S(2)}, u32[]{:S(2)}) async-start(bf16[128,2,3584]{2,1,0:T(2,128)(2,1)} %copy.69), calls=%async_computation.3 | async-start | bytes 3670016 | tf_op jit(solution)/shard_map/all_to_all | solution.py:167
  100.4 4.4 %copy-start.5 = (s32[16]{0:T(128)S(1)}, s32[16]{0:T(128)}, u32[]{:S(2)}) copy-start(s32[16]{0:T(128)} %param.19) | copy-start | bytes 196
  100.4 12.3 %copy-start.1 = (s32[2048]{0:T(1024)S(1)}, s32[2048]{0:T(1024)}, u32[]{:S(2)}) copy-start(s32[2048]{0:T(1024)} %param.18) | copy-start | bytes 24580
  100.4 13.2 %copy-start.3 = (bf16[16,576]{1,0:T(8,128)(2,1)S(1)}, bf16[16,576]{1,0:T(8,128)(2,1)}, u32[]{:S(2)}) copy-start(bf16[16,576]{1,0:T(8,128)(2,1)} %param.16) | copy-start | bytes 55300
  109.2 16.4 %collective-permute-start = (bf16[4,128,576]{1,2,0:T(8,128)(2,1)}, bf16[4,128,576]{1,2,0:T(8,128)(2,1)}, u32[]{:S(2)}, u32[]{:S(2)}) collective-permute-start(bf16[4,128,576]{1,2,0:T(8,128)(2,1)} %gather_fusion.3), channel_id=1, source_target_pairs={{0,64},{8,72},{16,80},{24,88},{32,96},{40,104},{48,112},{56,120},{... | collective-permute-start | bytes 1769480 | tf_op jit(solution)/shard_map/ppermute | solution.py:68
  133.3 38.6 %all-to-all-start.1 = ((bf16[128,2,3584]{2,1,0:T(2,128)(2,1)}), bf16[128,2,3584]{2,1,0:T(2,128)(2,1)}, u32[]{:S(2)}, u32[]{:S(2)}) async-start(bf16[128,2,3584]{2,1,0:T(2,128)(2,1)} %copy.62), calls=%async_computation.1 | async-start | bytes 3670016 | tf_op jit(solution)/shard_map/all_to_all | solution.py:167

commit v4 on v1

--- a/solution.py
+++ b/solution.py
@@ -156,9 +156,9 @@
     n_ep = lax.axis_size("ep")
     expert_count = lax.axis_size("dp") * n_ep
     packed, target = pack_rows(hidden, routes, expert_count, CAP)
-    received = all_to_all_rows(packed, n_ep, expert_count, 0)
+    received = lax.all_to_all(packed, ("dp", "ep"), 0, 0, tiled=True)
     finished = expert_rows(received, expert_in[0], expert_out[0])
-    returned = all_to_all_rows(finished, n_ep, expert_count, 1)
+    returned = lax.all_to_all(finished, ("dp", "ep"), 0, 0, tiled=True)
     mixed = unpack_rows(returned, target, route_weights)
     row_count = swapped.shape[0]
     top_bit = lax.axis_size("dp").bit_length() - 2

time: 213 us -> 174 us (0.82); the launches traced: 210 us -> 173 us
  Pallas kernels: 140 us -> 0 us
  waiting for transfers between devices: 0.01 us -> 88.9 us
  starting transfers between devices: 4.51 us -> 21.1 us
  other arithmetic: 10.1 us -> 7.81 us
    pallas_call x2 -> x0, Pallas kernels: 140 us -> none  [all_to_all_rows(): pl.pallas_call(functools.partial(_a2a_kernel, n_ep, n_all), out_shape=jax...]
    all_to_all x0 -> x2, waiting for transfers between devices: none -> 47.2 us  [the longest x1 47.2 us: per_device(): received = lax.all_to_all(packed, ('dp', 'ep'), 0, 0, tiled=True)]
    ppermute x1, waiting for transfers between devices: 0.01 us -> 41.6 us  [swapped_2(): return lax.ppermute(value, axis, pairs)]
    all_to_all x0 -> x2, starting transfers between devices: none -> 17.4 us  [the longest x1 11.9 us: per_device(): received = lax.all_to_all(packed, ('dp', 'ep'), 0, 0, tiled=True)]
    convert_element_type x0 -> x2, local copies, waits for them, and re-layouts: none -> 9.33 us  [the longest x1 4.67 us: expert_rows(): return jnp.einsum('skf,fc->skc', activated, expert_out, preferred_element...]
    dot_general x2 -> x0, local copies, waits for them, and re-layouts: 9.3 us -> none  [the longest x1 4.67 us: expert_rows(): jnp.einsum('skf,fc->skc', activated, expert_out, preferred_element_type=j...]
    unnamed x17 -> x13, local copies, waits for them, and re-layouts: 4.53 us -> 5.28 us
  transfers between devices with their start and end apart: 1 -> 3, of which waited for: 0 -> 2; matrix products, arithmetic and copies ran while one was open for 23% -> 13% of each run, Pallas kernels for 67% -> 0%
where the time goes in v4:
time: 174 us; the launch traced here: 173 us
  waiting for transfers between devices  88.9 us (51%)
  local copies, waits for them, and re-layouts  29.9 us (17%)
  matrix products  24.8 us (14%)
  starting transfers between devices  21.1 us (12%)
  other arithmetic  7.81 us (4%)
    all_to_all x1, waiting for transfers between devices, per_device(): received = lax.all_to_all(packed, ('dp', 'ep'), 0, 0, tiled=True)  47.2 us
    ppermute x1, waiting for transfers between devices, swapped_2(): return lax.ppermute(value, axis, pairs)  41.6 us
    dot_general x1, matrix products, expert_rows(): jnp.einsum('skc,cf->skf', picked, expert_in, preferred_element_type=jnp.f...  12.1 us
    all_to_all x1, starting transfers between devices, per_device(): received = lax.all_to_all(packed, ('dp', 'ep'), 0, 0, tiled=True)  11.9 us
    dot_general x1, matrix products, expert_rows(): jnp.einsum('skf,fc->skc', activated, expert_out, preferred_element_type=j...  7.29 us
    gather x2, local copies, waits for them, and re-layouts, per_device(): incoming_cache[arrival]  6.61 us
    all_to_all x1, starting transfers between devices, per_device(): returned = lax.all_to_all(finished, ('dp', 'ep'), 0, 0, tiled=True)  5.46 us
    gather x1, local copies, waits for them, and re-layouts, unpack_rows(): returned[flat_target // width, flat_target % width]  5.39 us
  transfers between devices with their start and end apart: 3, of which 2 were waited for; matrix products, arithmetic and copies ran while one was open for 13% of the time, Pallas kernels for 0%

profile of v4, /device:TPU:1, one launch (start us, length us, event | category | flops | bytes accessed | tf_op | source)
XLA Modules:
  0.0 173.4 jit_solution(3126185363995547477)
XLA Ops:
  0.6 0.0 copy-start
  0.7 0.9 copy.39
  1.5 0.1 eq.38
  1.6 0.1 fusion.22
  1.7 0.2 reduce_window_sum.18
  1.9 0.2 select_reduce_fusion
  2.1 0.1 reshape.206
  2.2 0.1 add_add_fusion
  2.3 0.2 compare_reduce_fusion
  2.5 2.1 %convolution_convert_fusion = bf16[128,4,3584]{2,0,1:T(8,128)(2,1)S(1)} fusion(pred[128,4,32]{0,2,1:T(8,128)(4,1)S(1)} %compare_reduce_fusion, bf16[32,3584,1]{1,0,2:T(8,128)(2,1)} %bitcast.30), kind=kOutput, calls=%fused_computation.9 | convolution fusion | flops 119275520 | bytes 3915776 | tf_op jit(solution)/shard_map/dkt,tc->dkc/dot_general | solution.py:100
  4.6 4.7 %copy.43 = bf16[128,4,3584]{2,1,0:T(4,128)(2,1)} copy(bf16[128,4,3584]{2,0,1:T(8,128)(2,1)S(1)} %convolution_convert_fusion) | data formatting | bytes 7340032 | tf_op jit(solution)/shard_map/convert_element_type | solution.py:102
  9.3 11.9 %all-to-all-start = ((bf16[128,4,3584]{2,1,0:T(4,128)(2,1)}), bf16[128,4,3584]{2,1,0:T(4,128)(2,1)}, u32[]{:S(2)}, u32[]{:S(2)}) async-start(bf16[128,4,3584]{2,1,0:T(4,128)(2,1)} %copy.43), calls=%async_computation | async-start | bytes 7340032 | tf_op jit(solution)/shard_map/all_to_all | solution.py:159
  21.2 47.2 %all-to-all-done = bf16[128,4,3584]{2,1,0:T(4,128)(2,1)} async-done(((bf16[128,4,3584]{2,1,0:T(4,128)(2,1)}), bf16[128,4,3584]{2,1,0:T(4,128)(2,1)}, u32[]{:S(2)}, u32[]{:S(2)}) %all-to-all-start) | async-done | bytes 3670048 | tf_op jit(solution)/shard_map/all_to_all | solution.py:159
  68.5 12.1 %fusion = f32[128,4,2048]{2,0,1:T(8,128)S(1)} fusion(bf16[1,3584,2048]{2,1,0:T(8,128)(2,1)} %param.13, bf16[128,4,3584]{2,1,0:T(4,128)(2,1)} %all-to-all-done), kind=kOutput, calls=%fused_computation.4 | convolution fusion | flops 7516192768 | bytes 22544384 | tf_op jit(solution)/shard_map/skc,cf->skf/dot_general | solution.py:72
  80.5 7.3 %fusion.4 = bf16[128,4,3584]{2,0,1:T(8,128)(2,1)S(1)} fusion(bf16[1,1024,3584]{2,1,0:T(8,128)(2,1)} %param.14, f32[128,4,2048]{2,0,1:T(8,128)S(1)} %fusion), kind=kOutput, calls=%fused_computation.8 | convolution fusion | flops 3763077120 | bytes 15204352 | tf_op jit(solution)/shard_map/skf,fc->skc/dot_general | solution.py:77
  87.8 4.7 %copy.45 = bf16[128,4,3584]{2,1,0:T(4,128)(2,1)} copy(bf16[128,4,3584]{2,0,1:T(8,128)(2,1)S(1)} %fusion.4) | data formatting | bytes 7340032 | tf_op jit(solution)/shard_map/convert_element_type | solution.py:79
  92.5 0.0 copy-start.4
  92.5 5.5 %all-to-all-start.1 = ((bf16[128,4,3584]{2,1,0:T(4,128)(2,1)}), bf16[128,4,3584]{2,1,0:T(4,128)(2,1)}, u32[]{:S(2)}, u32[]{:S(2)}) async-start(bf16[128,4,3584]{2,1,0:T(4,128)(2,1)} %copy.45), calls=%async_computation.1 | async-start | bytes 7340032 | tf_op jit(solution)/shard_map/all_to_all | solution.py:161
  98.0 0.0 copy-done.4
  98.0 1.2 sort.17
  99.3 2.3 %gather_fusion.2 = bf16[4,128,576]{1,2,0:T(8,128)(2,1)S(1)} fusion(bf16[16,128,576]{1,2,0:T(8,128)(2,1)} %param.17, s32[1024]{0:T(1024)S(1)} %pad_clamp_fusion.1), kind=kCustom, calls=%fused_computation.2 | custom fusion | bytes 1179664 | tf_op jit(solution)/shard_map/gather | solution.py:171
  101.6 0.0 copy-start.3
  101.6 0.0 copy-start.1
  101.6 3.7 %collective-permute-start = (bf16[4,128,576]{1,2,0:T(8,128)(2,1)S(1)}, bf16[4,128,576]{1,2,0:T(8,128)(2,1)S(1)}, u32[]{:S(2)}, u32[]{:S(2)}) collective-permute-start(bf16[4,128,576]{1,2,0:T(8,128)(2,1)S(1)} %gather_fusion.2), channel_id=1, source_target_pairs={{0,64},{8,72},{16,80},{24,88},{32,96},{40,104},{48,112},{56,120},{... | collective-permute-start | bytes 1769480 | tf_op jit(solution)/shard_map/ppermute | solution.py:68
  105.4 0.1 reshape.208
  105.4 0.0 copy-start.2
  105.5 4.3 %copy.49 = bf16[16,128,576]{2,1,0:T(8,128)(2,1)} copy(bf16[16,128,576]{1,2,0:T(8,128)(2,1)} %param.17) | data formatting | bytes 4718592 | tf_op args[7]
  109.8 0.0 copy-done.3
  109.8 0.1 copy.46
  109.8 0.1 copy.47
  110.0 0.0 copy-done.1
  110.0 0.7 gather_fusion.1
  110.6 0.1 fusion.25
  110.8 0.1 iota_compare_fusion.1
  110.9 0.0 copy-done.2
  110.9 0.0 copy-done
  110.9 0.5 fusion.23
  111.4 41.6 %collective-permute-done = bf16[4,128,576]{1,2,0:T(8,128)(2,1)S(1)} collective-permute-done((bf16[4,128,576]{1,2,0:T(8,128)(2,1)S(1)}, bf16[4,128,576]{1,2,0:T(8,128)(2,1)S(1)}, u32[]{:S(2)}, u32[]{:S(2)}) %collective-permute-start) | collective-permute-done | bytes 589856 | tf_op jit(solution)/shard_map/ppermute | solution.py:68
  153.1 2.3 %gather_fusion.3 = bf16[16,128,576]{1,2,0:T(8,128)(2,1)} fusion(bf16[4,128,576]{1,2,0:T(8,128)(2,1)S(1)} %collective-permute-done, s32[1024]{0:T(1024)S(1)} %pad_clamp_fusion), kind=kCustom, calls=%fused_computation.3 | custom fusion | bytes 4718656 | tf_op jit(solution)/shard_map/gather | solution.py:172
  155.3 4.3 %copy.48 = bf16[16,128,576]{2,1,0:T(8,128)(2,1)} copy(bf16[16,128,576]{1,2,0:T(8,128)(2,1)} %gather_fusion.3) | data formatting | bytes 4718592 | tf_op jit(solution)/shard_map/gather | solution.py:172
  159.7 2.9 %broadcast_select_fusion = bf16[16,128,576]{2,1,0:T(8,128)(2,1)S(1)} fusion(bf16[16,128,576]{2,1,0:T(8,128)(2,1)} %copy.48, bf16[16,128,576]{2,1,0:T(8,128)(2,1)} %copy.49, pred[16]{0:T(512)(128)(4,1)S(1)} %broadcast_compare_fusion), kind=kLoop, calls=%fused_computation.13 | loop fusion | flops 1179648 | bytes 7077904 | tf_op jit(solution)/shard_map/jit(_where)/select_n | solution.py:172
  162.5 1.3 fusion.36
  163.8 0.4 fusion.18
  164.3 1.6 divide_convert_fusion
  165.8 0.0 all-to-all-done.1
  165.8 5.4 %gather_fusion = bf16[256,3584]{1,0:T(8,128)(2,1)S(1)} fusion(bf16[128,4,3584]{2,1,0:T(4,128)(2,1)} %all-to-all-done.1, s32[256]{0:T(256)S(1)} %bitcast.29), kind=kCustom, calls=%fused_computation | custom fusion | bytes 3672064 | tf_op jit(solution)/shard_map/gather | solution.py:109
  171.2 2.2 %fusion.7 = bf16[2,16,3584]{2,1,0:T(8,128)(2,1)} fusion(f32[2,16,8]{2,1,0:T(8,128)S(1)} %copy.46, bf16[256,3584]{1,0:T(8,128)(2,1)S(1)} %gather_fusion), kind=kLoop, calls=%fused_computation.11 | loop fusion | flops 2637824 | bytes 2065408 | tf_op jit(solution)/shard_map/reduce_sum | solution.py:112
  (15 shorter events, 0.1 us)
Async XLA Ops:
  0.6 110.3 %copy-start = (bf16[16,64,576]{2,1,0:T(8,128)(2,1)S(1)}, bf16[16,64,576]{2,1,0:T(8,128)(2,1)}, u32[]{:S(2)}) copy-start(bf16[16,64,576]{2,1,0:T(8,128)(2,1)} %param.15) | copy-start | bytes 3538948
  9.3 59.2 %all-to-all-start = ((bf16[128,4,3584]{2,1,0:T(4,128)(2,1)}), bf16[128,4,3584]{2,1,0:T(4,128)(2,1)}, u32[]{:S(2)}, u32[]{:S(2)}) async-start(bf16[128,4,3584]{2,1,0:T(4,128)(2,1)} %copy.43), calls=%async_computation | async-start | bytes 7340032 | tf_op jit(solution)/shard_map/all_to_all | solution.py:159
  92.5 5.5 %copy-start.4 = (s32[16]{0:T(128)S(1)}, s32[16]{0:T(128)}, u32[]{:S(2)}) copy-start(s32[16]{0:T(128)} %param.19) | copy-start | bytes 196
  92.5 73.3 %all-to-all-start.1 = ((bf16[128,4,3584]{2,1,0:T(4,128)(2,1)}), bf16[128,4,3584]{2,1,0:T(4,128)(2,1)}, u32[]{:S(2)}, u32[]{:S(2)}) async-start(bf16[128,4,3584]{2,1,0:T(4,128)(2,1)} %copy.45), calls=%async_computation.1 | async-start | bytes 7340032 | tf_op jit(solution)/shard_map/all_to_all | solution.py:161
  101.6 8.2 %copy-start.3 = (f32[2,16,8]{1,2,0:T(8,128)S(1)}, f32[2,16,8]{1,2,0:T(8,128)}, u32[]{:S(2)}) copy-start(f32[2,16,8]{1,2,0:T(8,128)} %param.12) | copy-start | bytes 3076
  101.6 8.3 %copy-start.1 = (s32[2048]{0:T(1024)S(1)}, s32[2048]{0:T(1024)}, u32[]{:S(2)}) copy-start(s32[2048]{0:T(1024)} %param.18) | copy-start | bytes 24580
  101.6 51.4 %collective-permute-start = (bf16[4,128,576]{1,2,0:T(8,128)(2,1)S(1)}, bf16[4,128,576]{1,2,0:T(8,128)(2,1)S(1)}, u32[]{:S(2)}, u32[]{:S(2)}) collective-permute-start(bf16[4,128,576]{1,2,0:T(8,128)(2,1)S(1)} %gather_fusion.2), channel_id=1, source_target_pairs={{0,64},{8,72},{16,80},{24,88},{32,96},{40,104},{48,112},{56,120},{... | collective-permute-start | bytes 1769480 | tf_op jit(solution)/shard_map/ppermute | solution.py:68
  105.4 5.4 %copy-start.2 = (bf16[16,576]{1,0:T(8,128)(2,1)S(1)}, bf16[16,576]{1,0:T(8,128)(2,1)}, u32[]{:S(2)}) copy-start(bf16[16,576]{1,0:T(8,128)(2,1)} %param.16) | copy-start | bytes 55300

commit v5 on v4

--- a/solution.py
+++ b/solution.py
@@ -157,18 +157,31 @@
     expert_count = lax.axis_size("dp") * n_ep
     packed, target = pack_rows(hidden, routes, expert_count, CAP)
     received = lax.all_to_all(packed, ("dp", "ep"), 0, 0, tiled=True)
-    finished = expert_rows(received, expert_in[0], expert_out[0])
-    returned = lax.all_to_all(finished, ("dp", "ep"), 0, 0, tiled=True)
-    mixed = unpack_rows(returned, target, route_weights)
     row_count = swapped.shape[0]
+    outgoing = jnp.argsort(1 - swapped, stable=True)[:MOVE]
+    leaving = latent_cache[outgoing] + received[0, 0, 0] * jnp.zeros((), received.dtype)
     top_bit = lax.axis_size("dp").bit_length() - 2
-    outgoing = jnp.argsort(1 - swapped, stable=True)[:MOVE]
+    incoming_cache = swapped_2(leaving, "dp", top_bit)
+    finished = [
+        expert_rows(received[:, step * CAP : (step + 1) * CAP], expert_in[0], expert_out[0])
+        for step in range(STEPS)
+    ]
+    arrived = incoming_cache[0, 0, 0] * jnp.zeros((), incoming_cache.dtype)
+    finished = [f + arrived for f in finished]
+    returned = [lax.all_to_all(f, ("dp", "ep"), 0, 0, tiled=True) for f in finished]
+    step_target = target - jnp.arange(STEPS, dtype=jnp.int32)[:, None, None] * CAP
+    step_target = step_target + (target // (STEPS * CAP)) * (CAP - STEPS * CAP)
+    mixed = jnp.concatenate(
+        [
+            unpack_rows(returned[step], step_target[step : step + 1], route_weights[step : step + 1])
+            for step in range(STEPS)
+        ]
+    )
     arrival = jnp.clip(jnp.cumsum(swapped) - 1, 0, MOVE - 1)
     is_moved = swapped == 1
     device_rows = lax.axis_index(("dp", "ep")) * row_count + jnp.arange(row_count, dtype=jnp.int32)
     total_rows = expert_count * row_count
     anchor = jnp.where(is_moved, (device_rows + total_rows // 2) % total_rows, device_rows)
-    incoming_cache = swapped_2(latent_cache[outgoing], "dp", top_bit)
     merged_cache = jnp.where(is_moved[:, None, None], incoming_cache[arrival], latent_cache)
     context = attend_block(queries, merged_cache, lengths[anchor], fresh_key)
     return (mixed, context)

time: 174 us -> 166 us (0.954)
  waiting for transfers between devices: 88.9 us -> 57.2 us
  local copies, waits for them, and re-layouts: 29.9 us -> 43.7 us
  starting transfers between devices: 21.1 us -> 24.7 us
  matrix products: 24.8 us -> 27.9 us
    ppermute x1, waiting for transfers between devices: 41.6 us -> 0.01 us  [swapped_2(): return lax.ppermute(value, axis, pairs)]
    all_to_all x1 -> x2, waiting for transfers between devices: 0.01 us -> 19.9 us  [per_device(): lax.all_to_all(f, ('dp', 'ep'), 0, 0, tiled=True)]
    all_to_all x1, waiting for transfers between devices: 47.2 us -> 37.3 us  [per_device(): received = lax.all_to_all(packed, ('dp', 'ep'), 0, 0, tiled=True)]
    slice x0 -> x4, local copies, waits for them, and re-layouts: none -> 9.49 us  [the longest x1 7.75 us: per_device(): received[:, step * CAP:(step + 1) * CAP]]
    all_to_all x1 -> x2, starting transfers between devices: 5.46 us -> 12.2 us  [per_device(): lax.all_to_all(f, ('dp', 'ep'), 0, 0, tiled=True)]
    add x0 -> x2, local copies, waits for them, and re-layouts: none -> 6.27 us  [per_device(): finished = [f + arrived for f in finished]]
    convert_element_type x1 -> x0, local copies, waits for them, and re-layouts: 4.67 us -> none  [expert_rows(): return jnp.einsum('skf,fc->skc', activated, expert_out, preferred_element...]
    dot_general x1 -> x2, matrix products: 12.1 us -> 15.2 us  [expert_rows(): jnp.einsum('skc,cf->skf', picked, expert_in, preferred_element_type=jnp.f...]
  transfers between devices with their start and end apart: 3 -> 4, of which waited for: 2 -> 3; matrix products, arithmetic and copies ran while one was open for 13% -> 36% of each run, Pallas kernels for 0% -> 0%
where the time goes in v5:
time: 166 us; the launch traced here: 165 us
  waiting for transfers between devices  57.2 us (34%)
  local copies, waits for them, and re-layouts  43.7 us (26%)
  matrix products  27.9 us (17%)
  starting transfers between devices  24.7 us (15%)
  other arithmetic  9.01 us (5%)
  between operations  2.3 us (1%)
    all_to_all x1, waiting for transfers between devices, per_device(): received = lax.all_to_all(packed, ('dp', 'ep'), 0, 0, tiled=True)  37.3 us
    all_to_all x2, waiting for transfers between devices, per_device(): lax.all_to_all(f, ('dp', 'ep'), 0, 0, tiled=True)  19.9 us
    dot_general x2, matrix products, expert_rows(): jnp.einsum('skc,cf->skf', picked, expert_in, preferred_element_type=jnp.f...  15.2 us
    all_to_all x2, starting transfers between devices, per_device(): lax.all_to_all(f, ('dp', 'ep'), 0, 0, tiled=True)  12.2 us
    all_to_all x1, starting transfers between devices, per_device(): received = lax.all_to_all(packed, ('dp', 'ep'), 0, 0, tiled=True)  11.9 us
    gather x2, local copies, waits for them, and re-layouts, per_device(): incoming_cache[arrival]  7.76 us
    slice x1, local copies, waits for them, and re-layouts, per_device(): received[:, step * CAP:(step + 1) * CAP]  7.75 us
    dot_general x2, matrix products, expert_rows(): jnp.einsum('skf,fc->skc', activated, expert_out, preferred_element_type=j...  7.29 us
  transfers between devices with their start and end apart: 4, of which 3 were waited for; matrix products, arithmetic and copies ran while one was open for 36% of the time, Pallas kernels for 0%

profile of v5, /device:TPU:1, one launch (start us, length us, event | category | flops | bytes accessed | tf_op | source)
XLA Modules:
  0.0 164.9 jit_solution(1969303462970313725)
XLA Ops:
  0.6 0.0 copy-start
  0.7 0.9 copy.52
  1.5 0.1 eq.39
  1.6 0.1 fusion.40
  1.7 0.2 reduce_window_sum.18
  1.9 0.2 select_reduce_fusion
  2.1 0.1 reshape.393
  2.2 0.1 fusion.45
  2.3 0.2 compare_reduce_fusion
  2.5 2.1 %convolution_convert_fusion = bf16[128,4,3584]{2,0,1:T(8,128)(2,1)S(1)} fusion(pred[128,4,32]{0,2,1:T(8,128)(4,1)S(1)} %compare_reduce_fusion, bf16[32,3584,1]{1,0,2:T(8,128)(2,1)} %bitcast.60), kind=kOutput, calls=%fused_computation.13 | convolution fusion | flops 119275520 | bytes 3915776 | tf_op jit(solution)/shard_map/dkt,tc->dkc/dot_general | solution.py:100
  4.6 4.7 %copy.56 = bf16[128,4,3584]{2,1,0:T(4,128)(2,1)} copy(bf16[128,4,3584]{2,0,1:T(8,128)(2,1)S(1)} %convolution_convert_fusion) | data formatting | bytes 7340032 | tf_op jit(solution)/shard_map/convert_element_type | solution.py:102
  9.3 11.9 %all-to-all-start = ((bf16[128,4,3584]{2,1,0:T(4,128)(2,1)}), bf16[128,4,3584]{2,1,0:T(4,128)(2,1)}, u32[]{:S(2)}, u32[]{:S(2)}) async-start(bf16[128,4,3584]{2,1,0:T(4,128)(2,1)} %copy.56), calls=%async_computation | async-start | bytes 7340032 | tf_op jit(solution)/shard_map/all_to_all | solution.py:159
  21.3 0.0 copy-start.5
  21.3 0.0 copy-start.4
  21.3 0.0 copy-start.1
  21.3 0.0 copy-start.3
  21.3 4.3 %copy.66 = bf16[16,128,576]{2,1,0:T(8,128)(2,1)} copy(bf16[16,128,576]{1,2,0:T(8,128)(2,1)} %param.17) | data formatting | bytes 4718592 | tf_op args[7]
  25.6 0.0 copy-done.5
  25.7 1.2 sort.17
  26.9 2.3 %gather_fusion = bf16[4,128,576]{1,2,0:T(8,128)(2,1)S(1)} fusion(bf16[16,128,576]{1,2,0:T(8,128)(2,1)} %param.17, s32[1024]{0:T(1024)S(1)} %pad_clamp_fusion.2), kind=kCustom, calls=%fused_computation | custom fusion | bytes 1179664 | tf_op jit(solution)/shard_map/gather | solution.py:162
  29.3 0.1 reshape.396
  29.4 0.0 copy-done.4
  29.4 0.1 copy.63
  29.5 0.1 reshape.395
  29.5 0.1 copy.60
  29.6 0.1 copy.64
  29.7 0.0 copy-done.1
  29.8 0.7 gather_fusion.3
  30.4 0.1 fusion.47
  30.6 0.1 iota_compare_fusion.1
  30.7 0.0 copy-done.3
  30.7 0.0 copy-done
  30.7 0.5 fusion.41
  31.2 37.3 %all-to-all-done = bf16[128,4,3584]{2,1,0:T(4,128)(2,1)} async-done(((bf16[128,4,3584]{2,1,0:T(4,128)(2,1)}), bf16[128,4,3584]{2,1,0:T(4,128)(2,1)}, u32[]{:S(2)}, u32[]{:S(2)}) %all-to-all-start) | async-done | bytes 3670048 | tf_op jit(solution)/shard_map/all_to_all | solution.py:159
  68.5 1.2 slice.73
  70.4 0.6 collective-permute-start
  71.0 7.8 %fusion.66 = (bf16[128,2,3584]{2,1,0:T(2,128)(2,1)}, bf16[128,2,3584]{2,1,0:T(2,128)(2,1)S(1)}) fusion(bf16[128,4,3584]{2,1,0:T(4,128)(2,1)} %all-to-all-done), kind=kLoop, calls=%fused_computation.113 | loop fusion | bytes 7340032 | tf_op jit(solution)/shard_map/slice | solution.py:166
  78.8 7.4 %fusion = f32[128,2,2048]{2,0,1:T(8,128)S(1)} fusion(bf16[1,3584,2048]{2,1,0:T(8,128)(2,1)} %param.13, bf16[128,2,3584]{2,1,0:T(2,128)(2,1)S(1)} %get-tuple-element.7), kind=kOutput, calls=%fused_computation.5 | convolution fusion | flops 3758096384 | bytes 18612224 | tf_op jit(solution)/shard_map/skc,cf->skf/dot_general | solution.py:72
  86.2 0.0 collective-permute-done
  86.2 0.0 copy-start.2
  86.2 0.6 slice.74
  87.4 0.0 slice-done
  87.4 0.0 slice-done.1
  87.4 2.1 %fusion.14 = bf16[128,2,3584]{2,0,1:T(8,128)(2,1)S(1)} fusion(bf16[1,1024,3584]{2,1,0:T(8,128)(2,1)S(1)} %bitcast.67, bf16[]{:T(256)} %bitcast.8, f32[128,2,2048]{2,0,1:T(8,128)S(1)} %fusion), kind=kOutput, calls=%fused_computation.16 | convolution fusion | flops 1882456064 | bytes 11272194 | tf_op jit(solution)/shard_map/skf,fc->skc/dot_general | solution.py:77
  89.5 0.0 copy-done.2
  89.6 3.1 %copy.62 = bf16[128,2,3584]{2,1,0:T(2,128)(2,1)} copy(bf16[128,2,3584]{2,0,1:T(8,128)(2,1)S(1)} %fusion.14) | data formatting | bytes 3670016 | tf_op jit(solution)/shard_map/add | solution.py:170
  92.7 5.9 %all-to-all-start.2 = ((bf16[128,2,3584]{2,1,0:T(2,128)(2,1)}), bf16[128,2,3584]{2,1,0:T(2,128)(2,1)S(1)}, u32[]{:S(2)}, u32[]{:S(2)}) async-start(bf16[128,2,3584]{2,1,0:T(2,128)(2,1)} %copy.62), calls=%async_computation.2 | async-start | bytes 3670016 | tf_op jit(solution)/shard_map/all_to_all | solution.py:171
  98.6 7.8 %fusion.2 = f32[128,2,2048]{2,0,1:T(8,128)S(1)} fusion(bf16[1,3584,2048]{2,1,0:T(8,128)(2,1)} %param.13, bf16[128,2,3584]{2,1,0:T(2,128)(2,1)} %get-tuple-element.6), kind=kOutput, calls=%fused_computation.7 | convolution fusion | flops 3758096384 | bytes 18612224 | tf_op jit(solution)/shard_map/skc,cf->skf/dot_general | solution.py:72
  106.4 5.2 %fusion.17 = bf16[128,2,3584]{2,0,1:T(8,128)(2,1)S(1)} fusion(bf16[1,1024,3584]{2,1,0:T(8,128)(2,1)} %param.14, bf16[]{:T(256)} %bitcast.8, f32[128,2,2048]{2,0,1:T(8,128)S(1)} %fusion.2), kind=kOutput, calls=%fused_computation.17 | convolution fusion | flops 1882456064 | bytes 11272194 | tf_op jit(solution)/shard_map/skf,fc->skc/dot_general | solution.py:77
  111.6 3.1 %copy.59 = bf16[128,2,3584]{2,1,0:T(2,128)(2,1)} copy(bf16[128,2,3584]{2,0,1:T(8,128)(2,1)S(1)} %fusion.17) | data formatting | bytes 3670016 | tf_op jit(solution)/shard_map/add | solution.py:170
  114.7 3.4 %gather_fusion.4 = bf16[16,128,576]{1,2,0:T(8,128)(2,1)} fusion(bf16[4,128,576]{1,2,0:T(8,128)(2,1)} %copy-done.2, s32[1024]{0:T(1024)S(1)} %pad_clamp_fusion), kind=kCustom, calls=%fused_computation.4 | custom fusion | bytes 4718656 | tf_op jit(solution)/shard_map/gather | solution.py:185
  118.1 4.4 %copy.65 = bf16[16,128,576]{2,1,0:T(8,128)(2,1)} copy(bf16[16,128,576]{1,2,0:T(8,128)(2,1)} %gather_fusion.4) | data formatting | bytes 4718592 | tf_op jit(solution)/shard_map/gather | solution.py:185
  122.5 3.8 %all-to-all-done.2 = bf16[128,2,3584]{2,1,0:T(2,128)(2,1)S(1)} async-done(((bf16[128,2,3584]{2,1,0:T(2,128)(2,1)}), bf16[128,2,3584]{2,1,0:T(2,128)(2,1)S(1)}, u32[]{:S(2)}, u32[]{:S(2)}) %all-to-all-start.2) | async-done | bytes 1835040 | tf_op jit(solution)/shard_map/all_to_all | solution.py:171
  126.3 6.3 %all-to-all-start.1 = ((bf16[128,2,3584]{2,1,0:T(2,128)(2,1)}), bf16[128,2,3584]{2,1,0:T(2,128)(2,1)}, u32[]{:S(2)}, u32[]{:S(2)}) async-start(bf16[128,2,3584]{2,1,0:T(2,128)(2,1)} %copy.59), calls=%async_computation.1 | async-start | bytes 3670016 | tf_op jit(solution)/shard_map/all_to_all | solution.py:171
  132.7 2.9 %broadcast_select_fusion = bf16[16,128,576]{2,1,0:T(8,128)(2,1)S(1)} fusion(bf16[16,128,576]{2,1,0:T(8,128)(2,1)} %copy.65, bf16[16,128,576]{2,1,0:T(8,128)(2,1)} %copy.66, pred[16]{0:T(512)(128)(4,1)S(1)} %broadcast_compare_fusion), kind=kLoop, calls=%fused_computation.18 | loop fusion | flops 1179648 | bytes 7077904 | tf_op jit(solution)/shard_map/jit(_where)/select_n | solution.py:185
  135.5 1.3 fusion.68
  136.8 0.4 fusion.36
  137.2 1.6 divide_convert_fusion
  138.8 3.3 %gather_fusion.2 = bf16[128,3584]{1,0:T(8,128)(2,1)} fusion(bf16[128,2,3584]{2,1,0:T(2,128)(2,1)S(1)} %all-to-all-done.2, s32[128]{0:T(128)S(1)} %fusion.62), kind=kCustom, calls=%fused_computation.2 | custom fusion | bytes 1836032 | tf_op jit(solution)/shard_map/gather | solution.py:109
  142.1 1.9 %fusion.24 = bf16[16,3584]{1,0:T(8,128)(2,1)S(1)} fusion(bf16[128,3584]{1,0:T(8,128)(2,1)} %gather_fusion.2, f32[16,8]{1,0:T(8,128)S(1)} %copy.63), kind=kLoop, calls=%fused_computation.25 | loop fusion | flops 1318912 | bytes 1032704 | tf_op jit(solution)/shard_map/reduce_sum | solution.py:112
  144.0 16.1 %all-to-all-done.1 = bf16[128,2,3584]{2,1,0:T(2,128)(2,1)} async-done(((bf16[128,2,3584]{2,1,0:T(2,128)(2,1)}), bf16[128,2,3584]{2,1,0:T(2,128)(2,1)}, u32[]{:S(2)}, u32[]{:S(2)}) %all-to-all-start.1) | async-done | bytes 1835040 | tf_op jit(solution)/shard_map/all_to_all | solution.py:171
  160.1 3.4 %gather_fusion.1 = bf16[128,3584]{1,0:T(8,128)(2,1)S(1)} fusion(bf16[128,2,3584]{2,1,0:T(2,128)(2,1)} %all-to-all-done.1, s32[128]{0:T(128)S(1)} %fusion.63), kind=kCustom, calls=%fused_computation.1 | custom fusion | bytes 1836032 | tf_op jit(solution)/shard_map/gather | solution.py:109
  163.5 0.7 fusion.25
  164.2 0.7 pad_maximum_fusion
  (22 shorter events, 0.2 us)
Async XLA Ops:
  0.6 30.1 %copy-start = (bf16[16,64,576]{2,1,0:T(8,128)(2,1)S(1)}, bf16[16,64,576]{2,1,0:T(8,128)(2,1)}, u32[]{:S(2)}) copy-start(bf16[16,64,576]{2,1,0:T(8,128)(2,1)} %param.15) | copy-start | bytes 3538948
  9.3 59.2 %all-to-all-start = ((bf16[128,4,3584]{2,1,0:T(4,128)(2,1)}), bf16[128,4,3584]{2,1,0:T(4,128)(2,1)}, u32[]{:S(2)}, u32[]{:S(2)}) async-start(bf16[128,4,3584]{2,1,0:T(4,128)(2,1)} %copy.56), calls=%async_computation | async-start | bytes 7340032 | tf_op jit(solution)/shard_map/all_to_all | solution.py:159
  21.3 4.4 %copy-start.5 = (s32[16]{0:T(128)S(1)}, s32[16]{0:T(128)}, u32[]{:S(2)}) copy-start(s32[16]{0:T(128)} %param.19) | copy-start | bytes 196
  21.3 8.1 %copy-start.4 = (f32[2,16,8]{1,2,0:T(8,128)S(1)}, f32[2,16,8]{1,2,0:T(8,128)}, u32[]{:S(2)}) copy-start(f32[2,16,8]{1,2,0:T(8,128)} %param.12) | copy-start | bytes 3076
  21.3 8.5 %copy-start.1 = (s32[2048]{0:T(1024)S(1)}, s32[2048]{0:T(1024)}, u32[]{:S(2)}) copy-start(s32[2048]{0:T(1024)} %param.18) | copy-start | bytes 24580
  21.3 9.4 %copy-start.3 = (bf16[16,576]{1,0:T(8,128)(2,1)S(1)}, bf16[16,576]{1,0:T(8,128)(2,1)}, u32[]{:S(2)}) copy-start(bf16[16,576]{1,0:T(8,128)(2,1)} %param.16) | copy-start | bytes 55300
  70.4 15.8 %collective-permute-start = (bf16[4,128,576]{1,2,0:T(8,128)(2,1)S(1)}, bf16[4,128,576]{1,2,0:T(8,128)(2,1)S(1)}, u32[]{:S(2)}, u32[]{:S(2)}) collective-permute-start(bf16[4,128,576]{1,2,0:T(8,128)(2,1)S(1)} %broadcast_add_fusion), channel_id=1, source_target_pairs={{0,64},{8,72},{16,80},{24,88},{32,96},{40,104},{48,112},{56,120},{... | collective-permute-start | bytes 1769480 | tf_op jit(solution)/shard_map/ppermute | solution.py:68
  71.0 16.4 %slice-start = ((s8[7340032]{0:T(1024)(128)(4,1)}), s8[4194304]{0:T(1024)(128)(4,1)S(1)}, s32[]{:S(2)}) async-start(s8[7340032]{0:T(1024)(128)(4,1)} %bitcast.66), calls=%async_computation.3 | async-start | bytes 8388608
  78.8 8.7 %slice-start.1 = ((s8[7340032]{0:T(1024)(128)(4,1)}), s8[3145728]{0:T(1024)(128)(4,1)S(1)}, s32[]{:S(2)}) async-start(s8[7340032]{0:T(1024)(128)(4,1)} %bitcast.66), calls=%async_computation.4 | async-start | bytes 6291456
  86.2 3.4 %copy-start.2 = (bf16[4,128,576]{1,2,0:T(8,128)(2,1)}, bf16[4,128,576]{1,2,0:T(8,128)(2,1)S(1)}, u32[]{:S(2)}) copy-start(bf16[4,128,576]{1,2,0:T(8,128)(2,1)S(1)} %collective-permute-done) | copy-start | bytes 1769476
  92.7 33.6 %all-to-all-start.2 = ((bf16[128,2,3584]{2,1,0:T(2,128)(2,1)}), bf16[128,2,3584]{2,1,0:T(2,128)(2,1)S(1)}, u32[]{:S(2)}, u32[]{:S(2)}) async-start(bf16[128,2,3584]{2,1,0:T(2,128)(2,1)} %copy.62), calls=%async_computation.2 | async-start | bytes 3670016 | tf_op jit(solution)/shard_map/all_to_all | solution.py:171
  126.3 33.8 %all-to-all-start.1 = ((bf16[128,2,3584]{2,1,0:T(2,128)(2,1)}), bf16[128,2,3584]{2,1,0:T(2,128)(2,1)}, u32[]{:S(2)}, u32[]{:S(2)}) async-start(bf16[128,2,3584]{2,1,0:T(2,128)(2,1)} %copy.59), calls=%async_computation.1 | async-start | bytes 3670016 | tf_op jit(solution)/shard_map/all_to_all | solution.py:171

commit v6 on v2

--- a/solution.py
+++ b/solution.py
@@ -155,13 +155,15 @@
 ):
     n_ep = lax.axis_size("ep")
     expert_count = lax.axis_size("dp") * n_ep
+    n_dp = lax.axis_size("dp")
+    place = (routes % n_ep) * n_dp + routes // n_ep
     packs = [
-        pack_rows(hidden[step : step + 1], routes[step : step + 1], expert_count, CAP)
+        pack_rows(hidden[step : step + 1], place[step : step + 1], expert_count, CAP)
         for step in range(STEPS)
     ]
-    received = [lax.all_to_all(p[0], ("dp", "ep"), 0, 0, tiled=True) for p in packs]
+    received = [lax.all_to_all(p[0], ("ep", "dp"), 0, 0, tiled=True) for p in packs]
     finished = [expert_rows(r, expert_in[0], expert_out[0]) for r in received]
-    returned = [lax.all_to_all(f, ("dp", "ep"), 0, 0, tiled=True) for f in finished]
+    returned = [lax.all_to_all(f, ("ep", "dp"), 0, 0, tiled=True) for f in finished]
     mixed = jnp.concatenate(
         [unpack_rows(returned[step], packs[step][1], route_weights[step : step + 1]) for step in range(STEPS)]
     )

time: 156 us -> 167 us (1.071)
  waiting for transfers between devices: 47.5 us -> 53.9 us
  starting transfers between devices: 26.9 us -> 31.7 us
    ppermute x1, waiting for transfers between devices: 0.01 us -> 17.1 us  [swapped_2(): return lax.ppermute(value, axis, pairs)]
    all_to_all x4, waiting for transfers between devices: 47.5 us -> 36.8 us  [the longest x2 26.2 us: per_device(): lax.all_to_all(f, ('ep', 'dp'), 0, 0, tiled=True)]
    all_to_all x4, starting transfers between devices: 22.4 us -> 28.3 us  [the longest x2 17.9 us: per_device(): lax.all_to_all(p[0], ('ep', 'dp'), 0, 0, tiled=True)]
    unnamed x17 -> x16, local copies, waits for them, and re-layouts: 5.8 us -> 6.52 us
  transfers between devices with their start and end apart: 5 -> 5, of which waited for: 4 -> 4; matrix products, arithmetic and copies ran while one was open for 45% -> 40% of each run, Pallas kernels for 0% -> 0%
where the time goes in v6:
time: 167 us; the launch traced here: 166 us
  waiting for transfers between devices  53.9 us (32%)
  local copies, waits for them, and re-layouts  37.7 us (23%)
  matrix products  32.8 us (20%)
  starting transfers between devices  31.7 us (19%)
  other arithmetic  9.22 us (6%)
    all_to_all x2, waiting for transfers between devices, per_device(): lax.all_to_all(f, ('ep', 'dp'), 0, 0, tiled=True)  26.2 us
    all_to_all x2, starting transfers between devices, per_device(): lax.all_to_all(p[0], ('ep', 'dp'), 0, 0, tiled=True)  17.9 us
    ppermute x1, waiting for transfers between devices, swapped_2(): return lax.ppermute(value, axis, pairs)  17.1 us
    dot_general x2, matrix products, expert_rows(): jnp.einsum('skc,cf->skf', picked, expert_in, preferred_element_type=jnp.f...  15.6 us
    all_to_all x2, waiting for transfers between devices, per_device(): lax.all_to_all(p[0], ('ep', 'dp'), 0, 0, tiled=True)  10.7 us
    all_to_all x2, starting transfers between devices, per_device(): lax.all_to_all(f, ('ep', 'dp'), 0, 0, tiled=True)  10.5 us
    dot_general x2, matrix products, expert_rows(): jnp.einsum('skf,fc->skc', activated, expert_out, preferred_element_type=j...  10.4 us
    convert_element_type x2, local copies, waits for them, and re-layouts, pack_rows(): packed = jnp.einsum('dkt,tc->dkc', select, flat_tokens, preferred_element...  7.78 us
  transfers between devices with their start and end apart: 5, of which 4 were waited for; matrix products, arithmetic and copies ran while one was open for 40% of the time, Pallas kernels for 0%

profile of v6, /device:TPU:1, one launch (start us, length us, event | category | flops | bytes accessed | tf_op | source)
XLA Modules:
  0.0 166.3 jit_solution(9533885375778879831)
XLA Ops:
  0.6 0.0 copy-start
  0.7 0.9 copy.63
  1.6 0.1 eq.102
  1.7 0.1 fusion.39
  1.7 0.2 reduce_window_sum.24
  1.9 0.2 select_reduce_fusion.1
  2.1 0.1 reshape.591
  2.2 0.1 eq.110
  2.3 0.1 fusion.38
  2.4 0.2 reduce_window_sum.25
  2.6 0.2 select_reduce_fusion
  2.7 0.1 reshape.594
  2.8 0.2 compare_reduce_fusion.1
  3.0 1.6 convolution_convert_fusion.1
  4.6 3.1 %copy.69 = bf16[128,2,3584]{2,1,0:T(2,128)(2,1)} copy(bf16[128,2,3584]{2,0,1:T(8,128)(2,1)S(1)} %convolution_convert_fusion.1) | data formatting | bytes 3670016 | tf_op jit(solution)/shard_map/convert_element_type | solution.py:102
  7.7 11.9 %all-to-all-start = ((bf16[128,2,3584]{2,1,0:T(2,128)(2,1)}), bf16[128,2,3584]{2,1,0:T(2,128)(2,1)}, u32[]{:S(2)}, u32[]{:S(2)}) async-start(bf16[128,2,3584]{2,1,0:T(2,128)(2,1)} %copy.69), calls=%async_computation | async-start | bytes 3670016 | tf_op jit(solution)/shard_map/all_to_all | solution.py:164
  19.6 0.0 copy-start.5
  19.6 0.0 copy-done.6
  19.7 1.2 sort.17
  20.9 2.3 %gather_fusion.3 = bf16[4,128,576]{1,2,0:T(8,128)(2,1)S(1)} fusion(bf16[16,128,576]{1,2,0:T(8,128)(2,1)} %param.17, s32[1024]{0:T(1024)S(1)} %pad_clamp_fusion.1), kind=kCustom, calls=%fused_computation.3 | custom fusion | bytes 1179664 | tf_op jit(solution)/shard_map/gather | solution.py:178
  23.3 3.4 %collective-permute-start = (bf16[4,128,576]{1,2,0:T(8,128)(2,1)S(1)}, bf16[4,128,576]{1,2,0:T(8,128)(2,1)S(1)}, u32[]{:S(2)}, u32[]{:S(2)}) collective-permute-start(bf16[4,128,576]{1,2,0:T(8,128)(2,1)S(1)} %gather_fusion.3), channel_id=1, source_target_pairs={{0,64},{8,72},{16,80},{24,88},{32,96},{40,104},{48,112},{56,120},{... | collective-permute-start | bytes 1769480 | tf_op jit(solution)/shard_map/ppermute | solution.py:68
  26.6 0.0 copy-done.3
  26.6 1.9 %convolution_convert_fusion = bf16[128,2,3584]{2,0,1:T(8,128)(2,1)} fusion(pred[128,2,16]{0,2,1:T(8,128)(4,1)S(1)} %get-tuple-element.5, bf16[2,16,3584]{2,1,0:T(8,128)(2,1)S(1)} %copy-done.3), kind=kOutput, calls=%fused_computation.15 | convolution fusion | flops 30277632 | bytes 1953792 | tf_op jit(solution)/shard_map/dkt,tc->dkc/dot_general | solution.py:100
  28.5 0.0 copy-done.5
  28.5 0.1 reshape.593
  28.6 0.1 reshape.596
  28.7 4.3 %copy.81 = bf16[16,128,576]{2,1,0:T(8,128)(2,1)} copy(bf16[16,128,576]{1,2,0:T(8,128)(2,1)} %param.17) | data formatting | bytes 4718592 | tf_op args[7]
  33.1 0.1 copy.72
  33.1 4.7 %copy.75 = bf16[128,2,3584]{2,1,0:T(2,128)(2,1)} copy(bf16[128,2,3584]{2,0,1:T(8,128)(2,1)} %convolution_convert_fusion) | data formatting | bytes 3670016 | tf_op jit(solution)/shard_map/convert_element_type | solution.py:102
  37.8 0.1 copy.78
  37.9 0.1 copy.79
  38.0 0.0 copy-done.1
  38.0 0.7 gather_fusion.2
  38.7 0.1 fusion.48
  38.8 0.1 iota_compare_fusion.2
  38.9 0.0 copy-done.4
  38.9 0.0 copy-done
  39.0 0.5 fusion.40
  39.5 17.1 %collective-permute-done = bf16[4,128,576]{1,2,0:T(8,128)(2,1)S(1)} collective-permute-done((bf16[4,128,576]{1,2,0:T(8,128)(2,1)S(1)}, bf16[4,128,576]{1,2,0:T(8,128)(2,1)S(1)}, u32[]{:S(2)}, u32[]{:S(2)}) %collective-permute-start) | collective-permute-done | bytes 589856 | tf_op jit(solution)/shard_map/ppermute | solution.py:68
  56.6 2.3 %gather_fusion.4 = bf16[16,128,576]{1,2,0:T(8,128)(2,1)} fusion(bf16[4,128,576]{1,2,0:T(8,128)(2,1)S(1)} %collective-permute-done, s32[1024]{0:T(1024)S(1)} %pad_clamp_fusion), kind=kCustom, calls=%fused_computation.4 | custom fusion | bytes 4718656 | tf_op jit(solution)/shard_map/gather | solution.py:179
  58.9 4.4 %copy.80 = bf16[16,128,576]{2,1,0:T(8,128)(2,1)} copy(bf16[16,128,576]{1,2,0:T(8,128)(2,1)} %gather_fusion.4) | data formatting | bytes 4718592 | tf_op jit(solution)/shard_map/gather | solution.py:179
  63.2 0.0 all-to-all-done
  63.2 6.0 %all-to-all-start.2 = ((bf16[128,2,3584]{2,1,0:T(2,128)(2,1)}), bf16[128,2,3584]{2,1,0:T(2,128)(2,1)S(1)}, u32[]{:S(2)}, u32[]{:S(2)}) async-start(bf16[128,2,3584]{2,1,0:T(2,128)(2,1)} %copy.75), calls=%async_computation.2 | async-start | bytes 3670016 | tf_op jit(solution)/shard_map/all_to_all | solution.py:164
  69.2 7.8 %fusion.2 = f32[128,2,2048]{2,0,1:T(8,128)S(1)} fusion(bf16[1,3584,2048]{2,1,0:T(8,128)(2,1)} %param.13, bf16[128,2,3584]{2,1,0:T(2,128)(2,1)} %all-to-all-done), kind=kOutput, calls=%fused_computation.7 | convolution fusion | flops 3758096384 | bytes 18612224 | tf_op jit(solution)/shard_map/skc,cf->skf/dot_general | solution.py:72
  77.0 5.2 %fusion.8 = bf16[128,2,3584]{2,0,1:T(8,128)(2,1)S(1)} fusion(bf16[1,1024,3584]{2,1,0:T(8,128)(2,1)} %param.14, f32[128,2,2048]{2,0,1:T(8,128)S(1)} %fusion.2), kind=kOutput, calls=%fused_computation.13 | convolution fusion | flops 1881538560 | bytes 11272192 | tf_op jit(solution)/shard_map/skf,fc->skc/dot_general | solution.py:77
  82.2 3.2 %copy.71 = bf16[128,2,3584]{2,1,0:T(2,128)(2,1)} copy(bf16[128,2,3584]{2,0,1:T(8,128)(2,1)S(1)} %fusion.8) | data formatting | bytes 3670016 | tf_op jit(solution)/shard_map/convert_element_type | solution.py:79
  85.4 10.7 %all-to-all-done.2 = bf16[128,2,3584]{2,1,0:T(2,128)(2,1)S(1)} async-done(((bf16[128,2,3584]{2,1,0:T(2,128)(2,1)}), bf16[128,2,3584]{2,1,0:T(2,128)(2,1)S(1)}, u32[]{:S(2)}, u32[]{:S(2)}) %all-to-all-start.2) | async-done | bytes 1835040 | tf_op jit(solution)/shard_map/all_to_all | solution.py:164
  96.0 1.3 copy-done.2
  97.3 4.7 %all-to-all-start.1 = ((bf16[128,2,3584]{2,1,0:T(2,128)(2,1)}), bf16[128,2,3584]{2,1,0:T(2,128)(2,1)S(1)}, u32[]{:S(2)}, u32[]{:S(2)}) async-start(bf16[128,2,3584]{2,1,0:T(2,128)(2,1)} %copy.71), calls=%async_computation.1 | async-start | bytes 3670016 | tf_op jit(solution)/shard_map/all_to_all | solution.py:166
  102.0 7.8 %fusion = f32[128,2,2048]{2,0,1:T(8,128)S(1)} fusion(bf16[1,3584,2048]{2,1,0:T(8,128)(2,1)} %param.13, bf16[128,2,3584]{2,1,0:T(2,128)(2,1)} %copy-done.2), kind=kOutput, calls=%fused_computation.5 | convolution fusion | flops 3758096384 | bytes 18612224 | tf_op jit(solution)/shard_map/skc,cf->skf/dot_general | solution.py:72
  109.8 5.2 %fusion.11 = bf16[128,2,3584]{2,0,1:T(8,128)(2,1)S(1)} fusion(bf16[1,1024,3584]{2,1,0:T(8,128)(2,1)} %param.14, f32[128,2,2048]{2,0,1:T(8,128)S(1)} %fusion), kind=kOutput, calls=%fused_computation.14 | convolution fusion | flops 1881538560 | bytes 11272192 | tf_op jit(solution)/shard_map/skf,fc->skc/dot_general | solution.py:77
  115.0 3.2 %copy.77 = bf16[128,2,3584]{2,1,0:T(2,128)(2,1)} copy(bf16[128,2,3584]{2,0,1:T(8,128)(2,1)S(1)} %fusion.11) | data formatting | bytes 3670016 | tf_op jit(solution)/shard_map/convert_element_type | solution.py:79
  118.2 10.8 %all-to-all-done.1 = bf16[128,2,3584]{2,1,0:T(2,128)(2,1)S(1)} async-done(((bf16[128,2,3584]{2,1,0:T(2,128)(2,1)}), bf16[128,2,3584]{2,1,0:T(2,128)(2,1)S(1)}, u32[]{:S(2)}, u32[]{:S(2)}) %all-to-all-start.1) | async-done | bytes 1835040 | tf_op jit(solution)/shard_map/all_to_all | solution.py:166
  129.0 5.7 %all-to-all-start.3 = ((bf16[128,2,3584]{2,1,0:T(2,128)(2,1)}), bf16[128,2,3584]{2,1,0:T(2,128)(2,1)}, u32[]{:S(2)}, u32[]{:S(2)}) async-start(bf16[128,2,3584]{2,1,0:T(2,128)(2,1)} %copy.77), calls=%async_computation.3 | async-start | bytes 3670016 | tf_op jit(solution)/shard_map/all_to_all | solution.py:166
  134.8 2.9 %broadcast_select_fusion = bf16[16,128,576]{2,1,0:T(8,128)(2,1)S(1)} fusion(bf16[16,128,576]{2,1,0:T(8,128)(2,1)} %copy.80, bf16[16,128,576]{2,1,0:T(8,128)(2,1)} %copy.81, pred[16]{0:T(512)(128)(4,1)S(1)} %broadcast_compare_fusion), kind=kLoop, calls=%fused_computation.17 | loop fusion | flops 1179648 | bytes 7077904 | tf_op jit(solution)/shard_map/jit(_where)/select_n | solution.py:179
  137.6 1.3 fusion.68
  138.9 0.4 fusion.30
  139.4 1.6 divide_convert_fusion
  141.0 3.3 %gather_fusion = bf16[128,3584]{1,0:T(8,128)(2,1)} fusion(bf16[128,2,3584]{2,1,0:T(2,128)(2,1)S(1)} %all-to-all-done.1, s32[128]{0:T(128)S(1)} %fusion.64), kind=kCustom, calls=%fused_computation | custom fusion | bytes 1836032 | tf_op jit(solution)/shard_map/gather | solution.py:109
  144.2 1.9 %fusion.17 = bf16[16,3584]{1,0:T(8,128)(2,1)S(1)} fusion(bf16[128,3584]{1,0:T(8,128)(2,1)} %gather_fusion, f32[16,8]{1,0:T(8,128)S(1)} %copy.72), kind=kLoop, calls=%fused_computation.24 | loop fusion | flops 1318912 | bytes 1032704 | tf_op jit(solution)/shard_map/reduce_sum | solution.py:112
  146.1 15.3 %all-to-all-done.3 = bf16[128,2,3584]{2,1,0:T(2,128)(2,1)} async-done(((bf16[128,2,3584]{2,1,0:T(2,128)(2,1)}), bf16[128,2,3584]{2,1,0:T(2,128)(2,1)}, u32[]{:S(2)}, u32[]{:S(2)}) %all-to-all-start.3) | async-done | bytes 1835040 | tf_op jit(solution)/shard_map/all_to_all | solution.py:166
  161.5 3.4 %gather_fusion.1 = bf16[128,3584]{1,0:T(8,128)(2,1)S(1)} fusion(bf16[128,2,3584]{2,1,0:T(2,128)(2,1)} %all-to-all-done.3, s32[128]{0:T(128)S(1)} %fusion.63), kind=kCustom, calls=%fused_computation.1 | custom fusion | bytes 1836032 | tf_op jit(solution)/shard_map/gather | solution.py:109
  164.9 0.7 fusion.16
  165.6 0.7 pad_maximum_fusion
  (24 shorter events, 0.2 us)
Async XLA Ops:
  0.6 38.3 %copy-start = (bf16[16,64,576]{2,1,0:T(8,128)(2,1)S(1)}, bf16[16,64,576]{2,1,0:T(8,128)(2,1)}, u32[]{:S(2)}) copy-start(bf16[16,64,576]{2,1,0:T(8,128)(2,1)} %param.15) | copy-start | bytes 3538948
  7.7 11.9 %copy-start.6 = (s32[16]{0:T(128)S(1)}, s32[16]{0:T(128)}, u32[]{:S(2)}) copy-start(s32[16]{0:T(128)} %param.19) | copy-start | bytes 196
  7.7 18.9 %copy-start.3 = (bf16[2,16,3584]{2,1,0:T(8,128)(2,1)S(1)}, bf16[2,16,3584]{2,1,0:T(8,128)(2,1)}, u32[]{:S(2)}) copy-start(bf16[2,16,3584]{2,1,0:T(8,128)(2,1)} %param.10) | copy-start | bytes 688132
  7.7 55.5 %all-to-all-start = ((bf16[128,2,3584]{2,1,0:T(2,128)(2,1)}), bf16[128,2,3584]{2,1,0:T(2,128)(2,1)}, u32[]{:S(2)}, u32[]{:S(2)}) async-start(bf16[128,2,3584]{2,1,0:T(2,128)(2,1)} %copy.69), calls=%async_computation | async-start | bytes 3670016 | tf_op jit(solution)/shard_map/all_to_all | solution.py:164
  19.6 8.9 %copy-start.5 = (f32[2,16,8]{1,2,0:T(8,128)S(1)}, f32[2,16,8]{1,2,0:T(8,128)}, u32[]{:S(2)}) copy-start(f32[2,16,8]{1,2,0:T(8,128)} %param.12) | copy-start | bytes 3076
  23.3 33.3 %collective-permute-start = (bf16[4,128,576]{1,2,0:T(8,128)(2,1)S(1)}, bf16[4,128,576]{1,2,0:T(8,128)(2,1)S(1)}, u32[]{:S(2)}, u32[]{:S(2)}) collective-permute-start(bf16[4,128,576]{1,2,0:T(8,128)(2,1)S(1)} %gather_fusion.3), channel_id=1, source_target_pairs={{0,64},{8,72},{16,80},{24,88},{32,96},{40,104},{48,112},{56,120},{... | collective-permute-start | bytes 1769480 | tf_op jit(solution)/shard_map/ppermute | solution.py:68
  33.1 4.9 %copy-start.1 = (s32[2048]{0:T(1024)S(1)}, s32[2048]{0:T(1024)}, u32[]{:S(2)}) copy-start(s32[2048]{0:T(1024)} %param.18) | copy-start | bytes 24580
  33.1 5.8 %copy-start.4 = (bf16[16,576]{1,0:T(8,128)(2,1)S(1)}, bf16[16,576]{1,0:T(8,128)(2,1)}, u32[]{:S(2)}) copy-start(bf16[16,576]{1,0:T(8,128)(2,1)} %param.16) | copy-start | bytes 55300
  63.2 32.8 %all-to-all-start.2 = ((bf16[128,2,3584]{2,1,0:T(2,128)(2,1)}), bf16[128,2,3584]{2,1,0:T(2,128)(2,1)S(1)}, u32[]{:S(2)}, u32[]{:S(2)}) async-start(bf16[128,2,3584]{2,1,0:T(2,128)(2,1)} %copy.75), calls=%async_computation.2 | async-start | bytes 3670016 | tf_op jit(solution)/shard_map/all_to_all | solution.py:164
  96.0 1.3 copy-start.2
  97.3 31.7 %all-to-all-start.1 = ((bf16[128,2,3584]{2,1,0:T(2,128)(2,1)}), bf16[128,2,3584]{2,1,0:T(2,128)(2,1)S(1)}, u32[]{:S(2)}, u32[]{:S(2)}) async-start(bf16[128,2,3584]{2,1,0:T(2,128)(2,1)} %copy.71), calls=%async_computation.1 | async-start | bytes 3670016 | tf_op jit(solution)/shard_map/all_to_all | solution.py:166
  129.0 32.4 %all-to-all-start.3 = ((bf16[128,2,3584]{2,1,0:T(2,128)(2,1)}), bf16[128,2,3584]{2,1,0:T(2,128)(2,1)}, u32[]{:S(2)}, u32[]{:S(2)}) async-start(bf16[128,2,3584]{2,1,0:T(2,128)(2,1)} %copy.77), calls=%async_computation.3 | async-start | bytes 3670016 | tf_op jit(solution)/shard_map/all_to_all | solution.py:166

commit v7 on v2

--- a/solution.py
+++ b/solution.py
@@ -104,12 +104,17 @@
 
 
 def unpack_rows(returned, target, gate_values):
-    width = returned.shape[1]
-    flat_target = target.reshape(-1)
-    picked = returned[flat_target // width, flat_target % width].reshape(
-        target.shape + (returned.shape[2],)
-    )
-    summed = jnp.sum(picked.astype(jnp.float32) * gate_values[..., None], axis=2)
+    expert_count, slot_cap, _ = returned.shape
+    places = jnp.arange(expert_count * slot_cap, dtype=jnp.int32).reshape(expert_count, slot_cap)
+    chosen = target[..., None, None] == places
+    weights = jnp.sum(jnp.where(chosen, gate_values[..., None, None], 0.0), axis=2)
+    summed = jnp.einsum(
+        "stek,ekc->stc",
+        weights,
+        returned.astype(jnp.float32),
+        precision=lax.Precision.HIGHEST,
+        preferred_element_type=jnp.float32,
+    )
     return summed.astype(jnp.bfloat16)
 
 

time: 156 us -> 167 us (1.071)
  waiting for transfers between devices: 47.5 us -> 62.8 us
  local copies, waits for them, and re-layouts: 37.7 us -> 29.5 us
  starting transfers between devices: 26.9 us -> 31.8 us
  other arithmetic: 10 us -> 6.78 us
  matrix products: 31.9 us -> 34.7 us
    ppermute x1, waiting for transfers between devices: 0.01 us -> 19 us  [swapped_2(): return lax.ppermute(value, axis, pairs)]
    all_to_all x2, waiting for transfers between devices: 19.5 us -> 11.5 us  [per_device(): lax.all_to_all(p[0], ('dp', 'ep'), 0, 0, tiled=True)]
    gather x2 -> x0, local copies, waits for them, and re-layouts: 6.66 us -> none  [unpack_rows(): returned[flat_target // width, flat_target % width]]
    all_to_all x2, starting transfers between devices: 12.7 us -> 18.8 us  [per_device(): lax.all_to_all(p[0], ('dp', 'ep'), 0, 0, tiled=True)]
    all_to_all x2, waiting for transfers between devices: 27.9 us -> 32.3 us  [per_device(): lax.all_to_all(f, ('dp', 'ep'), 0, 0, tiled=True)]
    dot_general x0 -> x2, matrix products: none -> 3.15 us  [unpack_rows(): jnp.einsum('stek,ekc->stc', weights, returned.astype(jnp.float32), precis...]
    reduce_sum x2 -> x1, other arithmetic: 2.59 us -> 0.2 us  [unpack_rows(): jnp.sum(jnp.where(chosen, gate_values[..., None, None], 0.0), axis=2)]
  transfers between devices with their start and end apart: 5 -> 5, of which waited for: 4 -> 4; matrix products, arithmetic and copies ran while one was open for 45% -> 36% of each run, Pallas kernels for 0% -> 0%
where the time goes in v7:
time: 167 us; the launch traced here: 166 us
  waiting for transfers between devices  62.8 us (38%)
  matrix products  34.7 us (21%)
  starting transfers between devices  31.8 us (19%)
  local copies, waits for them, and re-layouts  29.5 us (18%)
  other arithmetic  6.78 us (4%)
    all_to_all x2, waiting for transfers between devices, per_device(): lax.all_to_all(f, ('dp', 'ep'), 0, 0, tiled=True)  32.3 us
    ppermute x1, waiting for transfers between devices, swapped_2(): return lax.ppermute(value, axis, pairs)  19 us
    all_to_all x2, starting transfers between devices, per_device(): lax.all_to_all(p[0], ('dp', 'ep'), 0, 0, tiled=True)  18.8 us
    dot_general x2, matrix products, expert_rows(): jnp.einsum('skc,cf->skf', picked, expert_in, preferred_element_type=jnp.f...  15.6 us
    all_to_all x2, waiting for transfers between devices, per_device(): lax.all_to_all(p[0], ('dp', 'ep'), 0, 0, tiled=True)  11.5 us
    dot_general x2, matrix products, expert_rows(): jnp.einsum('skf,fc->skc', activated, expert_out, preferred_element_type=j...  10.4 us
    all_to_all x2, starting transfers between devices, per_device(): lax.all_to_all(f, ('dp', 'ep'), 0, 0, tiled=True)  9.69 us
    gather x2, local copies, waits for them, and re-layouts, per_device(): incoming_cache[arrival]  6.65 us
  transfers between devices with their start and end apart: 5, of which 4 were waited for; matrix products, arithmetic and copies ran while one was open for 36% of the time, Pallas kernels for 0%

profile of v7, /device:TPU:1, one launch (start us, length us, event | category | flops | bytes accessed | tf_op | source)
XLA Modules:
  0.0 166.4 jit_solution(18318401679778767839)
XLA Ops:
  0.6 0.0 copy-start
  0.7 0.8 fusion.55
  1.5 0.1 copy.92
  1.5 0.1 eq.139
  1.6 0.1 fusion.43
  1.7 0.2 reduce_window_sum.24
  1.9 0.2 select_reduce_fusion.3
  2.1 0.1 reshape.331
  2.2 0.1 copy.93
  2.2 0.1 eq.150
  2.3 0.1 fusion.42
  2.4 0.2 reduce_window_sum.25
  2.6 0.2 select_reduce_fusion.2
  2.8 0.1 reshape.333
  2.9 0.2 compare_reduce_fusion.1
  3.1 1.6 convolution_convert_fusion.1
  4.6 3.2 %copy.66 = bf16[128,2,3584]{2,1,0:T(2,128)(2,1)} copy(bf16[128,2,3584]{2,0,1:T(8,128)(2,1)S(1)} %convolution_convert_fusion.1) | data formatting | bytes 3670016 | tf_op jit(solution)/shard_map/convert_element_type | solution.py:102
  7.8 11.9 %all-to-all-start = ((bf16[128,2,3584]{2,1,0:T(2,128)(2,1)}), bf16[128,2,3584]{2,1,0:T(2,128)(2,1)}, u32[]{:S(2)}, u32[]{:S(2)}) async-start(bf16[128,2,3584]{2,1,0:T(2,128)(2,1)} %copy.66), calls=%async_computation | async-start | bytes 3670016 | tf_op jit(solution)/shard_map/all_to_all | solution.py:167
  19.7 0.0 copy-done.6
  19.8 1.2 sort.17
  21.0 2.3 %gather_fusion.1 = bf16[4,128,576]{1,2,0:T(8,128)(2,1)S(1)} fusion(bf16[16,128,576]{1,2,0:T(8,128)(2,1)} %param.17, s32[1024]{0:T(1024)S(1)} %pad_clamp_fusion.1), kind=kCustom, calls=%fused_computation.1 | custom fusion | bytes 1179664 | tf_op jit(solution)/shard_map/gather | solution.py:181
  23.3 0.0 copy-start.5
  23.4 0.0 copy-start.3
  23.4 3.4 %collective-permute-start = (bf16[4,128,576]{1,2,0:T(8,128)(2,1)S(1)}, bf16[4,128,576]{1,2,0:T(8,128)(2,1)S(1)}, u32[]{:S(2)}, u32[]{:S(2)}) collective-permute-start(bf16[4,128,576]{1,2,0:T(8,128)(2,1)S(1)} %gather_fusion.1), channel_id=1, source_target_pairs={{0,64},{8,72},{16,80},{24,88},{32,96},{40,104},{48,112},{56,120},{... | collective-permute-start | bytes 1769480 | tf_op jit(solution)/shard_map/ppermute | solution.py:68
  26.7 4.3 %copy.83 = bf16[16,128,576]{2,1,0:T(8,128)(2,1)} copy(bf16[16,128,576]{1,2,0:T(8,128)(2,1)} %param.17) | data formatting | bytes 4718592 | tf_op args[7]
  31.1 0.0 copy-done.5
  31.1 0.1 copy.64
  31.1 0.1 copy.74
  31.2 0.0 copy-done.3
  31.2 0.7 convolution_convert_fusion
  31.9 0.0 copy-start.1
  31.9 0.0 copy-start.4
  31.9 3.1 %copy.76 = bf16[128,2,3584]{2,1,0:T(2,128)(2,1)} copy(bf16[128,2,3584]{2,0,1:T(8,128)(2,1)S(1)} %convolution_convert_fusion) | data formatting | bytes 3670016 | tf_op jit(solution)/shard_map/convert_element_type | solution.py:102
  35.0 0.1 copy.81
  35.2 0.0 copy-done.1
  35.2 0.7 gather_fusion
  35.8 0.1 fusion.48
  35.9 0.2 select_reduce_fusion.1
  36.1 0.1 iota_compare_fusion.2
  36.3 0.5 fusion.44
  36.8 19.0 %collective-permute-done = bf16[4,128,576]{1,2,0:T(8,128)(2,1)S(1)} collective-permute-done((bf16[4,128,576]{1,2,0:T(8,128)(2,1)S(1)}, bf16[4,128,576]{1,2,0:T(8,128)(2,1)S(1)}, u32[]{:S(2)}, u32[]{:S(2)}) %collective-permute-start) | collective-permute-done | bytes 589856 | tf_op jit(solution)/shard_map/ppermute | solution.py:68
  55.7 2.3 %gather_fusion.2 = bf16[16,128,576]{1,2,0:T(8,128)(2,1)} fusion(bf16[4,128,576]{1,2,0:T(8,128)(2,1)S(1)} %collective-permute-done, s32[1024]{0:T(1024)S(1)} %pad_clamp_fusion), kind=kCustom, calls=%fused_computation.2 | custom fusion | bytes 4718656 | tf_op jit(solution)/shard_map/gather | solution.py:182
  58.0 4.4 %copy.82 = bf16[16,128,576]{2,1,0:T(8,128)(2,1)} copy(bf16[16,128,576]{1,2,0:T(8,128)(2,1)} %gather_fusion.2) | data formatting | bytes 4718592 | tf_op jit(solution)/shard_map/gather | solution.py:182
  62.4 0.0 all-to-all-done
  62.4 6.9 %all-to-all-start.2 = ((bf16[128,2,3584]{2,1,0:T(2,128)(2,1)}), bf16[128,2,3584]{2,1,0:T(2,128)(2,1)S(1)}, u32[]{:S(2)}, u32[]{:S(2)}) async-start(bf16[128,2,3584]{2,1,0:T(2,128)(2,1)} %copy.76), calls=%async_computation.2 | async-start | bytes 3670016 | tf_op jit(solution)/shard_map/all_to_all | solution.py:167
  69.3 7.8 %fusion.2 = f32[128,2,2048]{2,0,1:T(8,128)S(1)} fusion(bf16[1,3584,2048]{2,1,0:T(8,128)(2,1)} %param.13, bf16[128,2,3584]{2,1,0:T(2,128)(2,1)} %all-to-all-done), kind=kOutput, calls=%fused_computation.5 | convolution fusion | flops 3758096384 | bytes 18612224 | tf_op jit(solution)/shard_map/skc,cf->skf/dot_general | solution.py:72
  77.1 5.2 %fusion.8 = bf16[128,2,3584]{2,0,1:T(8,128)(2,1)S(1)} fusion(bf16[1,1024,3584]{2,1,0:T(8,128)(2,1)} %param.14, f32[128,2,2048]{2,0,1:T(8,128)S(1)} %fusion.2), kind=kOutput, calls=%fused_computation.11 | convolution fusion | flops 1881538560 | bytes 11272192 | tf_op jit(solution)/shard_map/skf,fc->skc/dot_general | solution.py:77
  82.3 3.2 %copy.68 = bf16[128,2,3584]{2,1,0:T(2,128)(2,1)} copy(bf16[128,2,3584]{2,0,1:T(8,128)(2,1)S(1)} %fusion.8) | data formatting | bytes 3670016 | tf_op jit(solution)/shard_map/convert_element_type | solution.py:79
  85.5 11.5 %all-to-all-done.2 = bf16[128,2,3584]{2,1,0:T(2,128)(2,1)S(1)} async-done(((bf16[128,2,3584]{2,1,0:T(2,128)(2,1)}), bf16[128,2,3584]{2,1,0:T(2,128)(2,1)S(1)}, u32[]{:S(2)}, u32[]{:S(2)}) %all-to-all-start.2) | async-done | bytes 1835040 | tf_op jit(solution)/shard_map/all_to_all | solution.py:167
  97.0 1.3 copy-done.2
  98.3 4.3 %all-to-all-start.1 = ((bf16[128,2,3584]{2,1,0:T(2,128)(2,1)}), bf16[128,2,3584]{2,1,0:T(2,128)(2,1)S(1)}, u32[]{:S(2)}, u32[]{:S(2)}) async-start(bf16[128,2,3584]{2,1,0:T(2,128)(2,1)} %copy.68), calls=%async_computation.1 | async-start | bytes 3670016 | tf_op jit(solution)/shard_map/all_to_all | solution.py:169
  102.6 7.8 %fusion = f32[128,2,2048]{2,0,1:T(8,128)S(1)} fusion(bf16[1,3584,2048]{2,1,0:T(8,128)(2,1)} %param.13, bf16[128,2,3584]{2,1,0:T(2,128)(2,1)} %copy-done.2), kind=kOutput, calls=%fused_computation.3 | convolution fusion | flops 3758096384 | bytes 18612224 | tf_op jit(solution)/shard_map/skc,cf->skf/dot_general | solution.py:72
  110.4 5.2 %fusion.11 = bf16[128,2,3584]{2,0,1:T(8,128)(2,1)S(1)} fusion(bf16[1,1024,3584]{2,1,0:T(8,128)(2,1)} %param.14, f32[128,2,2048]{2,0,1:T(8,128)S(1)} %fusion), kind=kOutput, calls=%fused_computation.12 | convolution fusion | flops 1881538560 | bytes 11272192 | tf_op jit(solution)/shard_map/skf,fc->skc/dot_general | solution.py:77
  115.6 3.2 %copy.78 = bf16[128,2,3584]{2,1,0:T(2,128)(2,1)} copy(bf16[128,2,3584]{2,0,1:T(8,128)(2,1)S(1)} %fusion.11) | data formatting | bytes 3670016 | tf_op jit(solution)/shard_map/convert_element_type | solution.py:79
  118.8 11.7 %all-to-all-done.1 = bf16[128,2,3584]{2,1,0:T(2,128)(2,1)S(1)} async-done(((bf16[128,2,3584]{2,1,0:T(2,128)(2,1)}), bf16[128,2,3584]{2,1,0:T(2,128)(2,1)S(1)}, u32[]{:S(2)}, u32[]{:S(2)}) %all-to-all-start.1) | async-done | bytes 1835040 | tf_op jit(solution)/shard_map/all_to_all | solution.py:169
  130.5 5.3 %all-to-all-start.3 = ((bf16[128,2,3584]{2,1,0:T(2,128)(2,1)}), bf16[128,2,3584]{2,1,0:T(2,128)(2,1)}, u32[]{:S(2)}, u32[]{:S(2)}) async-start(bf16[128,2,3584]{2,1,0:T(2,128)(2,1)} %copy.78), calls=%async_computation.3 | async-start | bytes 3670016 | tf_op jit(solution)/shard_map/all_to_all | solution.py:169
  135.8 2.9 %broadcast_select_fusion = bf16[16,128,576]{2,1,0:T(8,128)(2,1)S(1)} fusion(bf16[16,128,576]{2,1,0:T(8,128)(2,1)} %copy.82, bf16[16,128,576]{2,1,0:T(8,128)(2,1)} %copy.83, pred[16]{0:T(512)(128)(4,1)S(1)} %broadcast_compare_fusion), kind=kLoop, calls=%fused_computation.21 | loop fusion | flops 1179648 | bytes 7077904 | tf_op jit(solution)/shard_map/jit(_where)/select_n | solution.py:182
  138.7 1.3 fusion.56
  140.0 0.4 fusion.34
  140.4 1.6 divide_convert_fusion
  142.0 0.8 fusion.17
  142.8 20.6 %all-to-all-done.3 = bf16[128,2,3584]{2,1,0:T(2,128)(2,1)} async-done(((bf16[128,2,3584]{2,1,0:T(2,128)(2,1)}), bf16[128,2,3584]{2,1,0:T(2,128)(2,1)}, u32[]{:S(2)}, u32[]{:S(2)}) %all-to-all-start.3) | async-done | bytes 1835040 | tf_op jit(solution)/shard_map/all_to_all | solution.py:169
  163.4 2.3 %fusion.16 = bf16[1,16,3584]{2,1,0:T(8,128)(2,1)S(1)} fusion(bf16[128,2,3584]{2,1,0:T(2,128)(2,1)} %all-to-all-done.3, f32[16,128,2]{1,2,0:T(2,128)S(1)} %get-tuple-element.5), kind=kOutput, calls=%fused_computation.19 | convolution fusion | flops 176218112 | bytes 1966080 | tf_op jit(solution)/shard_map/stek,ekc->stc/dot_general | solution.py:111
  165.7 0.7 pad_maximum_fusion
  (19 shorter events, 0.1 us)
Async XLA Ops:
  0.6 35.6 %copy-start = (bf16[16,64,576]{2,1,0:T(8,128)(2,1)S(1)}, bf16[16,64,576]{2,1,0:T(8,128)(2,1)}, u32[]{:S(2)}) copy-start(bf16[16,64,576]{2,1,0:T(8,128)(2,1)} %param.15) | copy-start | bytes 3538948
  7.8 11.9 %copy-start.6 = (s32[16]{0:T(128)S(1)}, s32[16]{0:T(128)}, u32[]{:S(2)}) copy-start(s32[16]{0:T(128)} %param.19) | copy-start | bytes 196
  7.8 54.6 %all-to-all-start = ((bf16[128,2,3584]{2,1,0:T(2,128)(2,1)}), bf16[128,2,3584]{2,1,0:T(2,128)(2,1)}, u32[]{:S(2)}, u32[]{:S(2)}) async-start(bf16[128,2,3584]{2,1,0:T(2,128)(2,1)} %copy.66), calls=%async_computation | async-start | bytes 3670016 | tf_op jit(solution)/shard_map/all_to_all | solution.py:167
  23.3 7.7 %copy-start.5 = (f32[2,16,8]{1,2,0:T(8,128)S(1)}, f32[2,16,8]{1,2,0:T(8,128)}, u32[]{:S(2)}) copy-start(f32[2,16,8]{1,2,0:T(8,128)} %param.12) | copy-start | bytes 3076
  23.4 7.9 %copy-start.3 = (bf16[2,16,3584]{2,1,0:T(8,128)(2,1)S(1)}, bf16[2,16,3584]{2,1,0:T(8,128)(2,1)}, u32[]{:S(2)}) copy-start(bf16[2,16,3584]{2,1,0:T(8,128)(2,1)} %param.10) | copy-start | bytes 688132
  23.4 32.4 %collective-permute-start = (bf16[4,128,576]{1,2,0:T(8,128)(2,1)S(1)}, bf16[4,128,576]{1,2,0:T(8,128)(2,1)S(1)}, u32[]{:S(2)}, u32[]{:S(2)}) collective-permute-start(bf16[4,128,576]{1,2,0:T(8,128)(2,1)S(1)} %gather_fusion.1), channel_id=1, source_target_pairs={{0,64},{8,72},{16,80},{24,88},{32,96},{40,104},{48,112},{56,120},{... | collective-permute-start | bytes 1769480 | tf_op jit(solution)/shard_map/ppermute | solution.py:68
  31.9 3.3 %copy-start.1 = (s32[2048]{0:T(1024)S(1)}, s32[2048]{0:T(1024)}, u32[]{:S(2)}) copy-start(s32[2048]{0:T(1024)} %param.18) | copy-start | bytes 24580
  31.9 4.3 %copy-start.4 = (bf16[16,576]{1,0:T(8,128)(2,1)S(1)}, bf16[16,576]{1,0:T(8,128)(2,1)}, u32[]{:S(2)}) copy-start(bf16[16,576]{1,0:T(8,128)(2,1)} %param.16) | copy-start | bytes 55300
  62.4 34.6 %all-to-all-start.2 = ((bf16[128,2,3584]{2,1,0:T(2,128)(2,1)}), bf16[128,2,3584]{2,1,0:T(2,128)(2,1)S(1)}, u32[]{:S(2)}, u32[]{:S(2)}) async-start(bf16[128,2,3584]{2,1,0:T(2,128)(2,1)} %copy.76), calls=%async_computation.2 | async-start | bytes 3670016 | tf_op jit(solution)/shard_map/all_to_all | solution.py:167
  97.0 1.3 copy-start.2
  98.3 32.2 %all-to-all-start.1 = ((bf16[128,2,3584]{2,1,0:T(2,128)(2,1)}), bf16[128,2,3584]{2,1,0:T(2,128)(2,1)S(1)}, u32[]{:S(2)}, u32[]{:S(2)}) async-start(bf16[128,2,3584]{2,1,0:T(2,128)(2,1)} %copy.68), calls=%async_computation.1 | async-start | bytes 3670016 | tf_op jit(solution)/shard_map/all_to_all | solution.py:169
  130.5 32.9 %all-to-all-start.3 = ((bf16[128,2,3584]{2,1,0:T(2,128)(2,1)}), bf16[128,2,3584]{2,1,0:T(2,128)(2,1)}, u32[]{:S(2)}, u32[]{:S(2)}) async-start(bf16[128,2,3584]{2,1,0:T(2,128)(2,1)} %copy.78), calls=%async_computation.3 | async-start | bytes 3670016 | tf_op jit(solution)/shard_map/all_to_all | solution.py:169

commit v8 on v7

--- a/solution.py
+++ b/solution.py
@@ -164,21 +164,23 @@
         pack_rows(hidden[step : step + 1], routes[step : step + 1], expert_count, CAP)
         for step in range(STEPS)
     ]
-    received = [lax.all_to_all(p[0], ("dp", "ep"), 0, 0, tiled=True) for p in packs]
+    row_count = swapped.shape[0]
+    top_bit = lax.axis_size("dp").bit_length() - 2
+    outgoing = jnp.argsort(1 - swapped, stable=True)[:MOVE]
+    incoming_cache = swapped_2(latent_cache[outgoing], "dp", top_bit)
+    arrived = incoming_cache[0, 0, 0] * jnp.zeros((), incoming_cache.dtype)
+    sends = [p[0] + arrived for p in packs]
+    received = [lax.all_to_all(p, ("dp", "ep"), 0, 0, tiled=True) for p in sends]
     finished = [expert_rows(r, expert_in[0], expert_out[0]) for r in received]
     returned = [lax.all_to_all(f, ("dp", "ep"), 0, 0, tiled=True) for f in finished]
     mixed = jnp.concatenate(
         [unpack_rows(returned[step], packs[step][1], route_weights[step : step + 1]) for step in range(STEPS)]
     )
-    row_count = swapped.shape[0]
-    top_bit = lax.axis_size("dp").bit_length() - 2
-    outgoing = jnp.argsort(1 - swapped, stable=True)[:MOVE]
     arrival = jnp.clip(jnp.cumsum(swapped) - 1, 0, MOVE - 1)
     is_moved = swapped == 1
     device_rows = lax.axis_index(("dp", "ep")) * row_count + jnp.arange(row_count, dtype=jnp.int32)
     total_rows = expert_count * row_count
     anchor = jnp.where(is_moved, (device_rows + total_rows // 2) % total_rows, device_rows)
-    incoming_cache = swapped_2(latent_cache[outgoing], "dp", top_bit)
     merged_cache = jnp.where(is_moved[:, None, None], incoming_cache[arrival], latent_cache)
     context = attend_block(queries, merged_cache, lengths[anchor], fresh_key)
     return (mixed, context)

time: 167 us -> 168 us (level)
  waiting for transfers between devices: 62.8 us -> 65.3 us
  starting transfers between devices: 31.8 us -> 29.5 us
    all_to_all x2, waiting for transfers between devices: 11.5 us -> 26.7 us  [per_device(): lax.all_to_all(p, ('dp', 'ep'), 0, 0, tiled=True)]
    ppermute x1, waiting for transfers between devices: 19 us -> 6.37 us  [swapped_2(): return lax.ppermute(value, axis, pairs)]
    add x0 -> x2, local copies, waits for them, and re-layouts: none -> 6.36 us  [per_device(): sends = [p[0] + arrived for p in packs]]
    convert_element_type x2 -> x0, local copies, waits for them, and re-layouts: 6.27 us -> none  [pack_rows(): packed = jnp.einsum('dkt,tc->dkc', select, flat_tokens, preferred_element...]
    all_to_all x2, starting transfers between devices: 18.8 us -> 15.3 us  [per_device(): lax.all_to_all(p, ('dp', 'ep'), 0, 0, tiled=True)]
  transfers between devices with their start and end apart: 5 -> 5, of which waited for: 4 -> 5; matrix products, arithmetic and copies ran while one was open for 36% -> 35% of each run, Pallas kernels for 0% -> 0%
where the time goes in v8:
time: 168 us
  waiting for transfers between devices  65.3 us (39%)
  matrix products  33.8 us (20%)
  local copies, waits for them, and re-layouts  29.9 us (18%)
  starting transfers between devices  29.5 us (18%)
  other arithmetic  7.54 us (4%)
    all_to_all x2, waiting for transfers between devices, per_device(): lax.all_to_all(f, ('dp', 'ep'), 0, 0, tiled=True)  32.2 us
    all_to_all x2, waiting for transfers between devices, per_device(): lax.all_to_all(p, ('dp', 'ep'), 0, 0, tiled=True)  26.7 us
    dot_general x2, matrix products, expert_rows(): jnp.einsum('skc,cf->skf', picked, expert_in, preferred_element_type=jnp.f...  15.6 us
    all_to_all x2, starting transfers between devices, per_device(): lax.all_to_all(p, ('dp', 'ep'), 0, 0, tiled=True)  15.3 us
    dot_general x2, matrix products, expert_rows(): jnp.einsum('skf,fc->skc', activated, expert_out, preferred_element_type=j...  10.4 us
    all_to_all x2, starting transfers between devices, per_device(): lax.all_to_all(f, ('dp', 'ep'), 0, 0, tiled=True)  9.69 us
    gather x2, local copies, waits for them, and re-layouts, per_device(): incoming_cache[arrival]  6.65 us
    ppermute x1, waiting for transfers between devices, swapped_2(): return lax.ppermute(value, axis, pairs)  6.37 us
  transfers between devices with their start and end apart: 5, of which 5 were waited for; matrix products, arithmetic and copies ran while one was open for 35% of the time, Pallas kernels for 0%

profile of v8, /device:TPU:1, one launch (start us, length us, event | category | flops | bytes accessed | tf_op | source)
XLA Modules:
  0.0 167.7 jit_solution(1983708863584176809)
XLA Ops:
  0.6 0.0 copy-start
  0.7 0.8 compare_select_fusion.1
  1.4 1.2 sort.17
  2.7 2.3 %gather_fusion = bf16[4,128,576]{1,2,0:T(8,128)(2,1)S(1)} fusion(bf16[16,128,576]{1,2,0:T(8,128)(2,1)} %param.17, s32[1024]{0:T(1024)S(1)} %pad_clamp_fusion.2), kind=kCustom, calls=%fused_computation | custom fusion | bytes 1179664 | tf_op jit(solution)/shard_map/gather | solution.py:170
  5.0 4.5 %collective-permute-start = (bf16[4,128,576]{1,2,0:T(8,128)(2,1)S(1)}, bf16[4,128,576]{1,2,0:T(8,128)(2,1)S(1)}, u32[]{:S(2)}, u32[]{:S(2)}) collective-permute-start(bf16[4,128,576]{1,2,0:T(8,128)(2,1)S(1)} %gather_fusion), channel_id=1, source_target_pairs={{0,64},{8,72},{16,80},{24,88},{32,96},{40,104},{48,112},{56,120},{... | collective-permute-start | bytes 1769480 | tf_op jit(solution)/shard_map/ppermute | solution.py:68
  9.5 0.7 fusion.57
  10.2 0.1 copy.92
  10.3 0.1 eq.139
  10.4 0.1 fusion.45
  10.5 0.1 copy.93
  10.6 0.1 eq.150
  10.7 0.1 fusion.44
  10.8 0.2 reduce_window_sum.24
  10.9 0.2 select_reduce_fusion.3
  11.1 0.0 copy-start.3
  11.1 4.4 %copy.83 = bf16[16,128,576]{2,1,0:T(8,128)(2,1)} copy(bf16[16,128,576]{1,2,0:T(8,128)(2,1)} %param.17) | data formatting | bytes 4718592 | tf_op args[7]
  15.5 0.1 reshape.333
  15.6 0.2 reduce_window_sum.25
  15.7 0.2 select_reduce_fusion.2
  15.9 0.1 reshape.335
  16.0 0.2 compare_reduce_fusion.1
  16.2 6.4 %collective-permute-done = bf16[4,128,576]{1,2,0:T(8,128)(2,1)S(1)} collective-permute-done((bf16[4,128,576]{1,2,0:T(8,128)(2,1)S(1)}, bf16[4,128,576]{1,2,0:T(8,128)(2,1)S(1)}, u32[]{:S(2)}, u32[]{:S(2)}) %collective-permute-start) | collective-permute-done | bytes 589856 | tf_op jit(solution)/shard_map/ppermute | solution.py:68
  22.6 0.5 slice.62
  23.8 0.0 copy-done.3
  23.8 0.7 fusion.14
  24.4 3.2 %copy.66 = bf16[128,2,3584]{2,1,0:T(2,128)(2,1)} copy(bf16[128,2,3584]{2,0,1:T(8,128)(2,1)S(1)} %fusion.14) | data formatting | bytes 3670016 | tf_op jit(solution)/shard_map/add | solution.py:172
  27.6 11.0 %all-to-all-start = ((bf16[128,2,3584]{2,1,0:T(2,128)(2,1)}), bf16[128,2,3584]{2,1,0:T(2,128)(2,1)}, u32[]{:S(2)}, u32[]{:S(2)}) async-start(bf16[128,2,3584]{2,1,0:T(2,128)(2,1)} %copy.66), calls=%async_computation | async-start | bytes 3670016 | tf_op jit(solution)/shard_map/all_to_all | solution.py:173
  38.6 0.0 copy-done.5
  38.6 0.1 copy.64
  38.7 0.1 copy.74
  38.8 0.0 copy-done.6
  38.8 0.1 copy.81
  38.9 0.0 copy-done.1
  38.9 0.7 gather_fusion.1
  39.6 0.1 fusion.50
  39.7 0.2 select_reduce_fusion.1
  39.9 0.1 iota_compare_fusion.2
  40.0 0.0 copy-done.4
  40.0 0.5 fusion.46
  40.5 0.7 fusion.15
  41.2 3.2 %copy.76 = bf16[128,2,3584]{2,1,0:T(2,128)(2,1)} copy(bf16[128,2,3584]{2,0,1:T(8,128)(2,1)S(1)} %fusion.15) | data formatting | bytes 3670016 | tf_op jit(solution)/shard_map/add | solution.py:172
  44.4 2.3 %gather_fusion.2 = bf16[16,128,576]{1,2,0:T(8,128)(2,1)} fusion(bf16[4,128,576]{1,2,0:T(8,128)(2,1)S(1)} %collective-permute-done, s32[1024]{0:T(1024)S(1)} %pad_clamp_fusion), kind=kCustom, calls=%fused_computation.2 | custom fusion | bytes 4718656 | tf_op jit(solution)/shard_map/gather | solution.py:184
  46.7 4.4 %copy.82 = bf16[16,128,576]{2,1,0:T(8,128)(2,1)} copy(bf16[16,128,576]{1,2,0:T(8,128)(2,1)} %gather_fusion.2) | data formatting | bytes 4718592 | tf_op jit(solution)/shard_map/gather | solution.py:184
  51.1 15.0 %all-to-all-done = bf16[128,2,3584]{2,1,0:T(2,128)(2,1)} async-done(((bf16[128,2,3584]{2,1,0:T(2,128)(2,1)}), bf16[128,2,3584]{2,1,0:T(2,128)(2,1)}, u32[]{:S(2)}, u32[]{:S(2)}) %all-to-all-start) | async-done | bytes 1835040 | tf_op jit(solution)/shard_map/all_to_all | solution.py:173
  66.0 4.3 %all-to-all-start.2 = ((bf16[128,2,3584]{2,1,0:T(2,128)(2,1)}), bf16[128,2,3584]{2,1,0:T(2,128)(2,1)S(1)}, u32[]{:S(2)}, u32[]{:S(2)}) async-start(bf16[128,2,3584]{2,1,0:T(2,128)(2,1)} %copy.76), calls=%async_computation.2 | async-start | bytes 3670016 | tf_op jit(solution)/shard_map/all_to_all | solution.py:173
  70.4 7.8 %fusion.2 = f32[128,2,2048]{2,0,1:T(8,128)S(1)} fusion(bf16[1,3584,2048]{2,1,0:T(8,128)(2,1)} %param.13, bf16[128,2,3584]{2,1,0:T(2,128)(2,1)} %all-to-all-done), kind=kOutput, calls=%fused_computation.5 | convolution fusion | flops 3758096384 | bytes 18612224 | tf_op jit(solution)/shard_map/skc,cf->skf/dot_general | solution.py:72
  78.2 5.2 %fusion.8 = bf16[128,2,3584]{2,0,1:T(8,128)(2,1)S(1)} fusion(bf16[1,1024,3584]{2,1,0:T(8,128)(2,1)} %param.14, f32[128,2,2048]{2,0,1:T(8,128)S(1)} %fusion.2), kind=kOutput, calls=%fused_computation.11 | convolution fusion | flops 1881538560 | bytes 11272192 | tf_op jit(solution)/shard_map/skf,fc->skc/dot_general | solution.py:77
  83.4 3.1 %copy.68 = bf16[128,2,3584]{2,1,0:T(2,128)(2,1)} copy(bf16[128,2,3584]{2,0,1:T(8,128)(2,1)S(1)} %fusion.8) | data formatting | bytes 3670016 | tf_op jit(solution)/shard_map/convert_element_type | solution.py:79
  86.5 11.8 %all-to-all-done.2 = bf16[128,2,3584]{2,1,0:T(2,128)(2,1)S(1)} async-done(((bf16[128,2,3584]{2,1,0:T(2,128)(2,1)}), bf16[128,2,3584]{2,1,0:T(2,128)(2,1)S(1)}, u32[]{:S(2)}, u32[]{:S(2)}) %all-to-all-start.2) | async-done | bytes 1835040 | tf_op jit(solution)/shard_map/all_to_all | solution.py:173
  98.2 1.3 copy-done.2
  99.5 4.3 %all-to-all-start.1 = ((bf16[128,2,3584]{2,1,0:T(2,128)(2,1)}), bf16[128,2,3584]{2,1,0:T(2,128)(2,1)S(1)}, u32[]{:S(2)}, u32[]{:S(2)}) async-start(bf16[128,2,3584]{2,1,0:T(2,128)(2,1)} %copy.68), calls=%async_computation.1 | async-start | bytes 3670016 | tf_op jit(solution)/shard_map/all_to_all | solution.py:175
  103.9 7.8 %fusion = f32[128,2,2048]{2,0,1:T(8,128)S(1)} fusion(bf16[1,3584,2048]{2,1,0:T(8,128)(2,1)} %param.13, bf16[128,2,3584]{2,1,0:T(2,128)(2,1)} %copy-done.2), kind=kOutput, calls=%fused_computation.3 | convolution fusion | flops 3758096384 | bytes 18612224 | tf_op jit(solution)/shard_map/skc,cf->skf/dot_general | solution.py:72
  111.7 5.2 %fusion.11 = bf16[128,2,3584]{2,0,1:T(8,128)(2,1)S(1)} fusion(bf16[1,1024,3584]{2,1,0:T(8,128)(2,1)} %param.14, f32[128,2,2048]{2,0,1:T(8,128)S(1)} %fusion), kind=kOutput, calls=%fused_computation.12 | convolution fusion | flops 1881538560 | bytes 11272192 | tf_op jit(solution)/shard_map/skf,fc->skc/dot_general | solution.py:77
  116.9 3.2 %copy.78 = bf16[128,2,3584]{2,1,0:T(2,128)(2,1)} copy(bf16[128,2,3584]{2,0,1:T(8,128)(2,1)S(1)} %fusion.11) | data formatting | bytes 3670016 | tf_op jit(solution)/shard_map/convert_element_type | solution.py:79
  120.0 11.7 %all-to-all-done.1 = bf16[128,2,3584]{2,1,0:T(2,128)(2,1)S(1)} async-done(((bf16[128,2,3584]{2,1,0:T(2,128)(2,1)}), bf16[128,2,3584]{2,1,0:T(2,128)(2,1)S(1)}, u32[]{:S(2)}, u32[]{:S(2)}) %all-to-all-start.1) | async-done | bytes 1835040 | tf_op jit(solution)/shard_map/all_to_all | solution.py:175
  131.7 5.3 %all-to-all-start.3 = ((bf16[128,2,3584]{2,1,0:T(2,128)(2,1)}), bf16[128,2,3584]{2,1,0:T(2,128)(2,1)}, u32[]{:S(2)}, u32[]{:S(2)}) async-start(bf16[128,2,3584]{2,1,0:T(2,128)(2,1)} %copy.78), calls=%async_computation.3 | async-start | bytes 3670016 | tf_op jit(solution)/shard_map/all_to_all | solution.py:175
  137.1 2.9 %broadcast_select_fusion = bf16[16,128,576]{2,1,0:T(8,128)(2,1)S(1)} fusion(bf16[16,128,576]{2,1,0:T(8,128)(2,1)} %copy.82, bf16[16,128,576]{2,1,0:T(8,128)(2,1)} %copy.83, pred[16]{0:T(512)(128)(4,1)S(1)} %broadcast_compare_fusion), kind=kLoop, calls=%fused_computation.23 | loop fusion | flops 1179648 | bytes 7077904 | tf_op jit(solution)/shard_map/jit(_where)/select_n | solution.py:184
  140.0 1.3 fusion.58
  141.2 0.4 fusion.36
  141.7 1.6 divide_convert_fusion
  143.3 0.8 fusion.19
  144.1 20.5 %all-to-all-done.3 = bf16[128,2,3584]{2,1,0:T(2,128)(2,1)} async-done(((bf16[128,2,3584]{2,1,0:T(2,128)(2,1)}), bf16[128,2,3584]{2,1,0:T(2,128)(2,1)}, u32[]{:S(2)}, u32[]{:S(2)}) %all-to-all-start.3) | async-done | bytes 1835040 | tf_op jit(solution)/shard_map/all_to_all | solution.py:175
  164.6 2.3 %fusion.18 = bf16[1,16,3584]{2,1,0:T(8,128)(2,1)S(1)} fusion(bf16[128,2,3584]{2,1,0:T(2,128)(2,1)} %all-to-all-done.3, f32[16,128,2]{1,2,0:T(2,128)S(1)} %get-tuple-element.5), kind=kOutput, calls=%fused_computation.21 | convolution fusion | flops 176218112 | bytes 1966080 | tf_op jit(solution)/shard_map/stek,ekc->stc/dot_general | solution.py:111
  167.0 0.7 pad_maximum_fusion
  (20 shorter events, 0.1 us)
Async XLA Ops:
  0.6 39.4 %copy-start = (bf16[16,64,576]{2,1,0:T(8,128)(2,1)S(1)}, bf16[16,64,576]{2,1,0:T(8,128)(2,1)}, u32[]{:S(2)}) copy-start(bf16[16,64,576]{2,1,0:T(8,128)(2,1)} %param.15) | copy-start | bytes 3538948
  5.0 17.6 %collective-permute-start = (bf16[4,128,576]{1,2,0:T(8,128)(2,1)S(1)}, bf16[4,128,576]{1,2,0:T(8,128)(2,1)S(1)}, u32[]{:S(2)}, u32[]{:S(2)}) collective-permute-start(bf16[4,128,576]{1,2,0:T(8,128)(2,1)S(1)} %gather_fusion), channel_id=1, source_target_pairs={{0,64},{8,72},{16,80},{24,88},{32,96},{40,104},{48,112},{56,120},{... | collective-permute-start | bytes 1769480 | tf_op jit(solution)/shard_map/ppermute | solution.py:68
  11.1 12.7 %copy-start.3 = (bf16[2,16,3584]{2,1,0:T(8,128)(2,1)S(1)}, bf16[2,16,3584]{2,1,0:T(8,128)(2,1)}, u32[]{:S(2)}) copy-start(bf16[2,16,3584]{2,1,0:T(8,128)(2,1)} %param.10) | copy-start | bytes 688132
  27.6 11.0 %copy-start.5 = (f32[2,16,8]{1,2,0:T(8,128)S(1)}, f32[2,16,8]{1,2,0:T(8,128)}, u32[]{:S(2)}) copy-start(f32[2,16,8]{1,2,0:T(8,128)} %param.12) | copy-start | bytes 3076
  27.6 11.2 %copy-start.6 = (s32[16]{0:T(128)S(1)}, s32[16]{0:T(128)}, u32[]{:S(2)}) copy-start(s32[16]{0:T(128)} %param.19) | copy-start | bytes 196
  27.6 11.3 %copy-start.1 = (s32[2048]{0:T(1024)S(1)}, s32[2048]{0:T(1024)}, u32[]{:S(2)}) copy-start(s32[2048]{0:T(1024)} %param.18) | copy-start | bytes 24580
  27.6 12.4 %copy-start.4 = (bf16[16,576]{1,0:T(8,128)(2,1)S(1)}, bf16[16,576]{1,0:T(8,128)(2,1)}, u32[]{:S(2)}) copy-start(bf16[16,576]{1,0:T(8,128)(2,1)} %param.16) | copy-start | bytes 55300
  27.6 38.4 %all-to-all-start = ((bf16[128,2,3584]{2,1,0:T(2,128)(2,1)}), bf16[128,2,3584]{2,1,0:T(2,128)(2,1)}, u32[]{:S(2)}, u32[]{:S(2)}) async-start(bf16[128,2,3584]{2,1,0:T(2,128)(2,1)} %copy.66), calls=%async_computation | async-start | bytes 3670016 | tf_op jit(solution)/shard_map/all_to_all | solution.py:173
  66.0 32.2 %all-to-all-start.2 = ((bf16[128,2,3584]{2,1,0:T(2,128)(2,1)}), bf16[128,2,3584]{2,1,0:T(2,128)(2,1)S(1)}, u32[]{:S(2)}, u32[]{:S(2)}) async-start(bf16[128,2,3584]{2,1,0:T(2,128)(2,1)} %copy.76), calls=%async_computation.2 | async-start | bytes 3670016 | tf_op jit(solution)/shard_map/all_to_all | solution.py:173
  98.2 1.3 copy-start.2
  99.5 32.2 %all-to-all-start.1 = ((bf16[128,2,3584]{2,1,0:T(2,128)(2,1)}), bf16[128,2,3584]{2,1,0:T(2,128)(2,1)S(1)}, u32[]{:S(2)}, u32[]{:S(2)}) async-start(bf16[128,2,3584]{2,1,0:T(2,128)(2,1)} %copy.68), calls=%async_computation.1 | async-start | bytes 3670016 | tf_op jit(solution)/shard_map/all_to_all | solution.py:175
  131.7 32.9 %all-to-all-start.3 = ((bf16[128,2,3584]{2,1,0:T(2,128)(2,1)}), bf16[128,2,3584]{2,1,0:T(2,128)(2,1)}, u32[]{:S(2)}, u32[]{:S(2)}) async-start(bf16[128,2,3584]{2,1,0:T(2,128)(2,1)} %copy.78), calls=%async_computation.3 | async-start | bytes 3670016 | tf_op jit(solution)/shard_map/all_to_all | solution.py:175

commit v9 on v7

--- a/solution.py
+++ b/solution.py
@@ -115,6 +115,16 @@
         precision=lax.Precision.HIGHEST,
         preferred_element_type=jnp.float32,
     )
+    return summed.astype(jnp.bfloat16)
+
+
+def gather_rows(returned, target, gate_values):
+    width = returned.shape[1]
+    flat_target = target.reshape(-1)
+    picked = returned[flat_target // width, flat_target % width].reshape(
+        target.shape + (returned.shape[2],)
+    )
+    summed = jnp.sum(picked.astype(jnp.float32) * gate_values[..., None], axis=2)
     return summed.astype(jnp.bfloat16)
 
 
@@ -168,7 +178,8 @@
     finished = [expert_rows(r, expert_in[0], expert_out[0]) for r in received]
     returned = [lax.all_to_all(f, ("dp", "ep"), 0, 0, tiled=True) for f in finished]
     mixed = jnp.concatenate(
-        [unpack_rows(returned[step], packs[step][1], route_weights[step : step + 1]) for step in range(STEPS)]
+        [gather_rows(returned[0], packs[0][1], route_weights[0:1])]
+        + [unpack_rows(returned[step], packs[step][1], route_weights[step : step + 1]) for step in range(1, STEPS)]
     )
     row_count = swapped.shape[0]
     top_bit = lax.axis_size("dp").bit_length() - 2

time: 167 us -> 154 us (0.922)
  waiting for transfers between devices: 62.8 us -> 50.2 us
  starting transfers between devices: 31.8 us -> 26.9 us
  local copies, waits for them, and re-layouts: 29.5 us -> 32.7 us
  other arithmetic: 6.78 us -> 9.44 us
  matrix products: 34.7 us -> 33 us
    ppermute x1, waiting for transfers between devices: 19 us -> 0.01 us  [swapped_2(): return lax.ppermute(value, axis, pairs)]
    all_to_all x2, waiting for transfers between devices: 11.5 us -> 22.3 us  [per_device(): lax.all_to_all(p[0], ('dp', 'ep'), 0, 0, tiled=True)]
    all_to_all x2, starting transfers between devices: 18.8 us -> 12.7 us  [per_device(): lax.all_to_all(p[0], ('dp', 'ep'), 0, 0, tiled=True)]
    all_to_all x2, waiting for transfers between devices: 32.3 us -> 27.9 us  [per_device(): lax.all_to_all(f, ('dp', 'ep'), 0, 0, tiled=True)]
    gather x0 -> x1, local copies, waits for them, and re-layouts: none -> 3.26 us  [gather_rows(): returned[flat_target // width, flat_target % width]]
    reduce_sum x0 -> x1, other arithmetic: none -> 1.89 us  [gather_rows(): jnp.sum(picked.astype(jnp.float32) * gate_values[..., None], axis=2)]
  transfers between devices with their start and end apart: 5 -> 5, of which waited for: 4 -> 4; matrix products, arithmetic and copies ran while one was open for 36% -> 43% of each run, Pallas kernels for 0% -> 0%
where the time goes in v9:
time: 154 us; the launch traced here: 153 us
  waiting for transfers between devices  50.2 us (33%)
  matrix products  33 us (21%)
  local copies, waits for them, and re-layouts  32.7 us (21%)
  starting transfers between devices  26.9 us (17%)
  other arithmetic  9.44 us (6%)
    all_to_all x2, waiting for transfers between devices, per_device(): lax.all_to_all(f, ('dp', 'ep'), 0, 0, tiled=True)  27.9 us
    all_to_all x2, waiting for transfers between devices, per_device(): lax.all_to_all(p[0], ('dp', 'ep'), 0, 0, tiled=True)  22.3 us
    dot_general x2, matrix products, expert_rows(): jnp.einsum('skc,cf->skf', picked, expert_in, preferred_element_type=jnp.f...  15.6 us
    all_to_all x2, starting transfers between devices, per_device(): lax.all_to_all(p[0], ('dp', 'ep'), 0, 0, tiled=True)  12.7 us
    dot_general x2, matrix products, expert_rows(): jnp.einsum('skf,fc->skc', activated, expert_out, preferred_element_type=j...  10.4 us
    all_to_all x2, starting transfers between devices, per_device(): lax.all_to_all(f, ('dp', 'ep'), 0, 0, tiled=True)  9.69 us
    gather x2, local copies, waits for them, and re-layouts, per_device(): incoming_cache[arrival]  6.67 us
    convert_element_type x2, local copies, waits for them, and re-layouts, expert_rows(): return jnp.einsum('skf,fc->skc', activated, expert_out, preferred_element...  6.37 us
  transfers between devices with their start and end apart: 5, of which 4 were waited for; matrix products, arithmetic and copies ran while one was open for 43% of the time, Pallas kernels for 0%

profile of v9, /device:TPU:1, one launch (start us, length us, event | category | flops | bytes accessed | tf_op | source)
XLA Modules:
  0.0 153.1 jit_solution(2828415584195363714)
XLA Ops:
  0.6 0.0 copy-start
  0.6 0.0 copy-start.3
  0.7 0.8 compare_select_fusion.2
  1.5 1.2 sort.17
  2.7 2.3 %gather_fusion.2 = bf16[4,128,576]{1,2,0:T(8,128)(2,1)S(1)} fusion(bf16[16,128,576]{1,2,0:T(8,128)(2,1)} %param.17, s32[1024]{0:T(1024)S(1)} %pad_clamp_fusion.1), kind=kCustom, calls=%fused_computation.2 | custom fusion | bytes 1179664 | tf_op jit(solution)/shard_map/gather | solution.py:192
  5.1 4.5 %collective-permute-start = (bf16[4,128,576]{1,2,0:T(8,128)(2,1)S(1)}, bf16[4,128,576]{1,2,0:T(8,128)(2,1)S(1)}, u32[]{:S(2)}, u32[]{:S(2)}) collective-permute-start(bf16[4,128,576]{1,2,0:T(8,128)(2,1)S(1)} %gather_fusion.2), channel_id=1, source_target_pairs={{0,64},{8,72},{16,80},{24,88},{32,96},{40,104},{48,112},{56,120},{... | collective-permute-start | bytes 1769480 | tf_op jit(solution)/shard_map/ppermute | solution.py:68
  9.6 0.7 fusion.58
  10.3 0.1 copy.87
  10.4 0.1 eq.128
  10.4 0.1 fusion.40
  10.5 0.2 reduce_window_sum.25
  10.7 0.2 select_reduce_fusion.1
  10.9 0.1 reshape.470
  11.0 0.1 copy.86
  11.1 0.1 eq.120
  11.2 0.1 fusion.41
  11.3 0.2 reduce_window_sum.24
  11.4 0.2 select_reduce_fusion.2
  11.6 0.1 reshape.467
  11.7 0.2 compare_reduce_fusion.1
  11.9 0.7 convolution_convert_fusion.1
  12.6 3.2 %copy.62 = bf16[128,2,3584]{2,1,0:T(2,128)(2,1)} copy(bf16[128,2,3584]{2,0,1:T(8,128)(2,1)S(1)} %convolution_convert_fusion.1) | data formatting | bytes 3670016 | tf_op jit(solution)/shard_map/convert_element_type | solution.py:102
  15.7 8.3 %all-to-all-start = ((bf16[128,2,3584]{2,1,0:T(2,128)(2,1)}), bf16[128,2,3584]{2,1,0:T(2,128)(2,1)}, u32[]{:S(2)}, u32[]{:S(2)}) async-start(bf16[128,2,3584]{2,1,0:T(2,128)(2,1)} %copy.62), calls=%async_computation | async-start | bytes 3670016 | tf_op jit(solution)/shard_map/all_to_all | solution.py:177
  24.1 0.0 copy-start.6
  24.1 4.3 %copy.78 = bf16[16,128,576]{2,1,0:T(8,128)(2,1)} copy(bf16[16,128,576]{1,2,0:T(8,128)(2,1)} %param.17) | data formatting | bytes 4718592 | tf_op args[7]
  28.4 0.1 reshape.469
  28.5 0.1 copy.76
  28.6 0.7 convolution_convert_fusion
  29.3 0.0 copy-start.5
  29.3 0.0 copy-start.1
  29.3 0.0 copy-start.4
  29.4 3.1 %copy.71 = bf16[128,2,3584]{2,1,0:T(2,128)(2,1)} copy(bf16[128,2,3584]{2,0,1:T(8,128)(2,1)S(1)} %convolution_convert_fusion) | data formatting | bytes 3670016 | tf_op jit(solution)/shard_map/convert_element_type | solution.py:102
  32.5 0.1 copy.69
  32.5 0.1 copy.65
  32.6 0.7 gather_fusion.1
  33.3 0.1 fusion.45
  33.4 0.1 select_reduce_fusion
  33.6 0.1 iota_compare_fusion.2
  33.7 0.5 fusion.42
  34.2 0.0 collective-permute-done
  34.2 2.3 %gather_fusion.3 = bf16[16,128,576]{1,2,0:T(8,128)(2,1)} fusion(bf16[4,128,576]{1,2,0:T(8,128)(2,1)S(1)} %collective-permute-done, s32[1024]{0:T(1024)S(1)} %pad_clamp_fusion), kind=kCustom, calls=%fused_computation.3 | custom fusion | bytes 4718656 | tf_op jit(solution)/shard_map/gather | solution.py:193
  36.5 4.4 %copy.77 = bf16[16,128,576]{2,1,0:T(8,128)(2,1)} copy(bf16[16,128,576]{1,2,0:T(8,128)(2,1)} %gather_fusion.3) | data formatting | bytes 4718592 | tf_op jit(solution)/shard_map/gather | solution.py:193
  40.9 10.6 %all-to-all-done = bf16[128,2,3584]{2,1,0:T(2,128)(2,1)} async-done(((bf16[128,2,3584]{2,1,0:T(2,128)(2,1)}), bf16[128,2,3584]{2,1,0:T(2,128)(2,1)}, u32[]{:S(2)}, u32[]{:S(2)}) %all-to-all-start) | async-done | bytes 1835040 | tf_op jit(solution)/shard_map/all_to_all | solution.py:177
  51.5 4.3 %all-to-all-start.2 = ((bf16[128,2,3584]{2,1,0:T(2,128)(2,1)}), bf16[128,2,3584]{2,1,0:T(2,128)(2,1)S(1)}, u32[]{:S(2)}, u32[]{:S(2)}) async-start(bf16[128,2,3584]{2,1,0:T(2,128)(2,1)} %copy.71), calls=%async_computation.2 | async-start | bytes 3670016 | tf_op jit(solution)/shard_map/all_to_all | solution.py:177
  55.8 7.8 %fusion.2 = f32[128,2,2048]{2,0,1:T(8,128)S(1)} fusion(bf16[1,3584,2048]{2,1,0:T(8,128)(2,1)} %param.13, bf16[128,2,3584]{2,1,0:T(2,128)(2,1)} %all-to-all-done), kind=kOutput, calls=%fused_computation.6 | convolution fusion | flops 3758096384 | bytes 18612224 | tf_op jit(solution)/shard_map/skc,cf->skf/dot_general | solution.py:72
  63.6 5.2 %fusion.8 = bf16[128,2,3584]{2,0,1:T(8,128)(2,1)S(1)} fusion(bf16[1,1024,3584]{2,1,0:T(8,128)(2,1)} %param.14, f32[128,2,2048]{2,0,1:T(8,128)S(1)} %fusion.2), kind=kOutput, calls=%fused_computation.12 | convolution fusion | flops 1881538560 | bytes 11272192 | tf_op jit(solution)/shard_map/skf,fc->skc/dot_general | solution.py:77
  68.8 3.2 %copy.64 = bf16[128,2,3584]{2,1,0:T(2,128)(2,1)} copy(bf16[128,2,3584]{2,0,1:T(8,128)(2,1)S(1)} %fusion.8) | data formatting | bytes 3670016 | tf_op jit(solution)/shard_map/convert_element_type | solution.py:79
  72.0 11.7 %all-to-all-done.2 = bf16[128,2,3584]{2,1,0:T(2,128)(2,1)S(1)} async-done(((bf16[128,2,3584]{2,1,0:T(2,128)(2,1)}), bf16[128,2,3584]{2,1,0:T(2,128)(2,1)S(1)}, u32[]{:S(2)}, u32[]{:S(2)}) %all-to-all-start.2) | async-done | bytes 1835040 | tf_op jit(solution)/shard_map/all_to_all | solution.py:177
  83.7 1.3 copy-done.2
  85.0 4.3 %all-to-all-start.1 = ((bf16[128,2,3584]{2,1,0:T(2,128)(2,1)}), bf16[128,2,3584]{2,1,0:T(2,128)(2,1)S(1)}, u32[]{:S(2)}, u32[]{:S(2)}) async-start(bf16[128,2,3584]{2,1,0:T(2,128)(2,1)} %copy.64), calls=%async_computation.1 | async-start | bytes 3670016 | tf_op jit(solution)/shard_map/all_to_all | solution.py:179
  89.3 7.8 %fusion = f32[128,2,2048]{2,0,1:T(8,128)S(1)} fusion(bf16[1,3584,2048]{2,1,0:T(8,128)(2,1)} %param.13, bf16[128,2,3584]{2,1,0:T(2,128)(2,1)} %copy-done.2), kind=kOutput, calls=%fused_computation.4 | convolution fusion | flops 3758096384 | bytes 18612224 | tf_op jit(solution)/shard_map/skc,cf->skf/dot_general | solution.py:72
  97.1 5.2 %fusion.11 = bf16[128,2,3584]{2,0,1:T(8,128)(2,1)S(1)} fusion(bf16[1,1024,3584]{2,1,0:T(8,128)(2,1)} %param.14, f32[128,2,2048]{2,0,1:T(8,128)S(1)} %fusion), kind=kOutput, calls=%fused_computation.13 | convolution fusion | flops 1881538560 | bytes 11272192 | tf_op jit(solution)/shard_map/skf,fc->skc/dot_general | solution.py:77
  102.3 3.2 %copy.73 = bf16[128,2,3584]{2,1,0:T(2,128)(2,1)} copy(bf16[128,2,3584]{2,0,1:T(8,128)(2,1)S(1)} %fusion.11) | data formatting | bytes 3670016 | tf_op jit(solution)/shard_map/convert_element_type | solution.py:79
  105.5 11.7 %all-to-all-done.1 = bf16[128,2,3584]{2,1,0:T(2,128)(2,1)S(1)} async-done(((bf16[128,2,3584]{2,1,0:T(2,128)(2,1)}), bf16[128,2,3584]{2,1,0:T(2,128)(2,1)S(1)}, u32[]{:S(2)}, u32[]{:S(2)}) %all-to-all-start.1) | async-done | bytes 1835040 | tf_op jit(solution)/shard_map/all_to_all | solution.py:179
  117.2 5.3 %all-to-all-start.3 = ((bf16[128,2,3584]{2,1,0:T(2,128)(2,1)}), bf16[128,2,3584]{2,1,0:T(2,128)(2,1)}, u32[]{:S(2)}, u32[]{:S(2)}) async-start(bf16[128,2,3584]{2,1,0:T(2,128)(2,1)} %copy.73), calls=%async_computation.3 | async-start | bytes 3670016 | tf_op jit(solution)/shard_map/all_to_all | solution.py:179
  122.5 2.9 %broadcast_select_fusion = bf16[16,128,576]{2,1,0:T(8,128)(2,1)S(1)} fusion(bf16[16,128,576]{2,1,0:T(8,128)(2,1)} %copy.77, bf16[16,128,576]{2,1,0:T(8,128)(2,1)} %copy.78, pred[16]{0:T(512)(128)(4,1)S(1)} %broadcast_compare_fusion), kind=kLoop, calls=%fused_computation.19 | loop fusion | flops 1179648 | bytes 7077904 | tf_op jit(solution)/shard_map/jit(_where)/select_n | solution.py:193
  125.4 1.3 fusion.59
  126.7 0.4 fusion.32
  127.1 1.6 %divide_convert_fusion = bf16[16,64,512]{2,1,0:T(8,128)(2,1)} fusion(bf16[16,128,576]{2,1,0:T(8,128)(2,1)S(1)} %broadcast_select_fusion, f32[16,64]{1,0:T(8,128)S(1)} %get-tuple-element.7, f32[16,512]{1,0:T(8,128)S(1)} %slice_convert_fusion, f32[16,64]{1,0:T(8,128)S(1)} %convert_element_type.125, f32[16,64,128]{2,1,0:T(8,128)S(1)} %get-tuple-element.15, ...), kind=kOutput, calls=%fused_computation.22 | convolution fusion | flops 136577024 | bytes 3727360 | tf_op jit(solution)/shard_map/nhl,nlc->nhc/dot_general | solution.py:146
  128.7 3.3 %gather_fusion = bf16[128,3584]{1,0:T(8,128)(2,1)} fusion(bf16[128,2,3584]{2,1,0:T(2,128)(2,1)S(1)} %all-to-all-done.1, s32[128]{0:T(128)S(1)} %fusion.55), kind=kCustom, calls=%fused_computation | custom fusion | bytes 1836032 | tf_op jit(solution)/shard_map/gather | solution.py:124
  132.0 1.9 %fusion.18 = bf16[16,3584]{1,0:T(8,128)(2,1)S(1)} fusion(bf16[128,3584]{1,0:T(8,128)(2,1)} %gather_fusion, f32[16,8]{1,0:T(8,128)S(1)} %copy.65), kind=kLoop, calls=%fused_computation.24 | loop fusion | flops 1318912 | bytes 1032704 | tf_op jit(solution)/shard_map/reduce_sum | solution.py:127
  133.9 16.2 %all-to-all-done.3 = bf16[128,2,3584]{2,1,0:T(2,128)(2,1)} async-done(((bf16[128,2,3584]{2,1,0:T(2,128)(2,1)}), bf16[128,2,3584]{2,1,0:T(2,128)(2,1)}, u32[]{:S(2)}, u32[]{:S(2)}) %all-to-all-start.3) | async-done | bytes 1835040 | tf_op jit(solution)/shard_map/all_to_all | solution.py:179
  150.1 2.3 %fusion.15 = bf16[1,16,3584]{2,1,0:T(8,128)(2,1)S(1)} fusion(bf16[128,2,3584]{2,1,0:T(2,128)(2,1)} %all-to-all-done.3, f32[16,128,2]{1,2,0:T(2,128)S(1)} %select_reduce_fusion), kind=kOutput, calls=%fused_computation.18 | convolution fusion | flops 176218112 | bytes 1966080 | tf_op jit(solution)/shard_map/stek,ekc->stc/dot_general | solution.py:111
  152.4 0.7 pad_maximum_fusion
  (23 shorter events, 0.2 us)
Async XLA Ops:
  0.6 33.1 %copy-start = (bf16[16,64,576]{2,1,0:T(8,128)(2,1)S(1)}, bf16[16,64,576]{2,1,0:T(8,128)(2,1)}, u32[]{:S(2)}) copy-start(bf16[16,64,576]{2,1,0:T(8,128)(2,1)} %param.15) | copy-start | bytes 3538948
  0.6 11.2 %copy-start.3 = (bf16[2,16,3584]{2,1,0:T(8,128)(2,1)S(1)}, bf16[2,16,3584]{2,1,0:T(8,128)(2,1)}, u32[]{:S(2)}) copy-start(bf16[2,16,3584]{2,1,0:T(8,128)(2,1)} %param.10) | copy-start | bytes 688132
  5.1 29.1 %collective-permute-start = (bf16[4,128,576]{1,2,0:T(8,128)(2,1)S(1)}, bf16[4,128,576]{1,2,0:T(8,128)(2,1)S(1)}, u32[]{:S(2)}, u32[]{:S(2)}) collective-permute-start(bf16[4,128,576]{1,2,0:T(8,128)(2,1)S(1)} %gather_fusion.2), channel_id=1, source_target_pairs={{0,64},{8,72},{16,80},{24,88},{32,96},{40,104},{48,112},{56,120},{... | collective-permute-start | bytes 1769480 | tf_op jit(solution)/shard_map/ppermute | solution.py:68
  15.7 35.8 %all-to-all-start = ((bf16[128,2,3584]{2,1,0:T(2,128)(2,1)}), bf16[128,2,3584]{2,1,0:T(2,128)(2,1)}, u32[]{:S(2)}, u32[]{:S(2)}) async-start(bf16[128,2,3584]{2,1,0:T(2,128)(2,1)} %copy.62), calls=%async_computation | async-start | bytes 3670016 | tf_op jit(solution)/shard_map/all_to_all | solution.py:177
  24.1 4.4 %copy-start.6 = (s32[16]{0:T(128)S(1)}, s32[16]{0:T(128)}, u32[]{:S(2)}) copy-start(s32[16]{0:T(128)} %param.19) | copy-start | bytes 196
  29.3 3.1 %copy-start.5 = (f32[2,16,8]{1,2,0:T(8,128)S(1)}, f32[2,16,8]{1,2,0:T(8,128)}, u32[]{:S(2)}) copy-start(f32[2,16,8]{1,2,0:T(8,128)} %param.12) | copy-start | bytes 3076
  29.3 3.3 %copy-start.1 = (s32[2048]{0:T(1024)S(1)}, s32[2048]{0:T(1024)}, u32[]{:S(2)}) copy-start(s32[2048]{0:T(1024)} %param.18) | copy-start | bytes 24580
  29.3 4.3 %copy-start.4 = (bf16[16,576]{1,0:T(8,128)(2,1)S(1)}, bf16[16,576]{1,0:T(8,128)(2,1)}, u32[]{:S(2)}) copy-start(bf16[16,576]{1,0:T(8,128)(2,1)} %param.16) | copy-start | bytes 55300
  51.5 32.2 %all-to-all-start.2 = ((bf16[128,2,3584]{2,1,0:T(2,128)(2,1)}), bf16[128,2,3584]{2,1,0:T(2,128)(2,1)S(1)}, u32[]{:S(2)}, u32[]{:S(2)}) async-start(bf16[128,2,3584]{2,1,0:T(2,128)(2,1)} %copy.71), calls=%async_computation.2 | async-start | bytes 3670016 | tf_op jit(solution)/shard_map/all_to_all | solution.py:177
  83.7 1.3 copy-start.2
  85.0 32.2 %all-to-all-start.1 = ((bf16[128,2,3584]{2,1,0:T(2,128)(2,1)}), bf16[128,2,3584]{2,1,0:T(2,128)(2,1)S(1)}, u32[]{:S(2)}, u32[]{:S(2)}) async-start(bf16[128,2,3584]{2,1,0:T(2,128)(2,1)} %copy.64), calls=%async_computation.1 | async-start | bytes 3670016 | tf_op jit(solution)/shard_map/all_to_all | solution.py:179
  117.2 32.9 %all-to-all-start.3 = ((bf16[128,2,3584]{2,1,0:T(2,128)(2,1)}), bf16[128,2,3584]{2,1,0:T(2,128)(2,1)}, u32[]{:S(2)}, u32[]{:S(2)}) async-start(bf16[128,2,3584]{2,1,0:T(2,128)(2,1)} %copy.73), calls=%async_computation.3 | async-start | bytes 3670016 | tf_op jit(solution)/shard_map/all_to_all | solution.py:179

commit v10 on v9

--- a/solution.py
+++ b/solution.py
@@ -183,13 +183,17 @@
     )
     row_count = swapped.shape[0]
     top_bit = lax.axis_size("dp").bit_length() - 2
-    outgoing = jnp.argsort(1 - swapped, stable=True)[:MOVE]
+    rank = jnp.cumsum(swapped) - 1
+    picks = (swapped[None, :] == 1) & (rank[None, :] == jnp.arange(MOVE, dtype=jnp.int32)[:, None])
     arrival = jnp.clip(jnp.cumsum(swapped) - 1, 0, MOVE - 1)
     is_moved = swapped == 1
     device_rows = lax.axis_index(("dp", "ep")) * row_count + jnp.arange(row_count, dtype=jnp.int32)
     total_rows = expert_count * row_count
     anchor = jnp.where(is_moved, (device_rows + total_rows // 2) % total_rows, device_rows)
-    incoming_cache = swapped_2(latent_cache[outgoing], "dp", top_bit)
+    leaving = jnp.einsum(
+        "mn,nlc->mlc", picks.astype(latent_cache.dtype), latent_cache, preferred_element_type=jnp.float32
+    ).astype(latent_cache.dtype)
+    incoming_cache = swapped_2(leaving, "dp", top_bit)
     merged_cache = jnp.where(is_moved[:, None, None], incoming_cache[arrival], latent_cache)
     context = attend_block(queries, merged_cache, lengths[anchor], fresh_key)
     return (mixed, context)

time: 154 us -> 154 us (level)
  matrix products: 33 us -> 36.9 us
    dot_general x0 -> x1, matrix products: none -> 3.91 us  [per_device(): jnp.einsum('mn,nlc->mlc', picks.astype(latent_cache.dtype), latent_cache,...]
    gather x1 -> x0, local copies, waits for them, and re-layouts: 2.33 us -> none  [per_device(): incoming_cache = swapped_2(latent_cache[outgoing], 'dp', top_bit)]
    unnamed x17 -> x19, local copies, waits for them, and re-layouts: 5.8 us -> 5.8 us
where the time goes in v10:
time: 154 us
  waiting for transfers between devices  49.2 us (32%)
  matrix products  36.9 us (24%)
  local copies, waits for them, and re-layouts  31.5 us (20%)
  starting transfers between devices  27.1 us (18%)
  other arithmetic  8.16 us (5%)
    all_to_all x2, waiting for transfers between devices, per_device(): lax.all_to_all(f, ('dp', 'ep'), 0, 0, tiled=True)  27.9 us
    all_to_all x2, waiting for transfers between devices, per_device(): lax.all_to_all(p[0], ('dp', 'ep'), 0, 0, tiled=True)  21.2 us
    dot_general x2, matrix products, expert_rows(): jnp.einsum('skc,cf->skf', picked, expert_in, preferred_element_type=jnp.f...  15.6 us
    all_to_all x2, starting transfers between devices, per_device(): lax.all_to_all(p[0], ('dp', 'ep'), 0, 0, tiled=True)  13 us
    dot_general x2, matrix products, expert_rows(): jnp.einsum('skf,fc->skc', activated, expert_out, preferred_element_type=j...  10.4 us
    all_to_all x2, starting transfers between devices, per_device(): lax.all_to_all(f, ('dp', 'ep'), 0, 0, tiled=True)  9.69 us
    gather x2, local copies, waits for them, and re-layouts, per_device(): incoming_cache[arrival]  6.65 us
    convert_element_type x2, local copies, waits for them, and re-layouts, expert_rows(): return jnp.einsum('skf,fc->skc', activated, expert_out, preferred_element...  6.37 us
  transfers between devices with their start and end apart: 5, of which 4 were waited for; matrix products, arithmetic and copies ran while one was open for 43% of the time, Pallas kernels for 0%

profile of v10, /device:TPU:1, one launch (start us, length us, event | category | flops | bytes accessed | tf_op | source)
XLA Modules:
  0.0 153.7 jit_solution(11774664275622399609)
XLA Ops:
  0.6 0.0 copy-start
  0.6 0.0 copy-start.5
  0.7 0.0 copy-start.3
  0.7 0.8 broadcast_compare_fusion
  1.4 0.7 copy.82
  2.2 0.1 fusion.50
  2.3 3.9 %fusion.26 = bf16[4,128,576]{1,0,2:T(4,128)(2,1)} fusion(bf16[16,128,576]{1,2,0:T(8,128)(2,1)} %param.17, s32[16]{0:T(128)S(1)} %get-tuple-element.3, pred[16]{0:T(512)(128)(4,1)S(1)} %broadcast_compare_fusion), kind=kOutput, calls=%fused_computation.29 | convolution fusion | flops 9732224 | bytes 2949200 | tf_op jit(solution)/shard_map/mn,nlc->mlc/dot_general | solution.py:193
  6.2 4.4 %collective-permute-start = (bf16[4,128,576]{1,0,2:T(4,128)(2,1)}, bf16[4,128,576]{1,0,2:T(4,128)(2,1)}, u32[]{:S(2)}, u32[]{:S(2)}) collective-permute-start(bf16[4,128,576]{1,0,2:T(4,128)(2,1)} %fusion.26), channel_id=1, source_target_pairs={{0,64},{8,72},{16,80},{24,88},{32,96},{40,104},{48,112},{56,120},{... | collective-permute-start | bytes 1769480 | tf_op jit(solution)/shard_map/ppermute | solution.py:68
  10.7 0.0 copy-done.5
  10.7 0.1 copy.95
  10.8 0.1 eq.143
  10.8 0.1 fusion.45
  10.9 0.2 reduce_window_sum.26
  11.1 0.2 select_reduce_fusion.1
  11.3 0.1 reshape.479
  11.4 0.1 copy.94
  11.5 0.1 eq.135
  11.6 0.1 fusion.46
  11.7 0.2 reduce_window_sum.25
  11.8 0.2 select_reduce_fusion.2
  12.0 0.1 reshape.476
  12.1 0.2 compare_reduce_fusion.1
  12.3 0.7 convolution_convert_fusion.1
  13.0 3.2 %copy.68 = bf16[128,2,3584]{2,1,0:T(2,128)(2,1)} copy(bf16[128,2,3584]{2,0,1:T(8,128)(2,1)S(1)} %convolution_convert_fusion.1) | data formatting | bytes 3670016 | tf_op jit(solution)/shard_map/convert_element_type | solution.py:102
  16.1 8.3 %all-to-all-start = ((bf16[128,2,3584]{2,1,0:T(2,128)(2,1)}), bf16[128,2,3584]{2,1,0:T(2,128)(2,1)}, u32[]{:S(2)}, u32[]{:S(2)}) async-start(bf16[128,2,3584]{2,1,0:T(2,128)(2,1)} %copy.68), calls=%async_computation | async-start | bytes 3670016 | tf_op jit(solution)/shard_map/all_to_all | solution.py:177
  24.5 0.7 convolution_convert_fusion
  25.1 4.3 %copy.86 = bf16[16,128,576]{2,1,0:T(8,128)(2,1)} copy(bf16[16,128,576]{1,2,0:T(8,128)(2,1)} %param.17) | data formatting | bytes 4718592 | tf_op args[7]
  29.5 0.1 reshape.478
  29.6 0.0 copy-start.4
  29.6 3.1 %copy.77 = bf16[128,2,3584]{2,1,0:T(2,128)(2,1)} copy(bf16[128,2,3584]{2,0,1:T(8,128)(2,1)S(1)} %convolution_convert_fusion) | data formatting | bytes 3670016 | tf_op jit(solution)/shard_map/convert_element_type | solution.py:102
  32.7 0.1 copy.75
  32.8 0.1 copy.71
  32.9 0.7 gather_fusion.1
  33.5 0.1 select_reduce_fusion
  33.7 0.1 iota_compare_fusion.2
  33.8 0.0 copy-done.4
  33.8 0.0 copy-done
  33.8 0.5 fusion.47
  34.3 0.0 collective-permute-done
  34.3 1.2 copy.84
  35.5 2.3 %gather_fusion.2 = bf16[16,128,576]{1,2,0:T(8,128)(2,1)} fusion(bf16[4,128,576]{1,2,0:T(8,128)(2,1)S(1)} %copy.84, s32[1024]{0:T(1024)S(1)} %pad_clamp_fusion), kind=kCustom, calls=%fused_computation.2 | custom fusion | bytes 4718656 | tf_op jit(solution)/shard_map/gather | solution.py:197
  37.8 4.4 %copy.85 = bf16[16,128,576]{2,1,0:T(8,128)(2,1)} copy(bf16[16,128,576]{1,2,0:T(8,128)(2,1)} %gather_fusion.2) | data formatting | bytes 4718592 | tf_op jit(solution)/shard_map/gather | solution.py:197
  42.2 9.7 %all-to-all-done = bf16[128,2,3584]{2,1,0:T(2,128)(2,1)} async-done(((bf16[128,2,3584]{2,1,0:T(2,128)(2,1)}), bf16[128,2,3584]{2,1,0:T(2,128)(2,1)}, u32[]{:S(2)}, u32[]{:S(2)}) %all-to-all-start) | async-done | bytes 1835040 | tf_op jit(solution)/shard_map/all_to_all | solution.py:177
  51.9 4.7 %all-to-all-start.2 = ((bf16[128,2,3584]{2,1,0:T(2,128)(2,1)}), bf16[128,2,3584]{2,1,0:T(2,128)(2,1)S(1)}, u32[]{:S(2)}, u32[]{:S(2)}) async-start(bf16[128,2,3584]{2,1,0:T(2,128)(2,1)} %copy.77), calls=%async_computation.2 | async-start | bytes 3670016 | tf_op jit(solution)/shard_map/all_to_all | solution.py:177
  56.6 7.8 %fusion.2 = f32[128,2,2048]{2,0,1:T(8,128)S(1)} fusion(bf16[1,3584,2048]{2,1,0:T(8,128)(2,1)} %param.13, bf16[128,2,3584]{2,1,0:T(2,128)(2,1)} %all-to-all-done), kind=kOutput, calls=%fused_computation.5 | convolution fusion | flops 3758096384 | bytes 18612224 | tf_op jit(solution)/shard_map/skc,cf->skf/dot_general | solution.py:72
  64.4 5.2 %fusion.8 = bf16[128,2,3584]{2,0,1:T(8,128)(2,1)S(1)} fusion(bf16[1,1024,3584]{2,1,0:T(8,128)(2,1)} %param.14, f32[128,2,2048]{2,0,1:T(8,128)S(1)} %fusion.2), kind=kOutput, calls=%fused_computation.11 | convolution fusion | flops 1881538560 | bytes 11272192 | tf_op jit(solution)/shard_map/skf,fc->skc/dot_general | solution.py:77
  69.6 3.2 %copy.70 = bf16[128,2,3584]{2,1,0:T(2,128)(2,1)} copy(bf16[128,2,3584]{2,0,1:T(8,128)(2,1)S(1)} %fusion.8) | data formatting | bytes 3670016 | tf_op jit(solution)/shard_map/convert_element_type | solution.py:79
  72.8 11.5 %all-to-all-done.2 = bf16[128,2,3584]{2,1,0:T(2,128)(2,1)S(1)} async-done(((bf16[128,2,3584]{2,1,0:T(2,128)(2,1)}), bf16[128,2,3584]{2,1,0:T(2,128)(2,1)S(1)}, u32[]{:S(2)}, u32[]{:S(2)}) %all-to-all-start.2) | async-done | bytes 1835040 | tf_op jit(solution)/shard_map/all_to_all | solution.py:177
  84.3 1.3 copy-done.2
  85.6 4.3 %all-to-all-start.1 = ((bf16[128,2,3584]{2,1,0:T(2,128)(2,1)}), bf16[128,2,3584]{2,1,0:T(2,128)(2,1)S(1)}, u32[]{:S(2)}, u32[]{:S(2)}) async-start(bf16[128,2,3584]{2,1,0:T(2,128)(2,1)} %copy.70), calls=%async_computation.1 | async-start | bytes 3670016 | tf_op jit(solution)/shard_map/all_to_all | solution.py:179
  89.9 7.8 %fusion = f32[128,2,2048]{2,0,1:T(8,128)S(1)} fusion(bf16[1,3584,2048]{2,1,0:T(8,128)(2,1)} %param.13, bf16[128,2,3584]{2,1,0:T(2,128)(2,1)} %copy-done.2), kind=kOutput, calls=%fused_computation.3 | convolution fusion | flops 3758096384 | bytes 18612224 | tf_op jit(solution)/shard_map/skc,cf->skf/dot_general | solution.py:72
  97.7 5.2 %fusion.11 = bf16[128,2,3584]{2,0,1:T(8,128)(2,1)S(1)} fusion(bf16[1,1024,3584]{2,1,0:T(8,128)(2,1)} %param.14, f32[128,2,2048]{2,0,1:T(8,128)S(1)} %fusion), kind=kOutput, calls=%fused_computation.12 | convolution fusion | flops 1881538560 | bytes 11272192 | tf_op jit(solution)/shard_map/skf,fc->skc/dot_general | solution.py:77
  102.9 3.2 %copy.79 = bf16[128,2,3584]{2,1,0:T(2,128)(2,1)} copy(bf16[128,2,3584]{2,0,1:T(8,128)(2,1)S(1)} %fusion.11) | data formatting | bytes 3670016 | tf_op jit(solution)/shard_map/convert_element_type | solution.py:79
  106.1 11.7 %all-to-all-done.1 = bf16[128,2,3584]{2,1,0:T(2,128)(2,1)S(1)} async-done(((bf16[128,2,3584]{2,1,0:T(2,128)(2,1)}), bf16[128,2,3584]{2,1,0:T(2,128)(2,1)S(1)}, u32[]{:S(2)}, u32[]{:S(2)}) %all-to-all-start.1) | async-done | bytes 1835040 | tf_op jit(solution)/shard_map/all_to_all | solution.py:179
  117.8 5.3 %all-to-all-start.3 = ((bf16[128,2,3584]{2,1,0:T(2,128)(2,1)}), bf16[128,2,3584]{2,1,0:T(2,128)(2,1)}, u32[]{:S(2)}, u32[]{:S(2)}) async-start(bf16[128,2,3584]{2,1,0:T(2,128)(2,1)} %copy.79), calls=%async_computation.3 | async-start | bytes 3670016 | tf_op jit(solution)/shard_map/all_to_all | solution.py:179
  123.1 2.9 %broadcast_select_fusion = bf16[16,128,576]{2,1,0:T(8,128)(2,1)S(1)} fusion(bf16[16,128,576]{2,1,0:T(8,128)(2,1)} %copy.85, bf16[16,128,576]{2,1,0:T(8,128)(2,1)} %copy.86, pred[16]{0:T(512)(128)(4,1)S(1)} %broadcast_compare_fusion), kind=kLoop, calls=%fused_computation.18 | loop fusion | flops 1179648 | bytes 7077904 | tf_op jit(solution)/shard_map/jit(_where)/select_n | solution.py:197
  126.0 1.3 fusion.69
  127.3 0.4 fusion.37
  127.7 1.6 %divide_convert_fusion = bf16[16,64,512]{2,1,0:T(8,128)(2,1)} fusion(bf16[16,128,576]{2,1,0:T(8,128)(2,1)S(1)} %broadcast_select_fusion, f32[16,64]{1,0:T(8,128)S(1)} %get-tuple-element.7, f32[16,512]{1,0:T(8,128)S(1)} %slice_convert_fusion, f32[16,64]{1,0:T(8,128)S(1)} %convert_element_type.130, f32[16,64,128]{2,1,0:T(8,128)S(1)} %get-tuple-element.13, ...), kind=kOutput, calls=%fused_computation.23 | convolution fusion | flops 136577024 | bytes 3727360 | tf_op jit(solution)/shard_map/nhl,nlc->nhc/dot_general | solution.py:146
  129.3 3.3 %gather_fusion = bf16[128,3584]{1,0:T(8,128)(2,1)} fusion(bf16[128,2,3584]{2,1,0:T(2,128)(2,1)S(1)} %all-to-all-done.1, s32[128]{0:T(128)S(1)} %fusion.65), kind=kCustom, calls=%fused_computation | custom fusion | bytes 1836032 | tf_op jit(solution)/shard_map/gather | solution.py:124
  132.5 1.9 %fusion.20 = bf16[16,3584]{1,0:T(8,128)(2,1)S(1)} fusion(bf16[128,3584]{1,0:T(8,128)(2,1)} %gather_fusion, f32[16,8]{1,0:T(8,128)S(1)} %copy.71), kind=kLoop, calls=%fused_computation.25 | loop fusion | flops 1318912 | bytes 1032704 | tf_op jit(solution)/shard_map/reduce_sum | solution.py:127
  134.4 16.2 %all-to-all-done.3 = bf16[128,2,3584]{2,1,0:T(2,128)(2,1)} async-done(((bf16[128,2,3584]{2,1,0:T(2,128)(2,1)}), bf16[128,2,3584]{2,1,0:T(2,128)(2,1)}, u32[]{:S(2)}, u32[]{:S(2)}) %all-to-all-start.3) | async-done | bytes 1835040 | tf_op jit(solution)/shard_map/all_to_all | solution.py:179
  150.7 2.3 %fusion.15 = bf16[1,16,3584]{2,1,0:T(8,128)(2,1)S(1)} fusion(bf16[128,2,3584]{2,1,0:T(2,128)(2,1)} %all-to-all-done.3, f32[16,128,2]{1,2,0:T(2,128)S(1)} %select_reduce_fusion), kind=kOutput, calls=%fused_computation.17 | convolution fusion | flops 176218112 | bytes 1966080 | tf_op jit(solution)/shard_map/stek,ekc->stc/dot_general | solution.py:111
  153.0 0.7 pad_maximum_fusion
  (22 shorter events, 0.2 us)
Async XLA Ops:
  0.6 33.2 %copy-start = (bf16[16,64,576]{2,1,0:T(8,128)(2,1)S(1)}, bf16[16,64,576]{2,1,0:T(8,128)(2,1)}, u32[]{:S(2)}) copy-start(bf16[16,64,576]{2,1,0:T(8,128)(2,1)} %param.15) | copy-start | bytes 3538948
  0.6 10.0 %copy-start.5 = (s32[2,16,8]{1,2,0:T(8,128)S(1)}, s32[2,16,8]{1,2,0:T(8,128)}, u32[]{:S(2)}) copy-start(s32[2,16,8]{1,2,0:T(8,128)} %param.11) | copy-start | bytes 3076
  0.7 11.6 %copy-start.3 = (bf16[2,16,3584]{2,1,0:T(8,128)(2,1)S(1)}, bf16[2,16,3584]{2,1,0:T(8,128)(2,1)}, u32[]{:S(2)}) copy-start(bf16[2,16,3584]{2,1,0:T(8,128)(2,1)} %param.10) | copy-start | bytes 688132
  6.2 28.1 %collective-permute-start = (bf16[4,128,576]{1,0,2:T(4,128)(2,1)}, bf16[4,128,576]{1,0,2:T(4,128)(2,1)}, u32[]{:S(2)}, u32[]{:S(2)}) collective-permute-start(bf16[4,128,576]{1,0,2:T(4,128)(2,1)} %fusion.26), channel_id=1, source_target_pairs={{0,64},{8,72},{16,80},{24,88},{32,96},{40,104},{48,112},{56,120},{... | collective-permute-start | bytes 1769480 | tf_op jit(solution)/shard_map/ppermute | solution.py:68
  16.1 35.8 %all-to-all-start = ((bf16[128,2,3584]{2,1,0:T(2,128)(2,1)}), bf16[128,2,3584]{2,1,0:T(2,128)(2,1)}, u32[]{:S(2)}, u32[]{:S(2)}) async-start(bf16[128,2,3584]{2,1,0:T(2,128)(2,1)} %copy.68), calls=%async_computation | async-start | bytes 3670016 | tf_op jit(solution)/shard_map/all_to_all | solution.py:177
  29.5 3.2 %copy-start.6 = (f32[2,16,8]{1,2,0:T(8,128)S(1)}, f32[2,16,8]{1,2,0:T(8,128)}, u32[]{:S(2)}) copy-start(f32[2,16,8]{1,2,0:T(8,128)} %param.12) | copy-start | bytes 3076
  29.5 3.4 %copy-start.7 = (s32[16]{0:T(128)S(1)}, s32[16]{0:T(128)}, u32[]{:S(2)}) copy-start(s32[16]{0:T(128)} %param.19) | copy-start | bytes 196
  29.5 3.4 %copy-start.1 = (s32[2048]{0:T(1024)S(1)}, s32[2048]{0:T(1024)}, u32[]{:S(2)}) copy-start(s32[2048]{0:T(1024)} %param.18) | copy-start | bytes 24580
  29.6 4.2 %copy-start.4 = (bf16[16,576]{1,0:T(8,128)(2,1)S(1)}, bf16[16,576]{1,0:T(8,128)(2,1)}, u32[]{:S(2)}) copy-start(bf16[16,576]{1,0:T(8,128)(2,1)} %param.16) | copy-start | bytes 55300
  51.9 32.4 %all-to-all-start.2 = ((bf16[128,2,3584]{2,1,0:T(2,128)(2,1)}), bf16[128,2,3584]{2,1,0:T(2,128)(2,1)S(1)}, u32[]{:S(2)}, u32[]{:S(2)}) async-start(bf16[128,2,3584]{2,1,0:T(2,128)(2,1)} %copy.77), calls=%async_computation.2 | async-start | bytes 3670016 | tf_op jit(solution)/shard_map/all_to_all | solution.py:177
  84.3 1.3 copy-start.2
  85.6 32.2 %all-to-all-start.1 = ((bf16[128,2,3584]{2,1,0:T(2,128)(2,1)}), bf16[128,2,3584]{2,1,0:T(2,128)(2,1)S(1)}, u32[]{:S(2)}, u32[]{:S(2)}) async-start(bf16[128,2,3584]{2,1,0:T(2,128)(2,1)} %copy.70), calls=%async_computation.1 | async-start | bytes 3670016 | tf_op jit(solution)/shard_map/all_to_all | solution.py:179
  117.8 32.9 %all-to-all-start.3 = ((bf16[128,2,3584]{2,1,0:T(2,128)(2,1)}), bf16[128,2,3584]{2,1,0:T(2,128)(2,1)}, u32[]{:S(2)}, u32[]{:S(2)}) async-start(bf16[128,2,3584]{2,1,0:T(2,128)(2,1)} %copy.79), calls=%async_computation.3 | async-start | bytes 3670016 | tf_op jit(solution)/shard_map/all_to_all | solution.py:179

commit v11 on v9

--- a/solution.py
+++ b/solution.py
@@ -101,6 +101,27 @@
         "dkt,tc->dkc", select, flat_tokens, preferred_element_type=jnp.float32
     ).astype(jnp.bfloat16)
     return packed, target
+
+
+def pack_rows_tiled(tokens, experts, expert_count, slot_cap, parts):
+    token_count, pick_count = experts.shape
+    onehot = (experts[:, :, None] == jnp.arange(expert_count, dtype=jnp.int32)).astype(jnp.int32)
+    flat = onehot.reshape(token_count * pick_count, expert_count)
+    earlier = jnp.cumsum(flat, axis=0) - flat
+    within = jnp.sum(earlier * flat, axis=1).reshape(token_count, pick_count)
+    target = experts * slot_cap + within
+    rows = jnp.arange(slot_cap * parts, dtype=jnp.int32)
+    slot_of = jnp.arange(expert_count, dtype=jnp.int32)[:, None] * slot_cap + rows[None, :] // parts
+    hit = jnp.any(target[None, None, :, :] == slot_of[:, :, None, None], axis=3)
+    same_part = (rows % parts)[:, None] == (jnp.arange(token_count * parts) % parts)[None, :]
+    select = (jnp.repeat(hit, parts, axis=2) & same_part[None, :, :]).astype(jnp.bfloat16)
+    pieces = tokens.reshape(token_count * parts, tokens.shape[1] // parts)
+    packed = jnp.dot(
+        select.reshape(expert_count * slot_cap * parts, token_count * parts),
+        pieces,
+        preferred_element_type=jnp.float32,
+    ).astype(jnp.bfloat16)
+    return packed.reshape(expert_count, slot_cap * parts, pieces.shape[1]), target[None]
 
 
 def unpack_rows(returned, target, gate_values):
@@ -174,7 +195,11 @@
         pack_rows(hidden[step : step + 1], routes[step : step + 1], expert_count, CAP)
         for step in range(STEPS)
     ]
+    parts = 4
+    tiled_pack = pack_rows_tiled(hidden[0], routes[0], expert_count, CAP, parts)
+    packs[0] = tiled_pack
     received = [lax.all_to_all(p[0], ("dp", "ep"), 0, 0, tiled=True) for p in packs]
+    received[0] = received[0].reshape(expert_count, CAP, hidden.shape[2])
     finished = [expert_rows(r, expert_in[0], expert_out[0]) for r in received]
     returned = [lax.all_to_all(f, ("dp", "ep"), 0, 0, tiled=True) for f in finished]
     mixed = jnp.concatenate(

time: 154 us -> 158 us (1.026)
  waiting for transfers between devices: 50.2 us -> 46.9 us
  local copies, waits for them, and re-layouts: 32.7 us -> 35.8 us
  other arithmetic: 9.44 us -> 11.8 us
    all_to_all x2, waiting for transfers between devices: 22.3 us -> 19 us  [per_device(): lax.all_to_all(p[0], ('dp', 'ep'), 0, 0, tiled=True)]
    convert_element_type x2 -> x1, local copies, waits for them, and re-layouts: 6.27 us -> 3.11 us  [pack_rows(): packed = jnp.einsum('dkt,tc->dkc', select, flat_tokens, preferred_element...]
    all_to_all x0 -> x1, local copies, waits for them, and re-layouts: none -> 3.14 us  [per_device(): lax.all_to_all(p[0], ('dp', 'ep'), 0, 0, tiled=True)]
    and x0 -> x1, local copies, waits for them, and re-layouts: none -> 2.64 us  [pack_rows_tiled(): jnp.repeat(hit, parts, axis=2) & same_part[None, :, :]]
    dot_general x0 -> x1, matrix products: none -> 1.97 us  [pack_rows_tiled(): jnp.dot(select.reshape(expert_count * slot_cap * parts, token_count * par...]
    unnamed x17 -> x13, local copies, waits for them, and re-layouts: 5.8 us -> 4.42 us
  transfers between devices with their start and end apart: 5 -> 5, of which waited for: 4 -> 4; matrix products, arithmetic and copies ran while one was open for 43% -> 47% of each run, Pallas kernels for 0% -> 0%
where the time goes in v11:
time: 158 us; the launch traced here: 157 us
  waiting for transfers between devices  46.9 us (30%)
  local copies, waits for them, and re-layouts  35.8 us (23%)
  matrix products  33.8 us (21%)
  starting transfers between devices  27.8 us (18%)
  other arithmetic  11.8 us (7%)
    all_to_all x2, waiting for transfers between devices, per_device(): lax.all_to_all(f, ('dp', 'ep'), 0, 0, tiled=True)  27.9 us
    all_to_all x2, waiting for transfers between devices, per_device(): lax.all_to_all(p[0], ('dp', 'ep'), 0, 0, tiled=True)  19 us
    dot_general x2, matrix products, expert_rows(): jnp.einsum('skc,cf->skf', picked, expert_in, preferred_element_type=jnp.f...  15.1 us
    all_to_all x2, starting transfers between devices, per_device(): lax.all_to_all(p[0], ('dp', 'ep'), 0, 0, tiled=True)  13.7 us
    dot_general x2, matrix products, expert_rows(): jnp.einsum('skf,fc->skc', activated, expert_out, preferred_element_type=j...  10.4 us
    all_to_all x2, starting transfers between devices, per_device(): lax.all_to_all(f, ('dp', 'ep'), 0, 0, tiled=True)  9.69 us
    gather x2, local copies, waits for them, and re-layouts, per_device(): incoming_cache[arrival]  6.67 us
    convert_element_type x2, local copies, waits for them, and re-layouts, expert_rows(): return jnp.einsum('skf,fc->skc', activated, expert_out, preferred_element...  6.37 us
  transfers between devices with their start and end apart: 5, of which 4 were waited for; matrix products, arithmetic and copies ran while one was open for 47% of the time, Pallas kernels for 0%

profile of v11, /device:TPU:1, one launch (start us, length us, event | category | flops | bytes accessed | tf_op | source)
XLA Modules:
  0.0 157.0 jit_solution(11692210182023778512)
XLA Ops:
  0.7 0.8 compare_select_fusion.2
  1.4 1.2 sort.17
  2.7 3.1 %gather_fusion.2 = bf16[4,128,576]{1,2,0:T(8,128)(2,1)} fusion(bf16[16,128,576]{1,2,0:T(8,128)(2,1)} %param.17, s32[1024]{0:T(1024)S(1)} %pad_clamp_fusion.1), kind=kCustom, calls=%fused_computation.2 | custom fusion | bytes 1179664 | tf_op jit(solution)/shard_map/gather | solution.py:217
  5.8 4.4 %collective-permute-start = (bf16[4,128,576]{1,2,0:T(8,128)(2,1)}, bf16[4,128,576]{1,2,0:T(8,128)(2,1)S(1)}, u32[]{:S(2)}, u32[]{:S(2)}) collective-permute-start(bf16[4,128,576]{1,2,0:T(8,128)(2,1)} %gather_fusion.2), channel_id=1, source_target_pairs={{0,64},{8,72},{16,80},{24,88},{32,96},{40,104},{48,112},{56,120},{... | collective-permute-start | bytes 1769480 | tf_op jit(solution)/shard_map/ppermute | solution.py:68
  10.2 0.7 slice.44
  10.9 0.1 copy.73
  11.0 0.1 eq.134
  11.1 0.1 fusion.37
  11.2 0.2 reduce_window_sum.30
  11.4 0.2 select_reduce_fusion.1
  11.5 0.1 reshape.504
  11.6 0.1 copy.74
  11.7 0.7 broadcast_multiply_fusion
  12.5 0.1 eq.124
  12.6 0.1 fusion.38
  12.7 0.2 reduce_window_sum.29
  12.9 0.2 select_reduce_fusion.2
  13.0 0.1 reshape.501
  13.1 0.1 copy.65
  13.2 0.7 bitcast_add_fusion
  13.9 0.1 copy.66
  14.1 0.2 compare_reduce_fusion
  14.3 0.5 copy.67
  14.7 0.1 broadcast_compare_fusion
  14.8 0.6 broadcast_and_fusion
  15.5 2.6 %and.106 = pred[1024,64]{0,1:T(32,128)(4,1)S(1)} reshape(pred[128,8,16,4]{1,0,3,2:T(32,128)(4,1)S(1)} %broadcast_and_fusion) | data formatting | bytes 131072 | tf_op jit(solution)/shard_map/and | solution.py:117
  18.1 0.1 reshape_squeeze.3
  18.2 2.0 %convert_bitcast_fusion = bf16[128,8,896]{2,1,0:T(8,128)(2,1)} fusion(pred[1024,64]{0,1:T(32,128)(4,1)S(1)} %and.106, bf16[64,896]{1,0:T(8,128)(2,1)S(1)} %reshape_squeeze.3), kind=kOutput, calls=%fused_computation.27 | convolution fusion | flops 118358016 | bytes 2015232 | tf_op jit(solution)/shard_map/dot_general | solution.py:119
  20.2 8.3 %all-to-all-start = ((bf16[128,8,896]{2,1,0:T(8,128)(2,1)}), bf16[128,8,896]{2,1,0:T(8,128)(2,1)}, u32[]{:S(2)}, u32[]{:S(2)}) async-start(bf16[128,8,896]{2,1,0:T(8,128)(2,1)} %convert_bitcast_fusion), calls=%async_computation | async-start | bytes 3670016 | tf_op jit(solution)/shard_map/all_to_all | solution.py:201
  28.6 4.4 %copy.85 = bf16[16,128,576]{2,1,0:T(8,128)(2,1)} copy(bf16[16,128,576]{1,2,0:T(8,128)(2,1)} %param.17) | data formatting | bytes 4718592 | tf_op args[7]
  32.9 0.1 copy.83
  33.1 0.1 mul.124
  33.5 0.1 compare_reduce_fusion.1
  33.6 0.7 convolution_convert_fusion
  34.3 3.1 %copy.78 = bf16[128,2,3584]{2,1,0:T(2,128)(2,1)} copy(bf16[128,2,3584]{2,0,1:T(8,128)(2,1)S(1)} %convolution_convert_fusion) | data formatting | bytes 3670016 | tf_op jit(solution)/shard_map/convert_element_type | solution.py:102
  37.4 0.7 gather_fusion.1
  38.1 0.1 fusion.42
  38.2 0.1 select_reduce_fusion
  38.4 0.1 iota_compare_fusion.2
  38.5 0.5 fusion.39
  39.0 2.3 %gather_fusion.3 = bf16[16,128,576]{1,2,0:T(8,128)(2,1)} fusion(bf16[4,128,576]{1,2,0:T(8,128)(2,1)S(1)} %collective-permute-done, s32[1024]{0:T(1024)S(1)} %pad_clamp_fusion), kind=kCustom, calls=%fused_computation.3 | custom fusion | bytes 4718656 | tf_op jit(solution)/shard_map/gather | solution.py:218
  41.3 4.4 %copy.84 = bf16[16,128,576]{2,1,0:T(8,128)(2,1)} copy(bf16[16,128,576]{1,2,0:T(8,128)(2,1)} %gather_fusion.3) | data formatting | bytes 4718592 | tf_op jit(solution)/shard_map/gather | solution.py:218
  45.7 10.3 %all-to-all-done = bf16[128,8,896]{2,1,0:T(8,128)(2,1)} async-done(((bf16[128,8,896]{2,1,0:T(8,128)(2,1)}), bf16[128,8,896]{2,1,0:T(8,128)(2,1)}, u32[]{:S(2)}, u32[]{:S(2)}) %all-to-all-start) | async-done | bytes 1835040 | tf_op jit(solution)/shard_map/all_to_all | solution.py:201
  55.9 5.4 %all-to-all-start.2 = ((bf16[128,2,3584]{2,1,0:T(2,128)(2,1)}), bf16[128,2,3584]{2,1,0:T(2,128)(2,1)}, u32[]{:S(2)}, u32[]{:S(2)}) async-start(bf16[128,2,3584]{2,1,0:T(2,128)(2,1)} %copy.78), calls=%async_computation.2 | async-start | bytes 3670016 | tf_op jit(solution)/shard_map/all_to_all | solution.py:201
  61.3 3.1 %copy.68 = bf16[128,8,896]{0,2,1:T(8,128)(2,1)S(1)} copy(bf16[128,8,896]{2,1,0:T(8,128)(2,1)} %all-to-all-done) | data formatting | bytes 3670016 | tf_op jit(solution)/shard_map/all_to_all | solution.py:201
  64.5 7.3 %fusion.2 = f32[128,2,2048]{2,0,1:T(8,128)S(1)} fusion(bf16[128,2,3584]{0,2,1:T(8,128)(2,1)S(1)} %bitcast.70, bf16[1,3584,2048]{2,1,0:T(8,128)(2,1)} %param.13), kind=kOutput, calls=%fused_computation.6 | convolution fusion | flops 3758096384 | bytes 18612224 | tf_op jit(solution)/shard_map/skc,cf->skf/dot_general | solution.py:72
  71.8 5.2 %fusion.8 = bf16[128,2,3584]{2,0,1:T(8,128)(2,1)S(1)} fusion(bf16[1,1024,3584]{2,1,0:T(8,128)(2,1)} %param.14, f32[128,2,2048]{2,0,1:T(8,128)S(1)} %fusion.2), kind=kOutput, calls=%fused_computation.12 | convolution fusion | flops 1881538560 | bytes 11272192 | tf_op jit(solution)/shard_map/skf,fc->skc/dot_general | solution.py:77
  76.9 3.2 %copy.70 = bf16[128,2,3584]{2,1,0:T(2,128)(2,1)} copy(bf16[128,2,3584]{2,0,1:T(8,128)(2,1)S(1)} %fusion.8) | data formatting | bytes 3670016 | tf_op jit(solution)/shard_map/convert_element_type | solution.py:79
  80.1 8.7 %all-to-all-done.2 = bf16[128,2,3584]{2,1,0:T(2,128)(2,1)} async-done(((bf16[128,2,3584]{2,1,0:T(2,128)(2,1)}), bf16[128,2,3584]{2,1,0:T(2,128)(2,1)}, u32[]{:S(2)}, u32[]{:S(2)}) %all-to-all-start.2) | async-done | bytes 1835040 | tf_op jit(solution)/shard_map/all_to_all | solution.py:201
  88.8 4.3 %all-to-all-start.1 = ((bf16[128,2,3584]{2,1,0:T(2,128)(2,1)}), bf16[128,2,3584]{2,1,0:T(2,128)(2,1)S(1)}, u32[]{:S(2)}, u32[]{:S(2)}) async-start(bf16[128,2,3584]{2,1,0:T(2,128)(2,1)} %copy.70), calls=%async_computation.1 | async-start | bytes 3670016 | tf_op jit(solution)/shard_map/all_to_all | solution.py:204
  93.2 7.8 %fusion = f32[128,2,2048]{2,0,1:T(8,128)S(1)} fusion(bf16[1,3584,2048]{2,1,0:T(8,128)(2,1)} %param.13, bf16[128,2,3584]{2,1,0:T(2,128)(2,1)} %all-to-all-done.2), kind=kOutput, calls=%fused_computation.4 | convolution fusion | flops 3758096384 | bytes 18612224 | tf_op jit(solution)/shard_map/skc,cf->skf/dot_general | solution.py:72
  101.0 5.2 %fusion.11 = bf16[128,2,3584]{2,0,1:T(8,128)(2,1)S(1)} fusion(bf16[1,1024,3584]{2,1,0:T(8,128)(2,1)} %param.14, f32[128,2,2048]{2,0,1:T(8,128)S(1)} %fusion), kind=kOutput, calls=%fused_computation.13 | convolution fusion | flops 1881538560 | bytes 11272192 | tf_op jit(solution)/shard_map/skf,fc->skc/dot_general | solution.py:77
  106.2 3.2 %copy.80 = bf16[128,2,3584]{2,1,0:T(2,128)(2,1)} copy(bf16[128,2,3584]{2,0,1:T(8,128)(2,1)S(1)} %fusion.11) | data formatting | bytes 3670016 | tf_op jit(solution)/shard_map/convert_element_type | solution.py:79
  109.4 11.7 %all-to-all-done.1 = bf16[128,2,3584]{2,1,0:T(2,128)(2,1)S(1)} async-done(((bf16[128,2,3584]{2,1,0:T(2,128)(2,1)}), bf16[128,2,3584]{2,1,0:T(2,128)(2,1)S(1)}, u32[]{:S(2)}, u32[]{:S(2)}) %all-to-all-start.1) | async-done | bytes 1835040 | tf_op jit(solution)/shard_map/all_to_all | solution.py:204
  121.0 5.3 %all-to-all-start.3 = ((bf16[128,2,3584]{2,1,0:T(2,128)(2,1)}), bf16[128,2,3584]{2,1,0:T(2,128)(2,1)}, u32[]{:S(2)}, u32[]{:S(2)}) async-start(bf16[128,2,3584]{2,1,0:T(2,128)(2,1)} %copy.80), calls=%async_computation.3 | async-start | bytes 3670016 | tf_op jit(solution)/shard_map/all_to_all | solution.py:204
  126.4 2.9 %broadcast_select_fusion = bf16[16,128,576]{2,1,0:T(8,128)(2,1)S(1)} fusion(bf16[16,128,576]{2,1,0:T(8,128)(2,1)} %copy.84, bf16[16,128,576]{2,1,0:T(8,128)(2,1)} %copy.85, pred[16]{0:T(512)(128)(4,1)S(1)} %broadcast_compare_fusion.1), kind=kLoop, calls=%fused_computation.18 | loop fusion | flops 1179648 | bytes 7077904 | tf_op jit(solution)/shard_map/jit(_where)/select_n | solution.py:218
  129.3 1.3 fusion.58
  130.6 0.4 fusion.31
  131.0 1.6 %divide_convert_fusion = bf16[16,64,512]{2,1,0:T(8,128)(2,1)} fusion(bf16[16,128,576]{2,1,0:T(8,128)(2,1)S(1)} %broadcast_select_fusion, f32[16,64]{1,0:T(8,128)S(1)} %get-tuple-element.5, f32[16,512]{1,0:T(8,128)S(1)} %slice_convert_fusion, f32[16,64]{1,0:T(8,128)S(1)} %convert_element_type.110, f32[16,64,128]{2,1,0:T(8,128)S(1)} %get-tuple-element.14, ...), kind=kOutput, calls=%fused_computation.21 | convolution fusion | flops 136577024 | bytes 3727360 | tf_op jit(solution)/shard_map/nhl,nlc->nhc/dot_general | solution.py:167
  132.6 3.3 %gather_fusion = bf16[128,3584]{1,0:T(8,128)(2,1)} fusion(bf16[128,2,3584]{2,1,0:T(2,128)(2,1)S(1)} %all-to-all-done.1, s32[128]{0:T(128)S(1)} %fusion.55), kind=kCustom, calls=%fused_computation | custom fusion | bytes 1836032 | tf_op jit(solution)/shard_map/gather | solution.py:145
  135.8 1.9 %fusion.18 = bf16[16,3584]{1,0:T(8,128)(2,1)S(1)} fusion(bf16[128,3584]{1,0:T(8,128)(2,1)} %gather_fusion, f32[16,8]{1,0:T(8,128)S(1)} %copy.72), kind=kLoop, calls=%fused_computation.24 | loop fusion | flops 1318912 | bytes 1032704 | tf_op jit(solution)/shard_map/reduce_sum | solution.py:148
  137.7 16.2 %all-to-all-done.3 = bf16[128,2,3584]{2,1,0:T(2,128)(2,1)} async-done(((bf16[128,2,3584]{2,1,0:T(2,128)(2,1)}), bf16[128,2,3584]{2,1,0:T(2,128)(2,1)}, u32[]{:S(2)}, u32[]{:S(2)}) %all-to-all-start.3) | async-done | bytes 1835040 | tf_op jit(solution)/shard_map/all_to_all | solution.py:204
  154.0 2.3 %fusion.15 = bf16[1,16,3584]{2,1,0:T(8,128)(2,1)S(1)} fusion(bf16[128,2,3584]{2,1,0:T(2,128)(2,1)} %all-to-all-done.3, f32[16,128,2]{1,2,0:T(2,128)S(1)} %select_reduce_fusion), kind=kOutput, calls=%fused_computation.17 | convolution fusion | flops 176218112 | bytes 1966080 | tf_op jit(solution)/shard_map/stek,ekc->stc/dot_general | solution.py:132
  156.3 0.7 pad_maximum_fusion
  (39 shorter events, 0.6 us)
Async XLA Ops:
  0.6 37.8 %copy-start = (bf16[16,64,576]{2,1,0:T(8,128)(2,1)S(1)}, bf16[16,64,576]{2,1,0:T(8,128)(2,1)}, u32[]{:S(2)}) copy-start(bf16[16,64,576]{2,1,0:T(8,128)(2,1)} %param.15) | copy-start | bytes 3538948
  5.8 12.3 %slice-start = ((bf16[2,16,3584]{2,1,0:T(8,128)(2,1)}), bf16[1,16,3584]{2,1,0:T(8,128)(2,1)S(1)}, s32[]{:S(2)}) async-start(bf16[2,16,3584]{2,1,0:T(8,128)(2,1)} %param.10), calls=%async_computation.4 | async-start | bytes 229376 | tf_op jit(solution)/shard_map/slice | solution.py:199
  5.8 33.2 %collective-permute-start = (bf16[4,128,576]{1,2,0:T(8,128)(2,1)}, bf16[4,128,576]{1,2,0:T(8,128)(2,1)S(1)}, u32[]{:S(2)}, u32[]{:S(2)}) collective-permute-start(bf16[4,128,576]{1,2,0:T(8,128)(2,1)} %gather_fusion.2), channel_id=1, source_target_pairs={{0,64},{8,72},{16,80},{24,88},{32,96},{40,104},{48,112},{56,120},{... | collective-permute-start | bytes 1769480 | tf_op jit(solution)/shard_map/ppermute | solution.py:68
  20.2 35.8 %all-to-all-start = ((bf16[128,8,896]{2,1,0:T(8,128)(2,1)}), bf16[128,8,896]{2,1,0:T(8,128)(2,1)}, u32[]{:S(2)}, u32[]{:S(2)}) async-start(bf16[128,8,896]{2,1,0:T(8,128)(2,1)} %convert_bitcast_fusion), calls=%async_computation | async-start | bytes 3670016 | tf_op jit(solution)/shard_map/all_to_all | solution.py:201
  28.5 4.4 %copy-start.5 = (s32[16]{0:T(128)S(1)}, s32[16]{0:T(128)}, u32[]{:S(2)}) copy-start(s32[16]{0:T(128)} %param.19) | copy-start | bytes 196
  28.5 4.7 %copy-start.4 = (f32[2,16,8]{1,2,0:T(8,128)S(1)}, f32[2,16,8]{1,2,0:T(8,128)}, u32[]{:S(2)}) copy-start(f32[2,16,8]{1,2,0:T(8,128)} %param.12) | copy-start | bytes 3076
  28.5 5.0 %copy-start.2 = (bf16[2,16,3584]{2,1,0:T(8,128)(2,1)S(1)}, bf16[2,16,3584]{2,1,0:T(8,128)(2,1)}, u32[]{:S(2)}) copy-start(bf16[2,16,3584]{2,1,0:T(8,128)(2,1)} %param.10) | copy-start | bytes 688132
  34.3 3.1 %copy-start.1 = (s32[2048]{0:T(1024)S(1)}, s32[2048]{0:T(1024)}, u32[]{:S(2)}) copy-start(s32[2048]{0:T(1024)} %param.18) | copy-start | bytes 24580
  34.3 4.2 %copy-start.3 = (bf16[16,576]{1,0:T(8,128)(2,1)S(1)}, bf16[16,576]{1,0:T(8,128)(2,1)}, u32[]{:S(2)}) copy-start(bf16[16,576]{1,0:T(8,128)(2,1)} %param.16) | copy-start | bytes 55300
  55.9 32.9 %all-to-all-start.2 = ((bf16[128,2,3584]{2,1,0:T(2,128)(2,1)}), bf16[128,2,3584]{2,1,0:T(2,128)(2,1)}, u32[]{:S(2)}, u32[]{:S(2)}) async-start(bf16[128,2,3584]{2,1,0:T(2,128)(2,1)} %copy.78), calls=%async_computation.2 | async-start | bytes 3670016 | tf_op jit(solution)/shard_map/all_to_all | solution.py:201
  88.8 32.2 %all-to-all-start.1 = ((bf16[128,2,3584]{2,1,0:T(2,128)(2,1)}), bf16[128,2,3584]{2,1,0:T(2,128)(2,1)S(1)}, u32[]{:S(2)}, u32[]{:S(2)}) async-start(bf16[128,2,3584]{2,1,0:T(2,128)(2,1)} %copy.70), calls=%async_computation.1 | async-start | bytes 3670016 | tf_op jit(solution)/shard_map/all_to_all | solution.py:204
  121.0 32.9 %all-to-all-start.3 = ((bf16[128,2,3584]{2,1,0:T(2,128)(2,1)}), bf16[128,2,3584]{2,1,0:T(2,128)(2,1)}, u32[]{:S(2)}, u32[]{:S(2)}) async-start(bf16[128,2,3584]{2,1,0:T(2,128)(2,1)} %copy.80), calls=%async_computation.3 | async-start | bytes 3670016 | tf_op jit(solution)/shard_map/all_to_all | solution.py:204

commit v12 on v9

--- a/solution.py
+++ b/solution.py
@@ -183,7 +183,9 @@
     )
     row_count = swapped.shape[0]
     top_bit = lax.axis_size("dp").bit_length() - 2
-    outgoing = jnp.argsort(1 - swapped, stable=True)[:MOVE]
+    rank = jnp.cumsum(swapped) - 1
+    picks = (swapped[None, :] == 1) & (rank[None, :] == jnp.arange(MOVE, dtype=jnp.int32)[:, None])
+    outgoing = jnp.sum(jnp.where(picks, jnp.arange(row_count, dtype=jnp.int32)[None, :], 0), axis=1)
     arrival = jnp.clip(jnp.cumsum(swapped) - 1, 0, MOVE - 1)
     is_moved = swapped == 1
     device_rows = lax.axis_index(("dp", "ep")) * row_count + jnp.arange(row_count, dtype=jnp.int32)

time: 154 us -> 154 us (level)
  waiting for transfers between devices: 50.2 us -> 47.7 us
  local copies, waits for them, and re-layouts: 32.7 us -> 34.8 us
    all_to_all x2, waiting for transfers between devices: 22.3 us -> 19.7 us  [per_device(): lax.all_to_all(p[0], ('dp', 'ep'), 0, 0, tiled=True)]
  transfers between devices with their start and end apart: 5 -> 5, of which waited for: 4 -> 4; matrix products, arithmetic and copies ran while one was open for 43% -> 45% of each run, Pallas kernels for 0% -> 0%
where the time goes in v12:
time: 154 us; the launch traced here: 153 us
  waiting for transfers between devices  47.7 us (31%)
  local copies, waits for them, and re-layouts  34.8 us (23%)
  matrix products  34.2 us (22%)
  starting transfers between devices  26.9 us (17%)
  other arithmetic  8.3 us (5%)
    all_to_all x2, waiting for transfers between devices, per_device(): lax.all_to_all(f, ('dp', 'ep'), 0, 0, tiled=True)  27.9 us
    all_to_all x2, waiting for transfers between devices, per_device(): lax.all_to_all(p[0], ('dp', 'ep'), 0, 0, tiled=True)  19.7 us
    dot_general x2, matrix products, expert_rows(): jnp.einsum('skc,cf->skf', picked, expert_in, preferred_element_type=jnp.f...  15.6 us
    all_to_all x2, starting transfers between devices, per_device(): lax.all_to_all(p[0], ('dp', 'ep'), 0, 0, tiled=True)  12.7 us
    dot_general x2, matrix products, expert_rows(): jnp.einsum('skf,fc->skc', activated, expert_out, preferred_element_type=j...  10.4 us
    all_to_all x2, starting transfers between devices, per_device(): lax.all_to_all(f, ('dp', 'ep'), 0, 0, tiled=True)  9.69 us
    convert_element_type x2, local copies, waits for them, and re-layouts, pack_rows(): packed = jnp.einsum('dkt,tc->dkc', select, flat_tokens, preferred_element...  7.77 us
    gather x2, local copies, waits for them, and re-layouts, per_device(): incoming_cache[arrival]  6.67 us
  transfers between devices with their start and end apart: 5, of which 4 were waited for; matrix products, arithmetic and copies ran while one was open for 45% of the time, Pallas kernels for 0%

profile of v12, /device:TPU:1, one launch (start us, length us, event | category | flops | bytes accessed | tf_op | source)
XLA Modules:
  0.0 152.8 jit_solution(13795837665621525496)
XLA Ops:
  0.6 0.0 copy-start
  0.6 0.0 copy-start.3
  0.7 0.8 broadcast_compare_fusion
  1.4 0.7 copy.76
  2.2 0.1 fusion.45
  2.3 0.1 select_reduce_fusion.3
  2.5 2.3 %gather_fusion.2 = bf16[4,128,576]{1,2,0:T(8,128)(2,1)S(1)} fusion(bf16[16,128,576]{1,2,0:T(8,128)(2,1)} %param.17, s32[1024]{0:T(1024)S(1)} %pad_clamp_fusion.1), kind=kCustom, calls=%fused_computation.2 | custom fusion | bytes 1179664 | tf_op jit(solution)/shard_map/gather | solution.py:194
  4.8 4.5 %collective-permute-start = (bf16[4,128,576]{1,2,0:T(8,128)(2,1)S(1)}, bf16[4,128,576]{1,2,0:T(8,128)(2,1)S(1)}, u32[]{:S(2)}, u32[]{:S(2)}) collective-permute-start(bf16[4,128,576]{1,2,0:T(8,128)(2,1)S(1)} %gather_fusion.2), channel_id=1, source_target_pairs={{0,64},{8,72},{16,80},{24,88},{32,96},{40,104},{48,112},{56,120},{... | collective-permute-start | bytes 1769480 | tf_op jit(solution)/shard_map/ppermute | solution.py:68
  9.3 0.7 fusion.60
  10.0 0.1 copy.87
  10.1 0.1 eq.143
  10.2 0.1 fusion.40
  10.3 0.2 reduce_window_sum.26
  10.4 0.2 select_reduce_fusion.1
  10.6 0.1 reshape.492
  10.7 0.1 copy.86
  10.8 0.1 eq.135
  10.9 0.1 fusion.41
  11.0 0.2 reduce_window_sum.25
  11.2 0.2 select_reduce_fusion.2
  11.3 0.1 reshape.489
  11.4 0.2 compare_reduce_fusion.1
  11.6 0.0 copy-done.3
  11.6 0.7 convolution_convert_fusion.1
  12.3 3.1 %copy.62 = bf16[128,2,3584]{2,1,0:T(2,128)(2,1)} copy(bf16[128,2,3584]{2,0,1:T(8,128)(2,1)S(1)} %convolution_convert_fusion.1) | data formatting | bytes 3670016 | tf_op jit(solution)/shard_map/convert_element_type | solution.py:102
  15.4 8.3 %all-to-all-start = ((bf16[128,2,3584]{2,1,0:T(2,128)(2,1)}), bf16[128,2,3584]{2,1,0:T(2,128)(2,1)}, u32[]{:S(2)}, u32[]{:S(2)}) async-start(bf16[128,2,3584]{2,1,0:T(2,128)(2,1)} %copy.62), calls=%async_computation | async-start | bytes 3670016 | tf_op jit(solution)/shard_map/all_to_all | solution.py:177
  23.8 1.9 %convolution_convert_fusion = bf16[128,2,3584]{2,0,1:T(8,128)(2,1)} fusion(pred[128,2,16]{0,2,1:T(8,128)(4,1)S(1)} %get-tuple-element.5, bf16[2,16,3584]{2,1,0:T(8,128)(2,1)S(1)} %copy-done.3), kind=kOutput, calls=%fused_computation.14 | convolution fusion | flops 30277632 | bytes 1953792 | tf_op jit(solution)/shard_map/dkt,tc->dkc/dot_general | solution.py:100
  25.7 4.3 %copy.78 = bf16[16,128,576]{2,1,0:T(8,128)(2,1)} copy(bf16[16,128,576]{1,2,0:T(8,128)(2,1)} %param.17) | data formatting | bytes 4718592 | tf_op args[7]
  30.0 0.1 reshape.491
  30.1 0.0 copy-start.4
  30.1 4.7 %copy.71 = bf16[128,2,3584]{2,1,0:T(2,128)(2,1)} copy(bf16[128,2,3584]{2,0,1:T(8,128)(2,1)} %convolution_convert_fusion) | data formatting | bytes 3670016 | tf_op jit(solution)/shard_map/convert_element_type | solution.py:102
  34.8 0.0 copy-done.5
  34.8 0.1 copy.69
  34.9 0.1 copy.65
  34.9 0.0 copy-done.6
  35.0 0.7 gather_fusion.1
  35.6 0.1 select_reduce_fusion
  35.8 0.1 iota_compare_fusion.2
  35.9 0.5 fusion.42
  36.4 0.0 collective-permute-done
  36.4 2.3 %gather_fusion.3 = bf16[16,128,576]{1,2,0:T(8,128)(2,1)} fusion(bf16[4,128,576]{1,2,0:T(8,128)(2,1)S(1)} %collective-permute-done, s32[1024]{0:T(1024)S(1)} %pad_clamp_fusion), kind=kCustom, calls=%fused_computation.3 | custom fusion | bytes 4718656 | tf_op jit(solution)/shard_map/gather | solution.py:195
  38.7 4.4 %copy.77 = bf16[16,128,576]{2,1,0:T(8,128)(2,1)} copy(bf16[16,128,576]{1,2,0:T(8,128)(2,1)} %gather_fusion.3) | data formatting | bytes 4718592 | tf_op jit(solution)/shard_map/gather | solution.py:195
  43.1 8.1 %all-to-all-done = bf16[128,2,3584]{2,1,0:T(2,128)(2,1)} async-done(((bf16[128,2,3584]{2,1,0:T(2,128)(2,1)}), bf16[128,2,3584]{2,1,0:T(2,128)(2,1)}, u32[]{:S(2)}, u32[]{:S(2)}) %all-to-all-start) | async-done | bytes 1835040 | tf_op jit(solution)/shard_map/all_to_all | solution.py:177
  51.2 4.3 %all-to-all-start.2 = ((bf16[128,2,3584]{2,1,0:T(2,128)(2,1)}), bf16[128,2,3584]{2,1,0:T(2,128)(2,1)S(1)}, u32[]{:S(2)}, u32[]{:S(2)}) async-start(bf16[128,2,3584]{2,1,0:T(2,128)(2,1)} %copy.71), calls=%async_computation.2 | async-start | bytes 3670016 | tf_op jit(solution)/shard_map/all_to_all | solution.py:177
  55.5 7.8 %fusion.2 = f32[128,2,2048]{2,0,1:T(8,128)S(1)} fusion(bf16[1,3584,2048]{2,1,0:T(8,128)(2,1)} %param.13, bf16[128,2,3584]{2,1,0:T(2,128)(2,1)} %all-to-all-done), kind=kOutput, calls=%fused_computation.6 | convolution fusion | flops 3758096384 | bytes 18612224 | tf_op jit(solution)/shard_map/skc,cf->skf/dot_general | solution.py:72
  63.3 5.2 %fusion.8 = bf16[128,2,3584]{2,0,1:T(8,128)(2,1)S(1)} fusion(bf16[1,1024,3584]{2,1,0:T(8,128)(2,1)} %param.14, f32[128,2,2048]{2,0,1:T(8,128)S(1)} %fusion.2), kind=kOutput, calls=%fused_computation.12 | convolution fusion | flops 1881538560 | bytes 11272192 | tf_op jit(solution)/shard_map/skf,fc->skc/dot_general | solution.py:77
  68.5 3.2 %copy.64 = bf16[128,2,3584]{2,1,0:T(2,128)(2,1)} copy(bf16[128,2,3584]{2,0,1:T(8,128)(2,1)S(1)} %fusion.8) | data formatting | bytes 3670016 | tf_op jit(solution)/shard_map/convert_element_type | solution.py:79
  71.7 11.7 %all-to-all-done.2 = bf16[128,2,3584]{2,1,0:T(2,128)(2,1)S(1)} async-done(((bf16[128,2,3584]{2,1,0:T(2,128)(2,1)}), bf16[128,2,3584]{2,1,0:T(2,128)(2,1)S(1)}, u32[]{:S(2)}, u32[]{:S(2)}) %all-to-all-start.2) | async-done | bytes 1835040 | tf_op jit(solution)/shard_map/all_to_all | solution.py:177
  83.4 1.3 copy-done.2
  84.7 4.3 %all-to-all-start.1 = ((bf16[128,2,3584]{2,1,0:T(2,128)(2,1)}), bf16[128,2,3584]{2,1,0:T(2,128)(2,1)S(1)}, u32[]{:S(2)}, u32[]{:S(2)}) async-start(bf16[128,2,3584]{2,1,0:T(2,128)(2,1)} %copy.64), calls=%async_computation.1 | async-start | bytes 3670016 | tf_op jit(solution)/shard_map/all_to_all | solution.py:179
  89.0 7.8 %fusion = f32[128,2,2048]{2,0,1:T(8,128)S(1)} fusion(bf16[1,3584,2048]{2,1,0:T(8,128)(2,1)} %param.13, bf16[128,2,3584]{2,1,0:T(2,128)(2,1)} %copy-done.2), kind=kOutput, calls=%fused_computation.4 | convolution fusion | flops 3758096384 | bytes 18612224 | tf_op jit(solution)/shard_map/skc,cf->skf/dot_general | solution.py:72
  96.8 5.2 %fusion.11 = bf16[128,2,3584]{2,0,1:T(8,128)(2,1)S(1)} fusion(bf16[1,1024,3584]{2,1,0:T(8,128)(2,1)} %param.14, f32[128,2,2048]{2,0,1:T(8,128)S(1)} %fusion), kind=kOutput, calls=%fused_computation.13 | convolution fusion | flops 1881538560 | bytes 11272192 | tf_op jit(solution)/shard_map/skf,fc->skc/dot_general | solution.py:77
  102.0 3.2 %copy.73 = bf16[128,2,3584]{2,1,0:T(2,128)(2,1)} copy(bf16[128,2,3584]{2,0,1:T(8,128)(2,1)S(1)} %fusion.11) | data formatting | bytes 3670016 | tf_op jit(solution)/shard_map/convert_element_type | solution.py:79
  105.2 11.7 %all-to-all-done.1 = bf16[128,2,3584]{2,1,0:T(2,128)(2,1)S(1)} async-done(((bf16[128,2,3584]{2,1,0:T(2,128)(2,1)}), bf16[128,2,3584]{2,1,0:T(2,128)(2,1)S(1)}, u32[]{:S(2)}, u32[]{:S(2)}) %all-to-all-start.1) | async-done | bytes 1835040 | tf_op jit(solution)/shard_map/all_to_all | solution.py:179
  116.9 5.3 %all-to-all-start.3 = ((bf16[128,2,3584]{2,1,0:T(2,128)(2,1)}), bf16[128,2,3584]{2,1,0:T(2,128)(2,1)}, u32[]{:S(2)}, u32[]{:S(2)}) async-start(bf16[128,2,3584]{2,1,0:T(2,128)(2,1)} %copy.73), calls=%async_computation.3 | async-start | bytes 3670016 | tf_op jit(solution)/shard_map/all_to_all | solution.py:179
  122.2 2.9 %broadcast_select_fusion = bf16[16,128,576]{2,1,0:T(8,128)(2,1)S(1)} fusion(bf16[16,128,576]{2,1,0:T(8,128)(2,1)} %copy.77, bf16[16,128,576]{2,1,0:T(8,128)(2,1)} %copy.78, pred[16]{0:T(512)(128)(4,1)S(1)} %broadcast_compare_fusion), kind=kLoop, calls=%fused_computation.19 | loop fusion | flops 1179648 | bytes 7077904 | tf_op jit(solution)/shard_map/jit(_where)/select_n | solution.py:195
  125.1 1.3 fusion.61
  126.4 0.4 fusion.32
  126.8 1.6 %divide_convert_fusion = bf16[16,64,512]{2,1,0:T(8,128)(2,1)} fusion(bf16[16,128,576]{2,1,0:T(8,128)(2,1)S(1)} %broadcast_select_fusion, f32[16,64]{1,0:T(8,128)S(1)} %get-tuple-element.7, f32[16,512]{1,0:T(8,128)S(1)} %slice_convert_fusion, f32[16,64]{1,0:T(8,128)S(1)} %convert_element_type.125, f32[16,64,128]{2,1,0:T(8,128)S(1)} %get-tuple-element.13, ...), kind=kOutput, calls=%fused_computation.22 | convolution fusion | flops 136577024 | bytes 3727360 | tf_op jit(solution)/shard_map/nhl,nlc->nhc/dot_general | solution.py:146
  128.4 3.3 %gather_fusion = bf16[128,3584]{1,0:T(8,128)(2,1)} fusion(bf16[128,2,3584]{2,1,0:T(2,128)(2,1)S(1)} %all-to-all-done.1, s32[128]{0:T(128)S(1)} %fusion.57), kind=kCustom, calls=%fused_computation | custom fusion | bytes 1836032 | tf_op jit(solution)/shard_map/gather | solution.py:124
  131.6 1.9 %fusion.18 = bf16[16,3584]{1,0:T(8,128)(2,1)S(1)} fusion(bf16[128,3584]{1,0:T(8,128)(2,1)} %gather_fusion, f32[16,8]{1,0:T(8,128)S(1)} %copy.65), kind=kLoop, calls=%fused_computation.24 | loop fusion | flops 1318912 | bytes 1032704 | tf_op jit(solution)/shard_map/reduce_sum | solution.py:127
  133.5 16.2 %all-to-all-done.3 = bf16[128,2,3584]{2,1,0:T(2,128)(2,1)} async-done(((bf16[128,2,3584]{2,1,0:T(2,128)(2,1)}), bf16[128,2,3584]{2,1,0:T(2,128)(2,1)}, u32[]{:S(2)}, u32[]{:S(2)}) %all-to-all-start.3) | async-done | bytes 1835040 | tf_op jit(solution)/shard_map/all_to_all | solution.py:179
  149.8 2.3 %fusion.15 = bf16[1,16,3584]{2,1,0:T(8,128)(2,1)S(1)} fusion(bf16[128,2,3584]{2,1,0:T(2,128)(2,1)} %all-to-all-done.3, f32[16,128,2]{1,2,0:T(2,128)S(1)} %select_reduce_fusion), kind=kOutput, calls=%fused_computation.18 | convolution fusion | flops 176218112 | bytes 1966080 | tf_op jit(solution)/shard_map/stek,ekc->stc/dot_general | solution.py:111
  152.1 0.7 pad_maximum_fusion
  (22 shorter events, 0.2 us)
Async XLA Ops:
  0.6 35.3 %copy-start = (bf16[16,64,576]{2,1,0:T(8,128)(2,1)S(1)}, bf16[16,64,576]{2,1,0:T(8,128)(2,1)}, u32[]{:S(2)}) copy-start(bf16[16,64,576]{2,1,0:T(8,128)(2,1)} %param.15) | copy-start | bytes 3538948
  0.6 11.0 %copy-start.3 = (bf16[2,16,3584]{2,1,0:T(8,128)(2,1)S(1)}, bf16[2,16,3584]{2,1,0:T(8,128)(2,1)}, u32[]{:S(2)}) copy-start(bf16[2,16,3584]{2,1,0:T(8,128)(2,1)} %param.10) | copy-start | bytes 688132
  4.8 31.6 %collective-permute-start = (bf16[4,128,576]{1,2,0:T(8,128)(2,1)S(1)}, bf16[4,128,576]{1,2,0:T(8,128)(2,1)S(1)}, u32[]{:S(2)}, u32[]{:S(2)}) collective-permute-start(bf16[4,128,576]{1,2,0:T(8,128)(2,1)S(1)} %gather_fusion.2), channel_id=1, source_target_pairs={{0,64},{8,72},{16,80},{24,88},{32,96},{40,104},{48,112},{56,120},{... | collective-permute-start | bytes 1769480 | tf_op jit(solution)/shard_map/ppermute | solution.py:68
  15.4 35.8 %all-to-all-start = ((bf16[128,2,3584]{2,1,0:T(2,128)(2,1)}), bf16[128,2,3584]{2,1,0:T(2,128)(2,1)}, u32[]{:S(2)}, u32[]{:S(2)}) async-start(bf16[128,2,3584]{2,1,0:T(2,128)(2,1)} %copy.62), calls=%async_computation | async-start | bytes 3670016 | tf_op jit(solution)/shard_map/all_to_all | solution.py:177
  30.0 4.8 %copy-start.5 = (f32[2,16,8]{1,2,0:T(8,128)S(1)}, f32[2,16,8]{1,2,0:T(8,128)}, u32[]{:S(2)}) copy-start(f32[2,16,8]{1,2,0:T(8,128)} %param.12) | copy-start | bytes 3076
  30.0 4.9 %copy-start.6 = (s32[16]{0:T(128)S(1)}, s32[16]{0:T(128)}, u32[]{:S(2)}) copy-start(s32[16]{0:T(128)} %param.19) | copy-start | bytes 196
  30.0 5.0 %copy-start.1 = (s32[2048]{0:T(1024)S(1)}, s32[2048]{0:T(1024)}, u32[]{:S(2)}) copy-start(s32[2048]{0:T(1024)} %param.18) | copy-start | bytes 24580
  30.1 5.8 %copy-start.4 = (bf16[16,576]{1,0:T(8,128)(2,1)S(1)}, bf16[16,576]{1,0:T(8,128)(2,1)}, u32[]{:S(2)}) copy-start(bf16[16,576]{1,0:T(8,128)(2,1)} %param.16) | copy-start | bytes 55300
  51.2 32.2 %all-to-all-start.2 = ((bf16[128,2,3584]{2,1,0:T(2,128)(2,1)}), bf16[128,2,3584]{2,1,0:T(2,128)(2,1)S(1)}, u32[]{:S(2)}, u32[]{:S(2)}) async-start(bf16[128,2,3584]{2,1,0:T(2,128)(2,1)} %copy.71), calls=%async_computation.2 | async-start | bytes 3670016 | tf_op jit(solution)/shard_map/all_to_all | solution.py:177
  83.4 1.3 copy-start.2
  84.7 32.2 %all-to-all-start.1 = ((bf16[128,2,3584]{2,1,0:T(2,128)(2,1)}), bf16[128,2,3584]{2,1,0:T(2,128)(2,1)S(1)}, u32[]{:S(2)}, u32[]{:S(2)}) async-start(bf16[128,2,3584]{2,1,0:T(2,128)(2,1)} %copy.64), calls=%async_computation.1 | async-start | bytes 3670016 | tf_op jit(solution)/shard_map/all_to_all | solution.py:179
  116.9 32.9 %all-to-all-start.3 = ((bf16[128,2,3584]{2,1,0:T(2,128)(2,1)}), bf16[128,2,3584]{2,1,0:T(2,128)(2,1)}, u32[]{:S(2)}, u32[]{:S(2)}) async-start(bf16[128,2,3584]{2,1,0:T(2,128)(2,1)} %copy.73), calls=%async_computation.3 | async-start | bytes 3670016 | tf_op jit(solution)/shard_map/all_to_all | solution.py:179

commit v13 on v12

--- a/solution.py
+++ b/solution.py
@@ -103,7 +103,7 @@
     return packed, target
 
 
-def unpack_rows(returned, target, gate_values):
+def unpack_rows(returned, target, gate_values, base):
     expert_count, slot_cap, _ = returned.shape
     places = jnp.arange(expert_count * slot_cap, dtype=jnp.int32).reshape(expert_count, slot_cap)
     chosen = target[..., None, None] == places
@@ -115,7 +115,7 @@
         precision=lax.Precision.HIGHEST,
         preferred_element_type=jnp.float32,
     )
-    return summed.astype(jnp.bfloat16)
+    return (summed + base).astype(jnp.bfloat16)
 
 
 def gather_rows(returned, target, gate_values):
@@ -177,10 +177,11 @@
     received = [lax.all_to_all(p[0], ("dp", "ep"), 0, 0, tiled=True) for p in packs]
     finished = [expert_rows(r, expert_in[0], expert_out[0]) for r in received]
     returned = [lax.all_to_all(f, ("dp", "ep"), 0, 0, tiled=True) for f in finished]
-    mixed = jnp.concatenate(
-        [gather_rows(returned[0], packs[0][1], route_weights[0:1])]
-        + [unpack_rows(returned[step], packs[step][1], route_weights[step : step + 1]) for step in range(1, STEPS)]
-    )
+    early = gather_rows(returned[0], packs[0][1], route_weights[0:1])
+    late_target = jnp.concatenate([jnp.zeros_like(packs[1][1]), packs[1][1]])
+    late_gates = jnp.concatenate([jnp.zeros_like(route_weights[0:1]), route_weights[1:2]])
+    earlier_rows = jnp.concatenate([early, jnp.zeros_like(early)]).astype(jnp.float32)
+    mixed = unpack_rows(returned[1], late_target, late_gates, earlier_rows)
     row_count = swapped.shape[0]
     top_bit = lax.axis_size("dp").bit_length() - 2
     rank = jnp.cumsum(swapped) - 1

time: 154 us -> 154 us (level)
  waiting for transfers between devices: 47.7 us -> 50.3 us
    all_to_all x2, waiting for transfers between devices: 19.7 us -> 22.4 us  [per_device(): lax.all_to_all(p[0], ('dp', 'ep'), 0, 0, tiled=True)]
    unnamed x17 -> x18, local copies, waits for them, and re-layouts: 5.79 us -> 5.87 us
  transfers between devices with their start and end apart: 5 -> 5, of which waited for: 4 -> 4; matrix products, arithmetic and copies ran while one was open for 45% -> 43% of each run, Pallas kernels for 0% -> 0%
where the time goes in v13:
time: 154 us; the launch traced here: 153 us
  waiting for transfers between devices  50.3 us (33%)
  matrix products  33.8 us (22%)
  local copies, waits for them, and re-layouts  33.4 us (22%)
  starting transfers between devices  26.9 us (17%)
  other arithmetic  7.64 us (5%)
    all_to_all x2, waiting for transfers between devices, per_device(): lax.all_to_all(f, ('dp', 'ep'), 0, 0, tiled=True)  27.9 us
    all_to_all x2, waiting for transfers between devices, per_device(): lax.all_to_all(p[0], ('dp', 'ep'), 0, 0, tiled=True)  22.4 us
    dot_general x2, matrix products, expert_rows(): jnp.einsum('skc,cf->skf', picked, expert_in, preferred_element_type=jnp.f...  15.6 us
    all_to_all x2, starting transfers between devices, per_device(): lax.all_to_all(p[0], ('dp', 'ep'), 0, 0, tiled=True)  12.7 us
    dot_general x2, matrix products, expert_rows(): jnp.einsum('skf,fc->skc', activated, expert_out, preferred_element_type=j...  10.4 us
    all_to_all x2, starting transfers between devices, per_device(): lax.all_to_all(f, ('dp', 'ep'), 0, 0, tiled=True)  9.69 us
    gather x2, local copies, waits for them, and re-layouts, per_device(): incoming_cache[arrival]  6.67 us
    convert_element_type x2, local copies, waits for them, and re-layouts, expert_rows(): return jnp.einsum('skf,fc->skc', activated, expert_out, preferred_element...  6.37 us
  transfers between devices with their start and end apart: 5, of which 4 were waited for; matrix products, arithmetic and copies ran while one was open for 43% of the time, Pallas kernels for 0%

profile of v13, /device:TPU:1, one launch (start us, length us, event | category | flops | bytes accessed | tf_op | source)
XLA Modules:
  0.0 153.0 jit_solution(1849552877080775165)
XLA Ops:
  0.6 0.0 copy-start
  0.6 0.0 copy-start.3
  0.7 0.8 broadcast_compare_fusion
  1.4 0.7 copy.72
  2.2 0.1 fusion.46
  2.3 0.1 select_reduce_fusion.3
  2.5 2.3 %gather_fusion.2 = bf16[4,128,576]{1,2,0:T(8,128)(2,1)S(1)} fusion(bf16[16,128,576]{1,2,0:T(8,128)(2,1)} %param.17, s32[1024]{0:T(1024)S(1)} %pad_clamp_fusion.1), kind=kCustom, calls=%fused_computation.2 | custom fusion | bytes 1179664 | tf_op jit(solution)/shard_map/gather | solution.py:195
  4.8 4.5 %collective-permute-start = (bf16[4,128,576]{1,2,0:T(8,128)(2,1)S(1)}, bf16[4,128,576]{1,2,0:T(8,128)(2,1)S(1)}, u32[]{:S(2)}, u32[]{:S(2)}) collective-permute-start(bf16[4,128,576]{1,2,0:T(8,128)(2,1)S(1)} %gather_fusion.2), channel_id=1, source_target_pairs={{0,64},{8,72},{16,80},{24,88},{32,96},{40,104},{48,112},{56,120},{... | collective-permute-start | bytes 1769480 | tf_op jit(solution)/shard_map/ppermute | solution.py:68
  9.3 0.7 fusion.62
  10.0 0.1 copy.82
  10.1 0.1 eq.127
  10.2 0.1 fusion.42
  10.3 0.2 reduce_window_sum.25
  10.4 0.2 select_reduce_fusion.2
  10.6 0.1 reshape.470
  10.7 0.1 copy.83
  10.8 0.1 eq.138
  10.9 0.1 fusion.41
  11.0 0.2 reduce_window_sum.26
  11.2 0.2 select_reduce_fusion.1
  11.3 0.1 reshape.472
  11.4 0.2 compare_reduce_fusion
  11.6 0.0 copy-done.3
  11.6 0.7 convolution_convert_fusion
  12.3 3.2 %copy.68 = bf16[128,2,3584]{2,1,0:T(2,128)(2,1)} copy(bf16[128,2,3584]{2,0,1:T(8,128)(2,1)S(1)} %convolution_convert_fusion) | data formatting | bytes 3670016 | tf_op jit(solution)/shard_map/convert_element_type | solution.py:102
  15.5 8.3 %all-to-all-start.2 = ((bf16[128,2,3584]{2,1,0:T(2,128)(2,1)}), bf16[128,2,3584]{2,1,0:T(2,128)(2,1)}, u32[]{:S(2)}, u32[]{:S(2)}) async-start(bf16[128,2,3584]{2,1,0:T(2,128)(2,1)} %copy.68), calls=%async_computation.2 | async-start | bytes 3670016 | tf_op jit(solution)/shard_map/all_to_all | solution.py:177
  23.8 4.3 %copy.74 = bf16[16,128,576]{2,1,0:T(8,128)(2,1)} copy(bf16[16,128,576]{1,2,0:T(8,128)(2,1)} %param.17) | data formatting | bytes 4718592 | tf_op args[7]
  28.2 0.1 reshape.474
  28.3 0.1 copy.71
  28.3 0.7 convolution_convert_fusion.1
  29.0 0.0 copy-start.6
  29.0 0.0 copy-start.1
  29.0 0.0 copy-start.4
  29.1 3.1 %copy.60 = bf16[128,2,3584]{2,1,0:T(2,128)(2,1)} copy(bf16[128,2,3584]{2,0,1:T(8,128)(2,1)S(1)} %convolution_convert_fusion.1) | data formatting | bytes 3670016 | tf_op jit(solution)/shard_map/convert_element_type | solution.py:102
  32.2 0.1 copy.84
  32.2 0.0 copy-done.6
  32.3 0.7 gather_fusion.1
  32.9 0.2 select_reduce_fusion
  33.2 0.1 iota_compare_fusion.2
  33.3 0.5 fusion.43
  33.8 0.0 collective-permute-done
  33.8 2.3 %gather_fusion.3 = bf16[16,128,576]{1,2,0:T(8,128)(2,1)} fusion(bf16[4,128,576]{1,2,0:T(8,128)(2,1)S(1)} %collective-permute-done, s32[1024]{0:T(1024)S(1)} %pad_clamp_fusion), kind=kCustom, calls=%fused_computation.3 | custom fusion | bytes 4718656 | tf_op jit(solution)/shard_map/gather | solution.py:196
  36.1 4.4 %copy.73 = bf16[16,128,576]{2,1,0:T(8,128)(2,1)} copy(bf16[16,128,576]{1,2,0:T(8,128)(2,1)} %gather_fusion.3) | data formatting | bytes 4718592 | tf_op jit(solution)/shard_map/gather | solution.py:196
  40.4 10.8 %all-to-all-done.2 = bf16[128,2,3584]{2,1,0:T(2,128)(2,1)} async-done(((bf16[128,2,3584]{2,1,0:T(2,128)(2,1)}), bf16[128,2,3584]{2,1,0:T(2,128)(2,1)}, u32[]{:S(2)}, u32[]{:S(2)}) %all-to-all-start.2) | async-done | bytes 1835040 | tf_op jit(solution)/shard_map/all_to_all | solution.py:177
  51.2 4.3 %all-to-all-start = ((bf16[128,2,3584]{2,1,0:T(2,128)(2,1)}), bf16[128,2,3584]{2,1,0:T(2,128)(2,1)S(1)}, u32[]{:S(2)}, u32[]{:S(2)}) async-start(bf16[128,2,3584]{2,1,0:T(2,128)(2,1)} %copy.60), calls=%async_computation | async-start | bytes 3670016 | tf_op jit(solution)/shard_map/all_to_all | solution.py:177
  55.6 7.8 %fusion = f32[128,2,2048]{2,0,1:T(8,128)S(1)} fusion(bf16[1,3584,2048]{2,1,0:T(8,128)(2,1)} %param.13, bf16[128,2,3584]{2,1,0:T(2,128)(2,1)} %all-to-all-done.2), kind=kOutput, calls=%fused_computation.4 | convolution fusion | flops 3758096384 | bytes 18612224 | tf_op jit(solution)/shard_map/skc,cf->skf/dot_general | solution.py:72
  63.4 5.2 %fusion.11 = bf16[128,2,3584]{2,0,1:T(8,128)(2,1)S(1)} fusion(bf16[1,1024,3584]{2,1,0:T(8,128)(2,1)} %param.14, f32[128,2,2048]{2,0,1:T(8,128)S(1)} %fusion), kind=kOutput, calls=%fused_computation.13 | convolution fusion | flops 1881538560 | bytes 11272192 | tf_op jit(solution)/shard_map/skf,fc->skc/dot_general | solution.py:77
  68.6 3.2 %copy.70 = bf16[128,2,3584]{2,1,0:T(2,128)(2,1)} copy(bf16[128,2,3584]{2,0,1:T(8,128)(2,1)S(1)} %fusion.11) | data formatting | bytes 3670016 | tf_op jit(solution)/shard_map/convert_element_type | solution.py:79
  71.8 11.7 %all-to-all-done = bf16[128,2,3584]{2,1,0:T(2,128)(2,1)S(1)} async-done(((bf16[128,2,3584]{2,1,0:T(2,128)(2,1)}), bf16[128,2,3584]{2,1,0:T(2,128)(2,1)S(1)}, u32[]{:S(2)}, u32[]{:S(2)}) %all-to-all-start) | async-done | bytes 1835040 | tf_op jit(solution)/shard_map/all_to_all | solution.py:177
  83.4 1.3 copy-done.2
  84.7 4.3 %all-to-all-start.3 = ((bf16[128,2,3584]{2,1,0:T(2,128)(2,1)}), bf16[128,2,3584]{2,1,0:T(2,128)(2,1)S(1)}, u32[]{:S(2)}, u32[]{:S(2)}) async-start(bf16[128,2,3584]{2,1,0:T(2,128)(2,1)} %copy.70), calls=%async_computation.3 | async-start | bytes 3670016 | tf_op jit(solution)/shard_map/all_to_all | solution.py:179
  89.1 7.8 %fusion.2 = f32[128,2,2048]{2,0,1:T(8,128)S(1)} fusion(bf16[1,3584,2048]{2,1,0:T(8,128)(2,1)} %param.13, bf16[128,2,3584]{2,1,0:T(2,128)(2,1)} %copy-done.2), kind=kOutput, calls=%fused_computation.6 | convolution fusion | flops 3758096384 | bytes 18612224 | tf_op jit(solution)/shard_map/skc,cf->skf/dot_general | solution.py:72
  96.9 5.2 %fusion.8 = bf16[128,2,3584]{2,0,1:T(8,128)(2,1)S(1)} fusion(bf16[1,1024,3584]{2,1,0:T(8,128)(2,1)} %param.14, f32[128,2,2048]{2,0,1:T(8,128)S(1)} %fusion.2), kind=kOutput, calls=%fused_computation.12 | convolution fusion | flops 1881538560 | bytes 11272192 | tf_op jit(solution)/shard_map/skf,fc->skc/dot_general | solution.py:77
  102.0 3.2 %copy.62 = bf16[128,2,3584]{2,1,0:T(2,128)(2,1)} copy(bf16[128,2,3584]{2,0,1:T(8,128)(2,1)S(1)} %fusion.8) | data formatting | bytes 3670016 | tf_op jit(solution)/shard_map/convert_element_type | solution.py:79
  105.2 11.7 %all-to-all-done.3 = bf16[128,2,3584]{2,1,0:T(2,128)(2,1)S(1)} async-done(((bf16[128,2,3584]{2,1,0:T(2,128)(2,1)}), bf16[128,2,3584]{2,1,0:T(2,128)(2,1)S(1)}, u32[]{:S(2)}, u32[]{:S(2)}) %all-to-all-start.3) | async-done | bytes 1835040 | tf_op jit(solution)/shard_map/all_to_all | solution.py:179
  116.9 5.3 %all-to-all-start.1 = ((bf16[128,2,3584]{2,1,0:T(2,128)(2,1)}), bf16[128,2,3584]{2,1,0:T(2,128)(2,1)}, u32[]{:S(2)}, u32[]{:S(2)}) async-start(bf16[128,2,3584]{2,1,0:T(2,128)(2,1)} %copy.62), calls=%async_computation.1 | async-start | bytes 3670016 | tf_op jit(solution)/shard_map/all_to_all | solution.py:179
  122.3 2.9 %broadcast_select_fusion = bf16[16,128,576]{2,1,0:T(8,128)(2,1)S(1)} fusion(bf16[16,128,576]{2,1,0:T(8,128)(2,1)} %copy.73, bf16[16,128,576]{2,1,0:T(8,128)(2,1)} %copy.74, pred[16]{0:T(512)(128)(4,1)S(1)} %broadcast_compare_fusion), kind=kLoop, calls=%fused_computation.19 | loop fusion | flops 1179648 | bytes 7077904 | tf_op jit(solution)/shard_map/jit(_where)/select_n | solution.py:196
  125.1 1.3 fusion.63
  126.4 0.4 fusion.33
  126.9 1.6 %divide_convert_fusion = bf16[16,64,512]{2,1,0:T(8,128)(2,1)} fusion(bf16[16,128,576]{2,1,0:T(8,128)(2,1)S(1)} %broadcast_select_fusion, f32[16,64]{1,0:T(8,128)S(1)} %get-tuple-element.7, f32[16,512]{1,0:T(8,128)S(1)} %slice_convert_fusion, f32[16,64]{1,0:T(8,128)S(1)} %convert_element_type.125, f32[16,64,128]{2,1,0:T(8,128)S(1)} %get-tuple-element.13, ...), kind=kOutput, calls=%fused_computation.22 | convolution fusion | flops 136577024 | bytes 3727360 | tf_op jit(solution)/shard_map/nhl,nlc->nhc/dot_general | solution.py:146
  128.4 3.3 %gather_fusion = bf16[128,3584]{1,0:T(8,128)(2,1)} fusion(bf16[128,2,3584]{2,1,0:T(2,128)(2,1)S(1)} %all-to-all-done.3, s32[128]{0:T(128)S(1)} %fusion.58), kind=kCustom, calls=%fused_computation | custom fusion | bytes 1836032 | tf_op jit(solution)/shard_map/gather | solution.py:124
  131.7 1.9 %fusion.18 = bf16[16,3584]{1,0:T(8,128)(2,1)S(1)} fusion(bf16[128,3584]{1,0:T(8,128)(2,1)} %gather_fusion, f32[16,8]{1,0:T(8,128)S(1)} %copy.71), kind=kLoop, calls=%fused_computation.24 | loop fusion | flops 1318912 | bytes 1032704 | tf_op jit(solution)/shard_map/reduce_sum | solution.py:127
  133.6 16.2 %all-to-all-done.1 = bf16[128,2,3584]{2,1,0:T(2,128)(2,1)} async-done(((bf16[128,2,3584]{2,1,0:T(2,128)(2,1)}), bf16[128,2,3584]{2,1,0:T(2,128)(2,1)}, u32[]{:S(2)}, u32[]{:S(2)}) %all-to-all-start.1) | async-done | bytes 1835040 | tf_op jit(solution)/shard_map/all_to_all | solution.py:179
  149.8 3.2 %fusion.15 = bf16[2,16,3584]{2,1,0:T(8,128)(2,1)} fusion(bf16[128,2,3584]{2,1,0:T(2,128)(2,1)} %all-to-all-done.1, bf16[1,16,3584]{2,1,0:T(8,128)(2,1)S(1)} %bitcast.61, f32[2,16,128,2]{2,3,1,0:T(2,128)S(1)} %select_reduce_fusion), kind=kOutput, calls=%fused_computation.18 | convolution fusion | flops 352665600 | bytes 2211840 | tf_op jit(solution)/shard_map/stek,ekc->stc/dot_general | solution.py:111
  (23 shorter events, 0.2 us)
Async XLA Ops:
  0.6 32.6 %copy-start = (bf16[16,64,576]{2,1,0:T(8,128)(2,1)S(1)}, bf16[16,64,576]{2,1,0:T(8,128)(2,1)}, u32[]{:S(2)}) copy-start(bf16[16,64,576]{2,1,0:T(8,128)(2,1)} %param.15) | copy-start | bytes 3538948
  0.6 11.0 %copy-start.3 = (bf16[2,16,3584]{2,1,0:T(8,128)(2,1)S(1)}, bf16[2,16,3584]{2,1,0:T(8,128)(2,1)}, u32[]{:S(2)}) copy-start(bf16[2,16,3584]{2,1,0:T(8,128)(2,1)} %param.10) | copy-start | bytes 688132
  4.8 29.0 %collective-permute-start = (bf16[4,128,576]{1,2,0:T(8,128)(2,1)S(1)}, bf16[4,128,576]{1,2,0:T(8,128)(2,1)S(1)}, u32[]{:S(2)}, u32[]{:S(2)}) collective-permute-start(bf16[4,128,576]{1,2,0:T(8,128)(2,1)S(1)} %gather_fusion.2), channel_id=1, source_target_pairs={{0,64},{8,72},{16,80},{24,88},{32,96},{40,104},{48,112},{56,120},{... | collective-permute-start | bytes 1769480 | tf_op jit(solution)/shard_map/ppermute | solution.py:68
  15.5 8.3 %copy-start.5 = (f32[2,16,8]{1,2,0:T(8,128)S(1)}, f32[2,16,8]{1,2,0:T(8,128)}, u32[]{:S(2)}) copy-start(f32[2,16,8]{1,2,0:T(8,128)} %param.12) | copy-start | bytes 3076
  15.5 35.8 %all-to-all-start.2 = ((bf16[128,2,3584]{2,1,0:T(2,128)(2,1)}), bf16[128,2,3584]{2,1,0:T(2,128)(2,1)}, u32[]{:S(2)}, u32[]{:S(2)}) async-start(bf16[128,2,3584]{2,1,0:T(2,128)(2,1)} %copy.68), calls=%async_computation.2 | async-start | bytes 3670016 | tf_op jit(solution)/shard_map/all_to_all | solution.py:177
  29.0 3.2 %copy-start.6 = (s32[16]{0:T(128)S(1)}, s32[16]{0:T(128)}, u32[]{:S(2)}) copy-start(s32[16]{0:T(128)} %param.19) | copy-start | bytes 196
  29.0 3.2 %copy-start.1 = (s32[2048]{0:T(1024)S(1)}, s32[2048]{0:T(1024)}, u32[]{:S(2)}) copy-start(s32[2048]{0:T(1024)} %param.18) | copy-start | bytes 24580
  29.0 4.2 %copy-start.4 = (bf16[16,576]{1,0:T(8,128)(2,1)S(1)}, bf16[16,576]{1,0:T(8,128)(2,1)}, u32[]{:S(2)}) copy-start(bf16[16,576]{1,0:T(8,128)(2,1)} %param.16) | copy-start | bytes 55300
  51.2 32.2 %all-to-all-start = ((bf16[128,2,3584]{2,1,0:T(2,128)(2,1)}), bf16[128,2,3584]{2,1,0:T(2,128)(2,1)S(1)}, u32[]{:S(2)}, u32[]{:S(2)}) async-start(bf16[128,2,3584]{2,1,0:T(2,128)(2,1)} %copy.60), calls=%async_computation | async-start | bytes 3670016 | tf_op jit(solution)/shard_map/all_to_all | solution.py:177
  83.4 1.3 copy-start.2
  84.7 32.2 %all-to-all-start.3 = ((bf16[128,2,3584]{2,1,0:T(2,128)(2,1)}), bf16[128,2,3584]{2,1,0:T(2,128)(2,1)S(1)}, u32[]{:S(2)}, u32[]{:S(2)}) async-start(bf16[128,2,3584]{2,1,0:T(2,128)(2,1)} %copy.70), calls=%async_computation.3 | async-start | bytes 3670016 | tf_op jit(solution)/shard_map/all_to_all | solution.py:179
  116.9 32.9 %all-to-all-start.1 = ((bf16[128,2,3584]{2,1,0:T(2,128)(2,1)}), bf16[128,2,3584]{2,1,0:T(2,128)(2,1)}, u32[]{:S(2)}, u32[]{:S(2)}) async-start(bf16[128,2,3584]{2,1,0:T(2,128)(2,1)} %copy.62), calls=%async_computation.1 | async-start | bytes 3670016 | tf_op jit(solution)/shard_map/all_to_all | solution.py:179

commit v14 on v13

--- a/solution.py
+++ b/solution.py
@@ -112,7 +112,7 @@
         "stek,ekc->stc",
         weights,
         returned.astype(jnp.float32),
-        precision=lax.Precision.HIGHEST,
+        precision=lax.Precision.HIGH,
         preferred_element_type=jnp.float32,
     )
     return (summed + base).astype(jnp.bfloat16)

time: 154 us -> 154 us (level)
  no operation moved by 1% of the time
where the time goes in v14:
time: 154 us; the launch traced here: 153 us
  waiting for transfers between devices  50.3 us (33%)
  matrix products  33.5 us (22%)
  local copies, waits for them, and re-layouts  33.4 us (22%)
  starting transfers between devices  26.9 us (17%)
  other arithmetic  7.64 us (5%)
    all_to_all x2, waiting for transfers between devices, per_device(): lax.all_to_all(f, ('dp', 'ep'), 0, 0, tiled=True)  27.9 us
    all_to_all x2, waiting for transfers between devices, per_device(): lax.all_to_all(p[0], ('dp', 'ep'), 0, 0, tiled=True)  22.4 us
    dot_general x2, matrix products, expert_rows(): jnp.einsum('skc,cf->skf', picked, expert_in, preferred_element_type=jnp.f...  15.6 us
    all_to_all x2, starting transfers between devices, per_device(): lax.all_to_all(p[0], ('dp', 'ep'), 0, 0, tiled=True)  12.7 us
    dot_general x2, matrix products, expert_rows(): jnp.einsum('skf,fc->skc', activated, expert_out, preferred_element_type=j...  10.4 us
    all_to_all x2, starting transfers between devices, per_device(): lax.all_to_all(f, ('dp', 'ep'), 0, 0, tiled=True)  9.69 us
    gather x2, local copies, waits for them, and re-layouts, per_device(): incoming_cache[arrival]  6.67 us
    convert_element_type x2, local copies, waits for them, and re-layouts, expert_rows(): return jnp.einsum('skf,fc->skc', activated, expert_out, preferred_element...  6.37 us
  transfers between devices with their start and end apart: 5, of which 4 were waited for; matrix products, arithmetic and copies ran while one was open for 43% of the time, Pallas kernels for 0%

profile of v14, /device:TPU:1, one launch (start us, length us, event | category | flops | bytes accessed | tf_op | source)
XLA Modules:
  0.0 152.7 jit_solution(10638370118216671733)
XLA Ops:
  0.6 0.0 copy-start
  0.6 0.0 copy-start.3
  0.7 0.8 broadcast_compare_fusion
  1.4 0.7 copy.72
  2.2 0.1 fusion.46
  2.3 0.1 select_reduce_fusion.3
  2.5 2.3 %gather_fusion.2 = bf16[4,128,576]{1,2,0:T(8,128)(2,1)S(1)} fusion(bf16[16,128,576]{1,2,0:T(8,128)(2,1)} %param.17, s32[1024]{0:T(1024)S(1)} %pad_clamp_fusion.1), kind=kCustom, calls=%fused_computation.2 | custom fusion | bytes 1179664 | tf_op jit(solution)/shard_map/gather | solution.py:195
  4.8 4.5 %collective-permute-start = (bf16[4,128,576]{1,2,0:T(8,128)(2,1)S(1)}, bf16[4,128,576]{1,2,0:T(8,128)(2,1)S(1)}, u32[]{:S(2)}, u32[]{:S(2)}) collective-permute-start(bf16[4,128,576]{1,2,0:T(8,128)(2,1)S(1)} %gather_fusion.2), channel_id=1, source_target_pairs={{0,64},{8,72},{16,80},{24,88},{32,96},{40,104},{48,112},{56,120},{... | collective-permute-start | bytes 1769480 | tf_op jit(solution)/shard_map/ppermute | solution.py:68
  9.3 0.7 fusion.62
  10.0 0.1 copy.82
  10.1 0.1 eq.127
  10.2 0.1 fusion.42
  10.3 0.2 reduce_window_sum.25
  10.4 0.2 select_reduce_fusion.2
  10.6 0.1 reshape.470
  10.7 0.1 copy.83
  10.8 0.1 eq.138
  10.9 0.1 fusion.41
  11.0 0.2 reduce_window_sum.26
  11.2 0.2 select_reduce_fusion.1
  11.3 0.1 reshape.472
  11.4 0.2 compare_reduce_fusion
  11.6 0.7 convolution_convert_fusion
  12.3 3.2 %copy.68 = bf16[128,2,3584]{2,1,0:T(2,128)(2,1)} copy(bf16[128,2,3584]{2,0,1:T(8,128)(2,1)S(1)} %convolution_convert_fusion) | data formatting | bytes 3670016 | tf_op jit(solution)/shard_map/convert_element_type | solution.py:102
  15.5 8.3 %all-to-all-start.2 = ((bf16[128,2,3584]{2,1,0:T(2,128)(2,1)}), bf16[128,2,3584]{2,1,0:T(2,128)(2,1)}, u32[]{:S(2)}, u32[]{:S(2)}) async-start(bf16[128,2,3584]{2,1,0:T(2,128)(2,1)} %copy.68), calls=%async_computation.2 | async-start | bytes 3670016 | tf_op jit(solution)/shard_map/all_to_all | solution.py:177
  23.8 4.3 %copy.74 = bf16[16,128,576]{2,1,0:T(8,128)(2,1)} copy(bf16[16,128,576]{1,2,0:T(8,128)(2,1)} %param.17) | data formatting | bytes 4718592 | tf_op args[7]
  28.2 0.1 reshape.474
  28.3 0.1 copy.71
  28.3 0.7 convolution_convert_fusion.1
  29.0 0.0 copy-start.6
  29.0 0.0 copy-start.1
  29.0 0.0 copy-start.4
  29.1 3.1 %copy.60 = bf16[128,2,3584]{2,1,0:T(2,128)(2,1)} copy(bf16[128,2,3584]{2,0,1:T(8,128)(2,1)S(1)} %convolution_convert_fusion.1) | data formatting | bytes 3670016 | tf_op jit(solution)/shard_map/convert_element_type | solution.py:102
  32.2 0.1 copy.84
  32.3 0.0 copy-done.1
  32.3 0.7 gather_fusion.1
  32.9 0.2 select_reduce_fusion
  33.2 0.1 iota_compare_fusion.2
  33.3 0.0 copy-done
  33.3 0.5 fusion.43
  33.8 0.0 collective-permute-done
  33.8 2.3 %gather_fusion.3 = bf16[16,128,576]{1,2,0:T(8,128)(2,1)} fusion(bf16[4,128,576]{1,2,0:T(8,128)(2,1)S(1)} %collective-permute-done, s32[1024]{0:T(1024)S(1)} %pad_clamp_fusion), kind=kCustom, calls=%fused_computation.3 | custom fusion | bytes 4718656 | tf_op jit(solution)/shard_map/gather | solution.py:196
  36.1 4.4 %copy.73 = bf16[16,128,576]{2,1,0:T(8,128)(2,1)} copy(bf16[16,128,576]{1,2,0:T(8,128)(2,1)} %gather_fusion.3) | data formatting | bytes 4718592 | tf_op jit(solution)/shard_map/gather | solution.py:196
  40.4 10.8 %all-to-all-done.2 = bf16[128,2,3584]{2,1,0:T(2,128)(2,1)} async-done(((bf16[128,2,3584]{2,1,0:T(2,128)(2,1)}), bf16[128,2,3584]{2,1,0:T(2,128)(2,1)}, u32[]{:S(2)}, u32[]{:S(2)}) %all-to-all-start.2) | async-done | bytes 1835040 | tf_op jit(solution)/shard_map/all_to_all | solution.py:177
  51.2 4.3 %all-to-all-start = ((bf16[128,2,3584]{2,1,0:T(2,128)(2,1)}), bf16[128,2,3584]{2,1,0:T(2,128)(2,1)S(1)}, u32[]{:S(2)}, u32[]{:S(2)}) async-start(bf16[128,2,3584]{2,1,0:T(2,128)(2,1)} %copy.60), calls=%async_computation | async-start | bytes 3670016 | tf_op jit(solution)/shard_map/all_to_all | solution.py:177
  55.6 7.8 %fusion = f32[128,2,2048]{2,0,1:T(8,128)S(1)} fusion(bf16[1,3584,2048]{2,1,0:T(8,128)(2,1)} %param.13, bf16[128,2,3584]{2,1,0:T(2,128)(2,1)} %all-to-all-done.2), kind=kOutput, calls=%fused_computation.4 | convolution fusion | flops 3758096384 | bytes 18612224 | tf_op jit(solution)/shard_map/skc,cf->skf/dot_general | solution.py:72
  63.4 5.2 %fusion.11 = bf16[128,2,3584]{2,0,1:T(8,128)(2,1)S(1)} fusion(bf16[1,1024,3584]{2,1,0:T(8,128)(2,1)} %param.14, f32[128,2,2048]{2,0,1:T(8,128)S(1)} %fusion), kind=kOutput, calls=%fused_computation.13 | convolution fusion | flops 1881538560 | bytes 11272192 | tf_op jit(solution)/shard_map/skf,fc->skc/dot_general | solution.py:77
  68.6 3.2 %copy.70 = bf16[128,2,3584]{2,1,0:T(2,128)(2,1)} copy(bf16[128,2,3584]{2,0,1:T(8,128)(2,1)S(1)} %fusion.11) | data formatting | bytes 3670016 | tf_op jit(solution)/shard_map/convert_element_type | solution.py:79
  71.8 11.7 %all-to-all-done = bf16[128,2,3584]{2,1,0:T(2,128)(2,1)S(1)} async-done(((bf16[128,2,3584]{2,1,0:T(2,128)(2,1)}), bf16[128,2,3584]{2,1,0:T(2,128)(2,1)S(1)}, u32[]{:S(2)}, u32[]{:S(2)}) %all-to-all-start) | async-done | bytes 1835040 | tf_op jit(solution)/shard_map/all_to_all | solution.py:177
  83.4 1.3 copy-done.2
  84.7 4.3 %all-to-all-start.3 = ((bf16[128,2,3584]{2,1,0:T(2,128)(2,1)}), bf16[128,2,3584]{2,1,0:T(2,128)(2,1)S(1)}, u32[]{:S(2)}, u32[]{:S(2)}) async-start(bf16[128,2,3584]{2,1,0:T(2,128)(2,1)} %copy.70), calls=%async_computation.3 | async-start | bytes 3670016 | tf_op jit(solution)/shard_map/all_to_all | solution.py:179
  89.1 7.8 %fusion.2 = f32[128,2,2048]{2,0,1:T(8,128)S(1)} fusion(bf16[1,3584,2048]{2,1,0:T(8,128)(2,1)} %param.13, bf16[128,2,3584]{2,1,0:T(2,128)(2,1)} %copy-done.2), kind=kOutput, calls=%fused_computation.6 | convolution fusion | flops 3758096384 | bytes 18612224 | tf_op jit(solution)/shard_map/skc,cf->skf/dot_general | solution.py:72
  96.9 5.2 %fusion.8 = bf16[128,2,3584]{2,0,1:T(8,128)(2,1)S(1)} fusion(bf16[1,1024,3584]{2,1,0:T(8,128)(2,1)} %param.14, f32[128,2,2048]{2,0,1:T(8,128)S(1)} %fusion.2), kind=kOutput, calls=%fused_computation.12 | convolution fusion | flops 1881538560 | bytes 11272192 | tf_op jit(solution)/shard_map/skf,fc->skc/dot_general | solution.py:77
  102.0 3.2 %copy.62 = bf16[128,2,3584]{2,1,0:T(2,128)(2,1)} copy(bf16[128,2,3584]{2,0,1:T(8,128)(2,1)S(1)} %fusion.8) | data formatting | bytes 3670016 | tf_op jit(solution)/shard_map/convert_element_type | solution.py:79
  105.2 11.7 %all-to-all-done.3 = bf16[128,2,3584]{2,1,0:T(2,128)(2,1)S(1)} async-done(((bf16[128,2,3584]{2,1,0:T(2,128)(2,1)}), bf16[128,2,3584]{2,1,0:T(2,128)(2,1)S(1)}, u32[]{:S(2)}, u32[]{:S(2)}) %all-to-all-start.3) | async-done | bytes 1835040 | tf_op jit(solution)/shard_map/all_to_all | solution.py:179
  116.9 5.3 %all-to-all-start.1 = ((bf16[128,2,3584]{2,1,0:T(2,128)(2,1)}), bf16[128,2,3584]{2,1,0:T(2,128)(2,1)}, u32[]{:S(2)}, u32[]{:S(2)}) async-start(bf16[128,2,3584]{2,1,0:T(2,128)(2,1)} %copy.62), calls=%async_computation.1 | async-start | bytes 3670016 | tf_op jit(solution)/shard_map/all_to_all | solution.py:179
  122.3 2.9 %broadcast_select_fusion = bf16[16,128,576]{2,1,0:T(8,128)(2,1)S(1)} fusion(bf16[16,128,576]{2,1,0:T(8,128)(2,1)} %copy.73, bf16[16,128,576]{2,1,0:T(8,128)(2,1)} %copy.74, pred[16]{0:T(512)(128)(4,1)S(1)} %broadcast_compare_fusion), kind=kLoop, calls=%fused_computation.19 | loop fusion | flops 1179648 | bytes 7077904 | tf_op jit(solution)/shard_map/jit(_where)/select_n | solution.py:196
  125.1 1.3 fusion.63
  126.4 0.4 fusion.33
  126.9 1.6 %divide_convert_fusion = bf16[16,64,512]{2,1,0:T(8,128)(2,1)} fusion(bf16[16,128,576]{2,1,0:T(8,128)(2,1)S(1)} %broadcast_select_fusion, f32[16,64]{1,0:T(8,128)S(1)} %get-tuple-element.7, f32[16,512]{1,0:T(8,128)S(1)} %slice_convert_fusion, f32[16,64]{1,0:T(8,128)S(1)} %convert_element_type.125, f32[16,64,128]{2,1,0:T(8,128)S(1)} %get-tuple-element.13, ...), kind=kOutput, calls=%fused_computation.22 | convolution fusion | flops 136577024 | bytes 3727360 | tf_op jit(solution)/shard_map/nhl,nlc->nhc/dot_general | solution.py:146
  128.4 3.3 %gather_fusion = bf16[128,3584]{1,0:T(8,128)(2,1)} fusion(bf16[128,2,3584]{2,1,0:T(2,128)(2,1)S(1)} %all-to-all-done.3, s32[128]{0:T(128)S(1)} %fusion.58), kind=kCustom, calls=%fused_computation | custom fusion | bytes 1836032 | tf_op jit(solution)/shard_map/gather | solution.py:124
  131.7 1.9 %fusion.18 = bf16[16,3584]{1,0:T(8,128)(2,1)S(1)} fusion(bf16[128,3584]{1,0:T(8,128)(2,1)} %gather_fusion, f32[16,8]{1,0:T(8,128)S(1)} %copy.71), kind=kLoop, calls=%fused_computation.24 | loop fusion | flops 1318912 | bytes 1032704 | tf_op jit(solution)/shard_map/reduce_sum | solution.py:127
  133.6 16.2 %all-to-all-done.1 = bf16[128,2,3584]{2,1,0:T(2,128)(2,1)} async-done(((bf16[128,2,3584]{2,1,0:T(2,128)(2,1)}), bf16[128,2,3584]{2,1,0:T(2,128)(2,1)}, u32[]{:S(2)}, u32[]{:S(2)}) %all-to-all-start.1) | async-done | bytes 1835040 | tf_op jit(solution)/shard_map/all_to_all | solution.py:179
  149.8 2.9 %fusion.15 = bf16[2,16,3584]{2,1,0:T(8,128)(2,1)} fusion(bf16[128,2,3584]{2,1,0:T(2,128)(2,1)} %all-to-all-done.1, bf16[1,16,3584]{2,1,0:T(8,128)(2,1)S(1)} %bitcast.61, f32[2,16,128,2]{2,3,1,0:T(2,128)S(1)} %select_reduce_fusion), kind=kOutput, calls=%fused_computation.18 | convolution fusion | flops 176504832 | bytes 2211840 | tf_op jit(solution)/shard_map/stek,ekc->stc/dot_general | solution.py:111
  (23 shorter events, 0.2 us)
Async XLA Ops:
  0.6 32.6 %copy-start = (bf16[16,64,576]{2,1,0:T(8,128)(2,1)S(1)}, bf16[16,64,576]{2,1,0:T(8,128)(2,1)}, u32[]{:S(2)}) copy-start(bf16[16,64,576]{2,1,0:T(8,128)(2,1)} %param.15) | copy-start | bytes 3538948
  0.6 11.0 %copy-start.3 = (bf16[2,16,3584]{2,1,0:T(8,128)(2,1)S(1)}, bf16[2,16,3584]{2,1,0:T(8,128)(2,1)}, u32[]{:S(2)}) copy-start(bf16[2,16,3584]{2,1,0:T(8,128)(2,1)} %param.10) | copy-start | bytes 688132
  4.8 29.0 %collective-permute-start = (bf16[4,128,576]{1,2,0:T(8,128)(2,1)S(1)}, bf16[4,128,576]{1,2,0:T(8,128)(2,1)S(1)}, u32[]{:S(2)}, u32[]{:S(2)}) collective-permute-start(bf16[4,128,576]{1,2,0:T(8,128)(2,1)S(1)} %gather_fusion.2), channel_id=1, source_target_pairs={{0,64},{8,72},{16,80},{24,88},{32,96},{40,104},{48,112},{56,120},{... | collective-permute-start | bytes 1769480 | tf_op jit(solution)/shard_map/ppermute | solution.py:68
  15.5 8.3 %copy-start.5 = (f32[2,16,8]{1,2,0:T(8,128)S(1)}, f32[2,16,8]{1,2,0:T(8,128)}, u32[]{:S(2)}) copy-start(f32[2,16,8]{1,2,0:T(8,128)} %param.12) | copy-start | bytes 3076
  15.5 35.8 %all-to-all-start.2 = ((bf16[128,2,3584]{2,1,0:T(2,128)(2,1)}), bf16[128,2,3584]{2,1,0:T(2,128)(2,1)}, u32[]{:S(2)}, u32[]{:S(2)}) async-start(bf16[128,2,3584]{2,1,0:T(2,128)(2,1)} %copy.68), calls=%async_computation.2 | async-start | bytes 3670016 | tf_op jit(solution)/shard_map/all_to_all | solution.py:177
  29.0 3.2 %copy-start.6 = (s32[16]{0:T(128)S(1)}, s32[16]{0:T(128)}, u32[]{:S(2)}) copy-start(s32[16]{0:T(128)} %param.19) | copy-start | bytes 196
  29.0 3.2 %copy-start.1 = (s32[2048]{0:T(1024)S(1)}, s32[2048]{0:T(1024)}, u32[]{:S(2)}) copy-start(s32[2048]{0:T(1024)} %param.18) | copy-start | bytes 24580
  29.0 4.2 %copy-start.4 = (bf16[16,576]{1,0:T(8,128)(2,1)S(1)}, bf16[16,576]{1,0:T(8,128)(2,1)}, u32[]{:S(2)}) copy-start(bf16[16,576]{1,0:T(8,128)(2,1)} %param.16) | copy-start | bytes 55300
  51.2 32.2 %all-to-all-start = ((bf16[128,2,3584]{2,1,0:T(2,128)(2,1)}), bf16[128,2,3584]{2,1,0:T(2,128)(2,1)S(1)}, u32[]{:S(2)}, u32[]{:S(2)}) async-start(bf16[128,2,3584]{2,1,0:T(2,128)(2,1)} %copy.60), calls=%async_computation | async-start | bytes 3670016 | tf_op jit(solution)/shard_map/all_to_all | solution.py:177
  83.4 1.3 copy-start.2
  84.7 32.2 %all-to-all-start.3 = ((bf16[128,2,3584]{2,1,0:T(2,128)(2,1)}), bf16[128,2,3584]{2,1,0:T(2,128)(2,1)S(1)}, u32[]{:S(2)}, u32[]{:S(2)}) async-start(bf16[128,2,3584]{2,1,0:T(2,128)(2,1)} %copy.70), calls=%async_computation.3 | async-start | bytes 3670016 | tf_op jit(solution)/shard_map/all_to_all | solution.py:179
  116.9 32.9 %all-to-all-start.1 = ((bf16[128,2,3584]{2,1,0:T(2,128)(2,1)}), bf16[128,2,3584]{2,1,0:T(2,128)(2,1)}, u32[]{:S(2)}, u32[]{:S(2)}) async-start(bf16[128,2,3584]{2,1,0:T(2,128)(2,1)} %copy.62), calls=%async_computation.1 | async-start | bytes 3670016 | tf_op jit(solution)/shard_map/all_to_all | solution.py:179

commit v15 on v13

--- a/solution.py
+++ b/solution.py
@@ -101,6 +101,28 @@
         "dkt,tc->dkc", select, flat_tokens, preferred_element_type=jnp.float32
     ).astype(jnp.bfloat16)
     return packed, target
+
+
+def pack_rows_tiled(tokens, experts, expert_count, slot_cap, parts):
+    token_count, pick_count = experts.shape
+    onehot = (experts[:, :, None] == jnp.arange(expert_count, dtype=jnp.int32)).astype(jnp.int32)
+    flat = onehot.reshape(token_count * pick_count, expert_count)
+    earlier = jnp.cumsum(flat, axis=0) - flat
+    within = jnp.sum(earlier * flat, axis=1).reshape(token_count, pick_count)
+    target = experts * slot_cap + within
+    slots = jnp.arange(expert_count * slot_cap, dtype=jnp.int32)
+    hit = jnp.any(target[None, :, :] == slots[:, None, None], axis=2).astype(jnp.bfloat16)
+    eye = jnp.eye(parts, dtype=jnp.bfloat16)
+    select = (hit[:, None, :, None] * eye[None, :, None, :]).reshape(
+        expert_count * slot_cap * parts, token_count * parts
+    )
+    pieces = tokens.reshape(token_count * parts, tokens.shape[1] // parts)
+    packed = jnp.dot(
+        select,
+        pieces,
+        preferred_element_type=jnp.float32,
+    ).astype(jnp.bfloat16)
+    return packed.reshape(expert_count, slot_cap * parts, pieces.shape[1]), target[None]
 
 
 def unpack_rows(returned, target, gate_values, base):
@@ -174,7 +196,11 @@
         pack_rows(hidden[step : step + 1], routes[step : step + 1], expert_count, CAP)
         for step in range(STEPS)
     ]
+    parts = 4
+    tiled_pack = pack_rows_tiled(hidden[0], routes[0], expert_count, CAP, parts)
+    packs[0] = tiled_pack
     received = [lax.all_to_all(p[0], ("dp", "ep"), 0, 0, tiled=True) for p in packs]
+    received[0] = received[0].reshape(expert_count, CAP, hidden.shape[2])
     finished = [expert_rows(r, expert_in[0], expert_out[0]) for r in received]
     returned = [lax.all_to_all(f, ("dp", "ep"), 0, 0, tiled=True) for f in finished]
     early = gather_rows(returned[0], packs[0][1], route_weights[0:1])

time: 154 us -> 162 us (1.052)
  local copies, waits for them, and re-layouts: 33.4 us -> 41.3 us
  waiting for transfers between devices: 50.3 us -> 46.5 us
  other arithmetic: 7.64 us -> 10 us
    mul x0 -> x2, local copies, waits for them, and re-layouts: none -> 9.23 us  [the longest x1 9.15 us: pack_rows_tiled(): hit[:, None, :, None] * eye[None, :, None, :]]
    all_to_all x2, waiting for transfers between devices: 22.4 us -> 18.6 us  [per_device(): lax.all_to_all(p[0], ('dp', 'ep'), 0, 0, tiled=True)]
    convert_element_type x2 -> x1, local copies, waits for them, and re-layouts: 6.27 us -> 3.11 us  [pack_rows(): packed = jnp.einsum('dkt,tc->dkc', select, flat_tokens, preferred_element...]
    all_to_all x0 -> x1, local copies, waits for them, and re-layouts: none -> 3.14 us  [per_device(): lax.all_to_all(p[0], ('dp', 'ep'), 0, 0, tiled=True)]
    mul x0 -> x2, other arithmetic: none -> 2.3 us  [the longest x1 2.29 us: pack_rows_tiled(): hit[:, None, :, None] * eye[None, :, None, :]]
    dot_general x0 -> x1, matrix products: none -> 1.94 us  [pack_rows_tiled(): jnp.dot(select, pieces, preferred_element_type=jnp.float32)]
    unnamed x18 -> x16, local copies, waits for them, and re-layouts: 5.87 us -> 4.63 us
  transfers between devices with their start and end apart: 5 -> 5, of which waited for: 4 -> 4; matrix products, arithmetic and copies ran while one was open for 43% -> 49% of each run, Pallas kernels for 0% -> 0%
where the time goes in v15:
time: 162 us; the launch traced here: 161 us
  waiting for transfers between devices  46.5 us (29%)
  local copies, waits for them, and re-layouts  41.3 us (25%)
  matrix products  34.6 us (21%)
  starting transfers between devices  27.9 us (17%)
  other arithmetic  10 us (6%)
    all_to_all x2, waiting for transfers between devices, per_device(): lax.all_to_all(f, ('dp', 'ep'), 0, 0, tiled=True)  27.9 us
    all_to_all x2, waiting for transfers between devices, per_device(): lax.all_to_all(p[0], ('dp', 'ep'), 0, 0, tiled=True)  18.6 us
    dot_general x2, matrix products, expert_rows(): jnp.einsum('skc,cf->skf', picked, expert_in, preferred_element_type=jnp.f...  15.1 us
    all_to_all x2, starting transfers between devices, per_device(): lax.all_to_all(p[0], ('dp', 'ep'), 0, 0, tiled=True)  13.7 us
    dot_general x2, matrix products, expert_rows(): jnp.einsum('skf,fc->skc', activated, expert_out, preferred_element_type=j...  10.4 us
    all_to_all x2, starting transfers between devices, per_device(): lax.all_to_all(f, ('dp', 'ep'), 0, 0, tiled=True)  9.69 us
    mul x1, local copies, waits for them, and re-layouts, pack_rows_tiled(): hit[:, None, :, None] * eye[None, :, None, :]  9.15 us
    gather x2, local copies, waits for them, and re-layouts, per_device(): incoming_cache[arrival]  6.67 us
  transfers between devices with their start and end apart: 5, of which 4 were waited for; matrix products, arithmetic and copies ran while one was open for 49% of the time, Pallas kernels for 0%

profile of v15, /device:TPU:1, one launch (start us, length us, event | category | flops | bytes accessed | tf_op | source)
XLA Modules:
  0.0 161.3 jit_solution(15141631236079162757)
XLA Ops:
  0.6 0.0 copy-start
  0.6 0.8 broadcast_compare_fusion
  1.4 0.7 copy.74
  2.2 0.1 fusion.44
  2.3 0.1 select_reduce_fusion.3
  2.4 2.3 %gather_fusion.2 = bf16[4,128,576]{1,2,0:T(8,128)(2,1)S(1)} fusion(bf16[16,128,576]{1,2,0:T(8,128)(2,1)} %param.17, s32[1024]{0:T(1024)S(1)} %pad_clamp_fusion.1), kind=kCustom, calls=%fused_computation.2 | custom fusion | bytes 1179664 | tf_op jit(solution)/shard_map/gather | solution.py:221
  4.8 4.5 %collective-permute-start = (bf16[4,128,576]{1,2,0:T(8,128)(2,1)S(1)}, bf16[4,128,576]{1,2,0:T(8,128)(2,1)S(1)}, u32[]{:S(2)}, u32[]{:S(2)}) collective-permute-start(bf16[4,128,576]{1,2,0:T(8,128)(2,1)S(1)} %gather_fusion.2), channel_id=1, source_target_pairs={{0,64},{8,72},{16,80},{24,88},{32,96},{40,104},{48,112},{56,120},{... | collective-permute-start | bytes 1769480 | tf_op jit(solution)/shard_map/ppermute | solution.py:68
  9.3 0.7 fusion.61
  10.0 0.1 copy.86
  10.1 0.1 eq.130
  10.2 0.1 fusion.39
  10.2 0.2 reduce_window_sum.31
  10.4 0.2 select_reduce_fusion.1
  10.6 0.1 reshape.385
  10.7 0.1 fusion.36
  10.8 2.3 %broadcast_multiply_fusion = bf16[256,4,16,4]{1,0,3,2:T(8,128)(2,1)} fusion(bf16[4,4]{0,1:T(4,128)(2,1)S(1)} %fusion.47, bf16[256,16]{0,1:T(8,128)(2,1)S(1)} %convert_element_type.112), kind=kLoop, calls=%fused_computation.22 | loop fusion | flops 65536 | bytes 139296 | tf_op jit(solution)/shard_map/mul | solution.py:116
  13.1 9.2 %mul.132 = bf16[1024,64]{0,1:T(8,128)(2,1)S(1)} reshape(bf16[256,4,16,4]{1,0,3,2:T(8,128)(2,1)} %broadcast_multiply_fusion) | data formatting | bytes 262144 | tf_op jit(solution)/shard_map/mul | solution.py:116
  22.3 0.1 reshape_squeeze.3
  22.4 1.9 %convert_bitcast_fusion = bf16[128,8,896]{2,1,0:T(8,128)(2,1)} fusion(bf16[1024,64]{0,1:T(8,128)(2,1)S(1)} %mul.132, bf16[64,896]{1,0:T(8,128)(2,1)S(1)} %reshape_squeeze.3), kind=kOutput, calls=%fused_computation.28 | convolution fusion | flops 118358016 | bytes 2080768 | tf_op jit(solution)/shard_map/dot_general | solution.py:120
  24.3 8.3 %all-to-all-start.2 = ((bf16[128,8,896]{2,1,0:T(8,128)(2,1)}), bf16[128,8,896]{2,1,0:T(8,128)(2,1)}, u32[]{:S(2)}, u32[]{:S(2)}) async-start(bf16[128,8,896]{2,1,0:T(8,128)(2,1)} %convert_bitcast_fusion), calls=%async_computation.2 | async-start | bytes 3670016 | tf_op jit(solution)/shard_map/all_to_all | solution.py:202
  32.7 0.1 copy.85
  32.8 0.1 eq.119
  32.9 0.1 fusion.40
  33.0 0.2 reduce_window_sum.30
  33.1 0.2 select_reduce_fusion.2
  33.3 0.1 reshape.383
  33.4 0.1 compare_reduce_fusion
  33.5 0.0 copy-start.2
  33.6 4.4 %copy.76 = bf16[16,128,576]{2,1,0:T(8,128)(2,1)} copy(bf16[16,128,576]{1,2,0:T(8,128)(2,1)} %param.17) | data formatting | bytes 4718592 | tf_op args[7]
  37.9 0.1 mul.135
  38.0 0.1 copy.73
  38.1 0.1 copy.87
  38.2 0.7 convolution_convert_fusion
  38.8 0.0 copy-start.5
  38.9 0.0 copy-start.1
  38.9 0.0 copy-start.3
  38.9 3.1 %copy.62 = bf16[128,2,3584]{2,1,0:T(2,128)(2,1)} copy(bf16[128,2,3584]{2,0,1:T(8,128)(2,1)S(1)} %convolution_convert_fusion) | data formatting | bytes 3670016 | tf_op jit(solution)/shard_map/convert_element_type | solution.py:102
  42.0 0.7 gather_fusion.1
  42.7 0.2 select_reduce_fusion
  42.9 0.1 iota_compare_fusion.3
  43.0 0.5 fusion.41
  43.5 2.3 %gather_fusion.3 = bf16[16,128,576]{1,2,0:T(8,128)(2,1)} fusion(bf16[4,128,576]{1,2,0:T(8,128)(2,1)S(1)} %collective-permute-done, s32[1024]{0:T(1024)S(1)} %pad_clamp_fusion), kind=kCustom, calls=%fused_computation.3 | custom fusion | bytes 4718656 | tf_op jit(solution)/shard_map/gather | solution.py:222
  45.9 4.4 %copy.75 = bf16[16,128,576]{2,1,0:T(8,128)(2,1)} copy(bf16[16,128,576]{1,2,0:T(8,128)(2,1)} %gather_fusion.3) | data formatting | bytes 4718592 | tf_op jit(solution)/shard_map/gather | solution.py:222
  50.2 9.9 %all-to-all-done.2 = bf16[128,8,896]{2,1,0:T(8,128)(2,1)} async-done(((bf16[128,8,896]{2,1,0:T(8,128)(2,1)}), bf16[128,8,896]{2,1,0:T(8,128)(2,1)}, u32[]{:S(2)}, u32[]{:S(2)}) %all-to-all-start.2) | async-done | bytes 1835040 | tf_op jit(solution)/shard_map/all_to_all | solution.py:202
  60.1 5.4 %all-to-all-start = ((bf16[128,2,3584]{2,1,0:T(2,128)(2,1)}), bf16[128,2,3584]{2,1,0:T(2,128)(2,1)}, u32[]{:S(2)}, u32[]{:S(2)}) async-start(bf16[128,2,3584]{2,1,0:T(2,128)(2,1)} %copy.62), calls=%async_computation | async-start | bytes 3670016 | tf_op jit(solution)/shard_map/all_to_all | solution.py:202
  65.4 3.1 %copy.70 = bf16[128,8,896]{0,2,1:T(8,128)(2,1)S(1)} copy(bf16[128,8,896]{2,1,0:T(8,128)(2,1)} %all-to-all-done.2) | data formatting | bytes 3670016 | tf_op jit(solution)/shard_map/all_to_all | solution.py:202
  68.6 7.3 %fusion = f32[128,2,2048]{2,0,1:T(8,128)S(1)} fusion(bf16[128,2,3584]{0,2,1:T(8,128)(2,1)S(1)} %bitcast.73, bf16[1,3584,2048]{2,1,0:T(8,128)(2,1)} %param.13), kind=kOutput, calls=%fused_computation.4 | convolution fusion | flops 3758096384 | bytes 18612224 | tf_op jit(solution)/shard_map/skc,cf->skf/dot_general | solution.py:72
  75.9 5.2 %fusion.11 = bf16[128,2,3584]{2,0,1:T(8,128)(2,1)S(1)} fusion(bf16[1,1024,3584]{2,1,0:T(8,128)(2,1)} %param.14, f32[128,2,2048]{2,0,1:T(8,128)S(1)} %fusion), kind=kOutput, calls=%fused_computation.13 | convolution fusion | flops 1881538560 | bytes 11272192 | tf_op jit(solution)/shard_map/skf,fc->skc/dot_general | solution.py:77
  81.1 3.2 %copy.72 = bf16[128,2,3584]{2,1,0:T(2,128)(2,1)} copy(bf16[128,2,3584]{2,0,1:T(8,128)(2,1)S(1)} %fusion.11) | data formatting | bytes 3670016 | tf_op jit(solution)/shard_map/convert_element_type | solution.py:79
  84.3 8.7 %all-to-all-done = bf16[128,2,3584]{2,1,0:T(2,128)(2,1)} async-done(((bf16[128,2,3584]{2,1,0:T(2,128)(2,1)}), bf16[128,2,3584]{2,1,0:T(2,128)(2,1)}, u32[]{:S(2)}, u32[]{:S(2)}) %all-to-all-start) | async-done | bytes 1835040 | tf_op jit(solution)/shard_map/all_to_all | solution.py:202
  93.0 4.3 %all-to-all-start.3 = ((bf16[128,2,3584]{2,1,0:T(2,128)(2,1)}), bf16[128,2,3584]{2,1,0:T(2,128)(2,1)S(1)}, u32[]{:S(2)}, u32[]{:S(2)}) async-start(bf16[128,2,3584]{2,1,0:T(2,128)(2,1)} %copy.72), calls=%async_computation.3 | async-start | bytes 3670016 | tf_op jit(solution)/shard_map/all_to_all | solution.py:205
  97.3 7.8 %fusion.2 = f32[128,2,2048]{2,0,1:T(8,128)S(1)} fusion(bf16[1,3584,2048]{2,1,0:T(8,128)(2,1)} %param.13, bf16[128,2,3584]{2,1,0:T(2,128)(2,1)} %all-to-all-done), kind=kOutput, calls=%fused_computation.6 | convolution fusion | flops 3758096384 | bytes 18612224 | tf_op jit(solution)/shard_map/skc,cf->skf/dot_general | solution.py:72
  105.1 5.2 %fusion.8 = bf16[128,2,3584]{2,0,1:T(8,128)(2,1)S(1)} fusion(bf16[1,1024,3584]{2,1,0:T(8,128)(2,1)} %param.14, f32[128,2,2048]{2,0,1:T(8,128)S(1)} %fusion.2), kind=kOutput, calls=%fused_computation.12 | convolution fusion | flops 1881538560 | bytes 11272192 | tf_op jit(solution)/shard_map/skf,fc->skc/dot_general | solution.py:77
  110.3 3.2 %copy.64 = bf16[128,2,3584]{2,1,0:T(2,128)(2,1)} copy(bf16[128,2,3584]{2,0,1:T(8,128)(2,1)S(1)} %fusion.8) | data formatting | bytes 3670016 | tf_op jit(solution)/shard_map/convert_element_type | solution.py:79
  113.5 11.7 %all-to-all-done.3 = bf16[128,2,3584]{2,1,0:T(2,128)(2,1)S(1)} async-done(((bf16[128,2,3584]{2,1,0:T(2,128)(2,1)}), bf16[128,2,3584]{2,1,0:T(2,128)(2,1)S(1)}, u32[]{:S(2)}, u32[]{:S(2)}) %all-to-all-start.3) | async-done | bytes 1835040 | tf_op jit(solution)/shard_map/all_to_all | solution.py:205
  125.2 5.3 %all-to-all-start.1 = ((bf16[128,2,3584]{2,1,0:T(2,128)(2,1)}), bf16[128,2,3584]{2,1,0:T(2,128)(2,1)}, u32[]{:S(2)}, u32[]{:S(2)}) async-start(bf16[128,2,3584]{2,1,0:T(2,128)(2,1)} %copy.64), calls=%async_computation.1 | async-start | bytes 3670016 | tf_op jit(solution)/shard_map/all_to_all | solution.py:205
  130.6 2.9 %broadcast_select_fusion = bf16[16,128,576]{2,1,0:T(8,128)(2,1)S(1)} fusion(bf16[16,128,576]{2,1,0:T(8,128)(2,1)} %copy.75, bf16[16,128,576]{2,1,0:T(8,128)(2,1)} %copy.76, pred[16]{0:T(512)(128)(4,1)S(1)} %broadcast_compare_fusion), kind=kLoop, calls=%fused_computation.18 | loop fusion | flops 1179648 | bytes 7077904 | tf_op jit(solution)/shard_map/jit(_where)/select_n | solution.py:222
  133.4 1.3 fusion.62
  134.7 0.4 fusion.32
  135.1 1.6 divide_convert_fusion
  136.7 3.3 %gather_fusion = bf16[128,3584]{1,0:T(8,128)(2,1)} fusion(bf16[128,2,3584]{2,1,0:T(2,128)(2,1)S(1)} %all-to-all-done.3, s32[128]{0:T(128)S(1)} %fusion.57), kind=kCustom, calls=%fused_computation | custom fusion | bytes 1836032 | tf_op jit(solution)/shard_map/gather | solution.py:146
  140.0 1.9 %fusion.18 = bf16[16,3584]{1,0:T(8,128)(2,1)S(1)} fusion(bf16[128,3584]{1,0:T(8,128)(2,1)} %gather_fusion, f32[16,8]{1,0:T(8,128)S(1)} %copy.73), kind=kLoop, calls=%fused_computation.24 | loop fusion | flops 1318912 | bytes 1032704 | tf_op jit(solution)/shard_map/reduce_sum | solution.py:149
  141.9 16.2 %all-to-all-done.1 = bf16[128,2,3584]{2,1,0:T(2,128)(2,1)} async-done(((bf16[128,2,3584]{2,1,0:T(2,128)(2,1)}), bf16[128,2,3584]{2,1,0:T(2,128)(2,1)}, u32[]{:S(2)}, u32[]{:S(2)}) %all-to-all-start.1) | async-done | bytes 1835040 | tf_op jit(solution)/shard_map/all_to_all | solution.py:205
  158.1 3.2 %fusion.15 = bf16[2,16,3584]{2,1,0:T(8,128)(2,1)} fusion(bf16[128,2,3584]{2,1,0:T(2,128)(2,1)} %all-to-all-done.1, bf16[1,16,3584]{2,1,0:T(8,128)(2,1)S(1)} %bitcast.74, f32[2,16,128,2]{2,3,1,0:T(2,128)S(1)} %select_reduce_fusion), kind=kOutput, calls=%fused_computation.17 | convolution fusion | flops 352665600 | bytes 2211840 | tf_op jit(solution)/shard_map/stek,ekc->stc/dot_general | solution.py:133
  (29 shorter events, 0.2 us)
Async XLA Ops:
  0.6 42.4 %copy-start = (bf16[16,64,576]{2,1,0:T(8,128)(2,1)S(1)}, bf16[16,64,576]{2,1,0:T(8,128)(2,1)}, u32[]{:S(2)}) copy-start(bf16[16,64,576]{2,1,0:T(8,128)(2,1)} %param.15) | copy-start | bytes 3538948
  4.8 38.8 %collective-permute-start = (bf16[4,128,576]{1,2,0:T(8,128)(2,1)S(1)}, bf16[4,128,576]{1,2,0:T(8,128)(2,1)S(1)}, u32[]{:S(2)}, u32[]{:S(2)}) collective-permute-start(bf16[4,128,576]{1,2,0:T(8,128)(2,1)S(1)} %gather_fusion.2), channel_id=1, source_target_pairs={{0,64},{8,72},{16,80},{24,88},{32,96},{40,104},{48,112},{56,120},{... | collective-permute-start | bytes 1769480 | tf_op jit(solution)/shard_map/ppermute | solution.py:68
  13.1 9.2 %slice-start = ((bf16[2,16,3584]{2,1,0:T(8,128)(2,1)}), bf16[1,16,3584]{2,1,0:T(8,128)(2,1)S(1)}, s32[]{:S(2)}) async-start(bf16[2,16,3584]{2,1,0:T(8,128)(2,1)} %param.10), calls=%async_computation.4 | async-start | bytes 229376 | tf_op jit(solution)/shard_map/slice | solution.py:200
  24.3 8.4 %copy-start.4 = (f32[2,16,8]{1,2,0:T(8,128)S(1)}, f32[2,16,8]{1,2,0:T(8,128)}, u32[]{:S(2)}) copy-start(f32[2,16,8]{1,2,0:T(8,128)} %param.12) | copy-start | bytes 3076
  24.3 35.8 %all-to-all-start.2 = ((bf16[128,8,896]{2,1,0:T(8,128)(2,1)}), bf16[128,8,896]{2,1,0:T(8,128)(2,1)}, u32[]{:S(2)}, u32[]{:S(2)}) async-start(bf16[128,8,896]{2,1,0:T(8,128)(2,1)} %convert_bitcast_fusion), calls=%async_computation.2 | async-start | bytes 3670016 | tf_op jit(solution)/shard_map/all_to_all | solution.py:202
  33.5 4.6 %copy-start.2 = (bf16[2,16,3584]{2,1,0:T(8,128)(2,1)S(1)}, bf16[2,16,3584]{2,1,0:T(8,128)(2,1)}, u32[]{:S(2)}) copy-start(bf16[2,16,3584]{2,1,0:T(8,128)(2,1)} %param.10) | copy-start | bytes 688132
  38.8 3.1 %copy-start.5 = (s32[16]{0:T(128)S(1)}, s32[16]{0:T(128)}, u32[]{:S(2)}) copy-start(s32[16]{0:T(128)} %param.19) | copy-start | bytes 196
  38.9 3.2 %copy-start.1 = (s32[2048]{0:T(1024)S(1)}, s32[2048]{0:T(1024)}, u32[]{:S(2)}) copy-start(s32[2048]{0:T(1024)} %param.18) | copy-start | bytes 24580
  38.9 4.1 %copy-start.3 = (bf16[16,576]{1,0:T(8,128)(2,1)S(1)}, bf16[16,576]{1,0:T(8,128)(2,1)}, u32[]{:S(2)}) copy-start(bf16[16,576]{1,0:T(8,128)(2,1)} %param.16) | copy-start | bytes 55300
  60.1 32.9 %all-to-all-start = ((bf16[128,2,3584]{2,1,0:T(2,128)(2,1)}), bf16[128,2,3584]{2,1,0:T(2,128)(2,1)}, u32[]{:S(2)}, u32[]{:S(2)}) async-start(bf16[128,2,3584]{2,1,0:T(2,128)(2,1)} %copy.62), calls=%async_computation | async-start | bytes 3670016 | tf_op jit(solution)/shard_map/all_to_all | solution.py:202
  93.0 32.2 %all-to-all-start.3 = ((bf16[128,2,3584]{2,1,0:T(2,128)(2,1)}), bf16[128,2,3584]{2,1,0:T(2,128)(2,1)S(1)}, u32[]{:S(2)}, u32[]{:S(2)}) async-start(bf16[128,2,3584]{2,1,0:T(2,128)(2,1)} %copy.72), calls=%async_computation.3 | async-start | bytes 3670016 | tf_op jit(solution)/shard_map/all_to_all | solution.py:205
  125.2 32.9 %all-to-all-start.1 = ((bf16[128,2,3584]{2,1,0:T(2,128)(2,1)}), bf16[128,2,3584]{2,1,0:T(2,128)(2,1)}, u32[]{:S(2)}, u32[]{:S(2)}) async-start(bf16[128,2,3584]{2,1,0:T(2,128)(2,1)} %copy.64), calls=%async_computation.1 | async-start | bytes 3670016 | tf_op jit(solution)/shard_map/all_to_all | solution.py:205
